TPU v7x, 32 devices: a whole 2x2x4 slice. The times are simulated.
32 devices in a mesh: dp: 2 (over x), fsdp: 16 (over z, y, core).
Axes of the slice: x: 2, y: 2, z: 4, core: 2. Of those that a mesh axis runs over, the one named last changes fastest.
Arguments:
- tokens: bfloat16 [32768, 1024], P(('dp', 'fsdp')), may hold values from -6 to 6
- time_embed: bfloat16 [32768, 256], P(('dp', 'fsdp')), may hold values from -6 to 6
- segments: int32 [32, 1024], P(('dp', 'fsdp')), may hold values from 0 to 3, never falling along the last dimension, each value on 1 to 512 neighbouring positions
- cotangent: bfloat16 [32768, 1024], P(('dp', 'fsdp')), may hold values from -6 to 6
- attn_norm_gain: bfloat16 [1024], P('fsdp'), may hold values from 0.5 to 1.5
- attn_norm_bias: bfloat16 [1024], P('fsdp'), may hold values from -0.5 to 0.5
- time_weight: bfloat16 [256, 2048], P('fsdp'), may hold values from -0.1875 to 0.1875
- qkv_weight: bfloat16 [1024, 3072], P('fsdp'), may hold values from -0.1875 to 0.1875
- qkv_bias: bfloat16 [3072], P('fsdp'), may hold values from -0.5 to 0.5
- out_weight: bfloat16 [1024, 1024], P('fsdp'), may hold values from -1.5 to 1.5
- out_bias: bfloat16 [1024], P('fsdp'), may hold values from -0.5 to 0.5
- mlp_norm_gain: bfloat16 [1024], P('fsdp'), may hold values from 0.5 to 1.5
- mlp_norm_bias: bfloat16 [1024], P('fsdp'), may hold values from -0.5 to 0.5
- up_weight: bfloat16 [1024, 4096], P('fsdp'), may hold values from -0.1875 to 0.1875
- up_bias: bfloat16 [4096], P('fsdp'), may hold values from -0.5 to 0.5
- down_weight: bfloat16 [4096, 1024], P('fsdp'), may hold values from -0.09375 to 0.09375
- down_bias: bfloat16 [1024], P('fsdp'), may hold values from -0.5 to 0.5
Outputs:
- layer_out: bfloat16 [32768, 1024], P(('dp', 'fsdp'))
- tokens_grad: bfloat16 [32768, 1024], P(('dp', 'fsdp'))
- attn_norm_gain_grad: float32 [1024], P('fsdp')
- attn_norm_bias_grad: float32 [1024], P('fsdp')
- time_weight_grad: float32 [256, 2048], P('fsdp')
- qkv_weight_grad: float32 [1024, 3072], P('fsdp')
- qkv_bias_grad: float32 [3072], P('fsdp')
- out_weight_grad: float32 [1024, 1024], P('fsdp')
- out_bias_grad: float32 [1024], P('fsdp')
- mlp_norm_gain_grad: float32 [1024], P('fsdp')
- mlp_norm_bias_grad: float32 [1024], P('fsdp')
- up_weight_grad: float32 [1024, 4096], P('fsdp')
- up_bias_grad: float32 [4096], P('fsdp')
- down_weight_grad: float32 [4096, 1024], P('fsdp')
- down_bias_grad: float32 [1024], P('fsdp')
Inputs may be any that keep to these rules, and one draw needn't show every extreme that they name: `segments`: within each packed row the segment ids never fall, each document holds 1 to 512 tokens, and one document holds exactly 512.
All inputs are finite; a program needn't handle non-finite values.
Results may differ from a plain program's by a relative error of at most 0.015.
Values may be sent and summed in bfloat16 or wider, within the bound.
No kernel may reach another device: no remote copies, remote signals or barrier semaphores. Data moves between devices by JAX's collectives and lax.ppermute only.
A program may use at most 320 MiB of HBM per device.

v0:
```python
import math

import jax
import jax.numpy as jnp
from jax import lax
from jax.sharding import PartitionSpec as P

HEADS = 16
HEAD_DIM = 64


def positions_of(segments):
    index = jnp.broadcast_to(jnp.arange(segments.shape[1], dtype=jnp.int32), segments.shape)
    starts = jnp.concatenate(
        [jnp.ones((segments.shape[0], 1), dtype=bool), segments[:, 1:] != segments[:, :-1]], axis=1
    )
    first = lax.cummax(jnp.where(starts, index, jnp.zeros_like(index)), axis=1)
    return index - first


def rotary_tables(positions, head_width):
    steps_half = jnp.arange(head_width // 2, dtype=jnp.float32)
    inverse = jnp.exp(steps_half * (-2.0 * math.log(10000.0) / head_width))
    angles = positions.astype(jnp.float32)[..., None] * inverse
    return (jnp.cos(angles), jnp.sin(angles))


def rotate(values, cosine, sine):
    half = values.shape[-1] // 2
    first, second = (values[..., :half], values[..., half:])
    cosine = cosine[..., None, :]
    sine = sine[..., None, :]
    return jnp.concatenate(
        [first * cosine - second * sine, second * cosine + first * sine], axis=-1
    )


def norm_mod(values, gain, bias, shift):
    center = jnp.mean(values, axis=-1, keepdims=True)
    centered = values - center
    spread = jnp.mean(centered * centered, axis=-1, keepdims=True)
    return (centered * lax.rsqrt(spread + 1e-05) * gain + bias) * (1.0 + shift)


def gelu_exact(values):
    return jax.nn.gelu(values, approximate=False)


def product(left, right):
    return jnp.dot(left, right, preferred_element_type=jnp.float32)


def product_left(left, right):
    return lax.dot_general(
        left, right, (((0,), (0,)), ((), ())), preferred_element_type=jnp.float32
    )


def product_right(left, right):
    return lax.dot_general(
        left, right, (((1,), (1,)), ((), ())), preferred_element_type=jnp.float32
    )


def block_scores(query_block, key, seg_block, seg):
    scale = query_block.shape[-1] ** (-0.5)
    raw = jnp.einsum("qhd,khd->hqk", query_block, key, preferred_element_type=jnp.float32)
    same = (seg_block[:, None] == seg[None, :])[None]
    return jnp.where(same, raw * scale, -1e30)


def attend_forward(item):
    query, key, value, seg = item
    seq, heads_count, head_width = query.shape
    block = min(512, seq)
    query_blocks = query.reshape(seq // block, block, heads_count, head_width)
    seg_blocks = seg.reshape(seq // block, block)

    def one_block(pair):
        query_block, seg_block = pair
        scores = block_scores(query_block, key, seg_block, seg)
        peak = jnp.max(scores, axis=-1, keepdims=True)
        expo = jnp.exp(scores - peak)
        total = jnp.sum(expo, axis=-1, keepdims=True)
        probs_low = (expo / total).astype(jnp.bfloat16)
        mixed = jnp.einsum("hqk,khd->qhd", probs_low, value, preferred_element_type=jnp.float32)
        return (mixed.astype(jnp.bfloat16), (peak + jnp.log(total))[..., 0])

    mixed, logsum = lax.map(one_block, (query_blocks, seg_blocks))
    return (mixed.reshape(seq, heads_count, head_width), logsum)


def attend_backward(item):
    query, key, value, seg, grad_mixed, logsum = item
    seq, heads_count, head_width = query.shape
    block = min(512, seq)
    scale = head_width ** (-0.5)
    query_blocks = query.reshape(seq // block, block, heads_count, head_width)
    grad_blocks = grad_mixed.reshape(seq // block, block, heads_count, head_width)
    seg_blocks = seg.reshape(seq // block, block)

    def one_block(carry, parts):
        key_grad, value_grad = carry
        query_block, seg_block, grad_block, logsum_block = parts
        scores = block_scores(query_block, key, seg_block, seg)
        probs = jnp.exp(scores - logsum_block[..., None])
        grad_probs = jnp.einsum(
            "qhd,khd->hqk", grad_block, value, preferred_element_type=jnp.float32
        )
        inner = jnp.sum(probs * grad_probs, axis=-1, keepdims=True)
        grad_raw = (probs * (grad_probs - inner) * scale).astype(jnp.bfloat16)
        query_grad = jnp.einsum("hqk,khd->qhd", grad_raw, key, preferred_element_type=jnp.float32)
        key_grad = key_grad + jnp.einsum(
            "hqk,qhd->khd", grad_raw, query_block, preferred_element_type=jnp.float32
        )
        value_grad = value_grad + jnp.einsum(
            "hqk,qhd->khd",
            probs.astype(jnp.bfloat16),
            grad_block,
            preferred_element_type=jnp.float32,
        )
        return ((key_grad, value_grad), query_grad)

    zeros_kv = jnp.zeros((seq, heads_count, head_width), jnp.float32)
    (key_grad, value_grad), query_grad = lax.scan(
        one_block, (zeros_kv, zeros_kv), (query_blocks, seg_blocks, grad_blocks, logsum)
    )
    return (query_grad.reshape(seq, heads_count, head_width), key_grad, value_grad)


def reduce_mlp(gain_grad, bias_grad, up_grad, upb_grad, down_grad, downb_grad, factor):
    shares = (
        lax.psum_scatter(gain_grad, "fsdp", scatter_dimension=0, tiled=True),
        lax.psum_scatter(bias_grad, "fsdp", scatter_dimension=0, tiled=True),
        lax.psum_scatter(up_grad, "fsdp", scatter_dimension=0, tiled=True),
        lax.psum_scatter(upb_grad, "fsdp", scatter_dimension=0, tiled=True),
        lax.psum_scatter(down_grad, "fsdp", scatter_dimension=0, tiled=True),
        lax.psum_scatter(downb_grad, "fsdp", scatter_dimension=0, tiled=True),
    )
    shares = (
        lax.psum(shares[0].astype(jnp.bfloat16), "dp").astype(jnp.float32),
        lax.psum(shares[1].astype(jnp.bfloat16), "dp").astype(jnp.float32),
        lax.psum(shares[2].astype(jnp.bfloat16), "dp").astype(jnp.float32),
        lax.psum(shares[3].astype(jnp.bfloat16), "dp").astype(jnp.float32),
        lax.psum(shares[4].astype(jnp.bfloat16), "dp").astype(jnp.float32),
        lax.psum(shares[5].astype(jnp.bfloat16), "dp").astype(jnp.float32),
    )
    return tuple((share * factor for share in shares))


def reduce_attn(gain_grad, bias_grad, time_grad, qkv_grad, qkvb_grad, out_grad, outb_grad, factor):
    shares = (
        lax.psum_scatter(gain_grad, "fsdp", scatter_dimension=0, tiled=True),
        lax.psum_scatter(bias_grad, "fsdp", scatter_dimension=0, tiled=True),
        lax.psum_scatter(time_grad, "fsdp", scatter_dimension=0, tiled=True),
        lax.psum_scatter(qkv_grad, "fsdp", scatter_dimension=0, tiled=True),
        lax.psum_scatter(qkvb_grad, "fsdp", scatter_dimension=0, tiled=True),
        lax.psum_scatter(out_grad, "fsdp", scatter_dimension=0, tiled=True),
        lax.psum_scatter(outb_grad, "fsdp", scatter_dimension=0, tiled=True),
    )
    shares = (
        lax.psum(shares[0].astype(jnp.bfloat16), "dp").astype(jnp.float32),
        lax.psum(shares[1].astype(jnp.bfloat16), "dp").astype(jnp.float32),
        lax.psum(shares[2].astype(jnp.bfloat16), "dp").astype(jnp.float32),
        lax.psum(shares[3].astype(jnp.bfloat16), "dp").astype(jnp.float32),
        lax.psum(shares[4].astype(jnp.bfloat16), "dp").astype(jnp.float32),
        lax.psum(shares[5].astype(jnp.bfloat16), "dp").astype(jnp.float32),
        lax.psum(shares[6].astype(jnp.bfloat16), "dp").astype(jnp.float32),
    )
    return tuple((share * factor for share in shares))


def per_device(
    tokens,
    time_embed,
    segments,
    cotangent,
    attn_norm_gain,
    attn_norm_bias,
    time_weight,
    qkv_weight,
    qkv_bias,
    out_weight,
    out_bias,
    mlp_norm_gain,
    mlp_norm_bias,
    up_weight,
    up_bias,
    down_weight,
    down_bias,
):
    width = tokens.shape[1]
    rows, seq = segments.shape
    total_tokens = tokens.shape[0] * lax.axis_size("dp") * lax.axis_size("fsdp")
    factor = 1.0 / math.sqrt(total_tokens)
    attn_set = (
        lax.all_gather(attn_norm_gain, "fsdp", axis=0, tiled=True),
        lax.all_gather(attn_norm_bias, "fsdp", axis=0, tiled=True),
        lax.all_gather(time_weight, "fsdp", axis=0, tiled=True),
        lax.all_gather(qkv_weight, "fsdp", axis=0, tiled=True),
        lax.all_gather(qkv_bias, "fsdp", axis=0, tiled=True),
        lax.all_gather(out_weight, "fsdp", axis=0, tiled=True),
        lax.all_gather(out_bias, "fsdp", axis=0, tiled=True),
    )
    gain_one, bias_one, w_time, w_qkv, b_qkv, w_out, b_out = attn_set
    modulation = product(time_embed, w_time)
    tokens_float = tokens.astype(jnp.float32)
    norm_one, pull_one = jax.vjp(
        norm_mod,
        tokens_float,
        gain_one.astype(jnp.float32),
        bias_one.astype(jnp.float32),
        modulation[:, :width],
    )
    normed_one = norm_one.astype(jnp.bfloat16)
    qkv = product(normed_one, w_qkv) + b_qkv.astype(jnp.float32)
    heads = qkv.reshape(rows, seq, 3, HEADS, HEAD_DIM)
    cosine, sine = rotary_tables(positions_of(segments), HEAD_DIM)
    query = rotate(heads[:, :, 0], cosine, sine).astype(jnp.bfloat16)
    key = rotate(heads[:, :, 1], cosine, sine).astype(jnp.bfloat16)
    value = heads[:, :, 2].astype(jnp.bfloat16)
    mixed, logsum = lax.map(attend_forward, (query, key, value, segments))
    mixed_flat = mixed.reshape(rows * seq, width)
    hidden = tokens_float + product(mixed_flat, w_out) + b_out.astype(jnp.float32)
    mlp_set = (
        lax.all_gather(mlp_norm_gain, "fsdp", axis=0, tiled=True),
        lax.all_gather(mlp_norm_bias, "fsdp", axis=0, tiled=True),
        lax.all_gather(up_weight, "fsdp", axis=0, tiled=True),
        lax.all_gather(up_bias, "fsdp", axis=0, tiled=True),
        lax.all_gather(down_weight, "fsdp", axis=0, tiled=True),
        lax.all_gather(down_bias, "fsdp", axis=0, tiled=True),
    )
    gain_two, bias_two, w_up, b_up, w_down, b_down = mlp_set
    norm_two, pull_two = jax.vjp(
        norm_mod,
        hidden,
        gain_two.astype(jnp.float32),
        bias_two.astype(jnp.float32),
        modulation[:, width:],
    )
    normed_two = norm_two.astype(jnp.bfloat16)
    up = product(normed_two, w_up) + b_up.astype(jnp.float32)
    active_float, pull_gelu = jax.vjp(gelu_exact, up)
    active = active_float.astype(jnp.bfloat16)
    output = hidden + product(active, w_down) + b_down.astype(jnp.float32)
    layer_out = output.astype(jnp.bfloat16)
    mlp_back = (
        lax.all_gather(mlp_norm_gain, "fsdp", axis=0, tiled=True),
        lax.all_gather(mlp_norm_bias, "fsdp", axis=0, tiled=True),
        lax.all_gather(up_weight, "fsdp", axis=0, tiled=True),
        lax.all_gather(up_bias, "fsdp", axis=0, tiled=True),
        lax.all_gather(down_weight, "fsdp", axis=0, tiled=True),
        lax.all_gather(down_bias, "fsdp", axis=0, tiled=True),
    )
    w_up_back = mlp_back[2]
    w_down_back = mlp_back[4]
    grad_out = cotangent.astype(jnp.float32)
    down_bias_sum = jnp.sum(grad_out, axis=0)
    down_sum = product_left(active, cotangent)
    grad_active = product_right(cotangent, w_down_back)
    (grad_up,) = pull_gelu(grad_active)
    up_bias_sum = jnp.sum(grad_up, axis=0)
    grad_up_low = grad_up.astype(jnp.bfloat16)
    up_sum = product_left(normed_two, grad_up_low)
    grad_normed_two = product_right(grad_up_low, w_up_back)
    grad_hidden_part, gain_two_sum, bias_two_sum, grad_shift_two = pull_two(grad_normed_two)
    grad_hidden = grad_out + grad_hidden_part
    mlp_grads = reduce_mlp(
        gain_two_sum, bias_two_sum, up_sum, up_bias_sum, down_sum, down_bias_sum, factor
    )
    attn_back = (
        lax.all_gather(attn_norm_gain, "fsdp", axis=0, tiled=True),
        lax.all_gather(attn_norm_bias, "fsdp", axis=0, tiled=True),
        lax.all_gather(time_weight, "fsdp", axis=0, tiled=True),
        lax.all_gather(qkv_weight, "fsdp", axis=0, tiled=True),
        lax.all_gather(qkv_bias, "fsdp", axis=0, tiled=True),
        lax.all_gather(out_weight, "fsdp", axis=0, tiled=True),
        lax.all_gather(out_bias, "fsdp", axis=0, tiled=True),
    )
    w_qkv_back = attn_back[3]
    w_out_back = attn_back[5]
    out_bias_sum = jnp.sum(grad_hidden, axis=0)
    grad_hidden_low = grad_hidden.astype(jnp.bfloat16)
    out_sum = product_left(mixed_flat, grad_hidden_low)
    grad_mixed = product_right(grad_hidden_low, w_out_back).astype(jnp.bfloat16)
    grad_mixed = grad_mixed.reshape(rows, seq, HEADS, HEAD_DIM)
    query_grad, key_grad, value_grad = lax.map(
        attend_backward, (query, key, value, segments, grad_mixed, logsum)
    )
    query_grad = rotate(query_grad, cosine, -sine)
    key_grad = rotate(key_grad, cosine, -sine)
    grad_qkv = jnp.stack([query_grad, key_grad, value_grad], axis=2).reshape(rows * seq, 3 * width)
    qkv_bias_sum = jnp.sum(grad_qkv, axis=0)
    grad_qkv_low = grad_qkv.astype(jnp.bfloat16)
    qkv_sum = product_left(normed_one, grad_qkv_low)
    grad_normed_one = product_right(grad_qkv_low, w_qkv_back)
    grad_tokens_part, gain_one_sum, bias_one_sum, grad_shift_one = pull_one(grad_normed_one)
    tokens_grad = (grad_hidden + grad_tokens_part).astype(jnp.bfloat16)
    grad_shift = jnp.concatenate([grad_shift_one, grad_shift_two], axis=1).astype(jnp.bfloat16)
    time_sum = product_left(time_embed, grad_shift)
    attn_grads = reduce_attn(
        gain_one_sum, bias_one_sum, time_sum, qkv_sum, qkv_bias_sum, out_sum, out_bias_sum, factor
    )
    return (
        layer_out,
        tokens_grad,
        attn_grads[0],
        attn_grads[1],
        attn_grads[2],
        attn_grads[3],
        attn_grads[4],
        attn_grads[5],
        attn_grads[6],
        mlp_grads[0],
        mlp_grads[1],
        mlp_grads[2],
        mlp_grads[3],
        mlp_grads[4],
        mlp_grads[5],
    )


def solution(mesh):
    placed = (
        P(("dp", "fsdp"), None),
        P(("dp", "fsdp"), None),
        P(("dp", "fsdp"), None),
        P(("dp", "fsdp"), None),
        P("fsdp"),
        P("fsdp"),
        P("fsdp", None),
        P("fsdp", None),
        P("fsdp"),
        P("fsdp", None),
        P("fsdp"),
        P("fsdp"),
        P("fsdp"),
        P("fsdp", None),
        P("fsdp"),
        P("fsdp", None),
        P("fsdp"),
    )
    return jax.shard_map(
        per_device,
        mesh=mesh,
        in_specs=placed,
        out_specs=(
            P(("dp", "fsdp"), None),
            P(("dp", "fsdp"), None),
            P("fsdp"),
            P("fsdp"),
            P("fsdp", None),
            P("fsdp", None),
            P("fsdp"),
            P("fsdp", None),
            P("fsdp"),
            P("fsdp"),
            P("fsdp"),
            P("fsdp", None),
            P("fsdp"),
            P("fsdp", None),
            P("fsdp"),
        ),
        check_vma=False,
    )
```

profile of v0, /device:TPU:0, one launch (start us, length us, event | category | flops | bytes accessed | tf_op | source)
XLA Modules:
  0.0 1565.1 jit_solution(3748685506322900785)
XLA Ops:
  19.2 63.9 %all-reduce.16 = (bf16[1024]{0:T(1024)(128)(2,1)S(1)}, bf16[3072]{0:T(1024)(128)(2,1)S(1)}, bf16[1024]{0:T(1024)(128)(2,1)S(1)}, bf16[1024]{0:T(1024)(128)(2,1)S...) all-reduce(bf16[1024]{0:T(1024)(128)(2,1)S(1)} %dynamic-update-slic, ...), channel_id=1, replica_groups=mesh['dp'=2,'fsdp'=16] {'fsdp'}, use_global_device_ids=true, to_apply=%add.3 | all-reduce | flops 9216 | bytes 36864
  91.3 18.0 %all-gather = bf16[16,1,256]{2,1,0:T(2,128)(2,1)S(1)} all-gather(bf16[1,1,256]{2,1,0:T(2,128)(2,1)S(1)} %reshape.465), channel_id=1, replica_groups=mesh['dp'=2,'fsdp'=16] {'fsdp'}, dimensions={0}, use_global_device_ids=true | all-gather | bytes 8704 | tf_op jit(solution)/shard_map/all_gather | solution.py:229
  113.7 3.2 copy-done.8
  119.2 12.1 broadcast_add_fusion
  131.3 12.6 copy.53
  143.9 4.3 slice_bitcast_fusion
  148.3 3.9 fusion.111
  152.2 3.3 fusion.112
  158.5 2.6 concatenate.42
  165.9 96.3 %while.47 = (s32[]{:T(128)}, bf16[2,512,16,64]{1,3,2,0:T(8,128)(2,1)}, f32[2,16,512]{2,1,0:T(8,128)S(1)}, s32[2,512]{1,0:T(2,128)S(1)}, s32[1024]{0:T(1024)S(1)}...) while((s32[]{:T(128)}, ...), condition=%wide.region_7.8_spmd, body=%wide.region_4.7_spmd.sunk | while | flops 2249187328 | bytes 134490288 | solution.py:89
  166.5 15.4 fusion.187
  182.0 16.1 %fusion.188 = f32[16,512]{1,0:T(8,128)S(1)} fusion(f32[16,512,1024]{2,1,0:T(8,128)} %get-tuple-element.507, f32[16,512]{1,0:T(8,128)S(1)} %get-tuple-element.508, pred[512,1024]{1,0:T(8,128)(4,1)S(1)} %broadcast_compare_fusion.4), kind=kLoop, calls=%fused_computation.4.clone.1 | loop fusion | flops 33546240 | bytes 34144256 | tf_op jit(solution)/shard_map/while/body/eval_jaxpr/while/body/eval_jaxpr/reduce_sum | solution.py:84
  198.1 14.7 fusion.189
  214.5 15.7 %fusion.187 = (f32[16,512]{1,0:T(8,128)S(1)}, f32[16,512,1024]{2,1,0:T(8,128)}) fusion(pred[512,1024]{1,0:T(8,128)(4,1)S(1)} %broadcast_compare_fusion.4, bf16[1024,16,64]{0,2,1:T(8,128)(2,1)S(1)} %get-tuple-element.544, bf16[2,512,16,64]{1,3,2,0:T(8,128)(2,1)} %get-tuple-element.543, s32[]{:T(128)S(6)} %copy.107), kind=kOutput, calls=%fused_computation.3.clone.1 | convolution fusion | flops 1098899456 | bytes 37257220 | tf_op jit(solution)/shard_map/while/body/eval_jaxpr/while/body/eval_jaxpr/qhd,khd->hqk/dot_general | solution.py:67
  230.2 15.5 fusion.188
  245.8 14.7 fusion.189
  262.3 4.5 copy.56
  268.8 5.9 fusion.132
  279.6 16.2 %fusion.134 = f32[1024,4096]{1,0:T(8,128)} fusion(bf16[1024,1024]{1,0:T(8,128)(2,1)} %multiply_convert_fusion.3, bf16[1024,4096]{1,0:T(8,128)(2,1)} %all-gather.13.cloned.1.call-done), kind=kOutput, calls=%fused_computation.203 | convolution fusion | flops 8589934592 | bytes 27262976 | tf_op jit(solution)/shard_map/dot_general | solution.py:50
  295.8 10.4 all-gather.15.cloned.1.call-done
  306.2 52.1 %fusion.126 = (f32[4096]{0:T(1024)}, bf16[1024,4096]{1,0:T(8,128)(2,1)}, f32[1024,4096]{1,0:T(8,128)}) fusion(f32[1024,4096]{1,0:T(8,128)} %fusion.134, f32[4096]{0:T(1024)S(1)} %bitcast.170, bf16[1024,1024]{1,0:T(8,128)(2,1)S(1)} %copy-done.14, bf16[4096,1024]{1,0:T(8,128)(2,1)} %all-gather.15.cloned.1.call-done), kind=kOutput, calls=%fused_computation.198 | convolution fusion | flops 8900308992 | bytes 52461568 | tf_op jit(solution)/shard_map/dot_general | solution.py:60
  358.4 18.2 %multiply_reduce_fusion.1 = (f32[1024]{0:T(1024)}, f32[1024]{0:T(1024)S(1)}, f32[1024]{0:T(1024)}, f32[1024,1024]{1,0:T(8,128)}, bf16[1024,1024]{1,0:T(8,128)(2,1)}) fusion(f32[1024,1024]{1,0:T(8,128)} %copy-done.10, f32[1024]{0:T(1024)S(1)} %copy-done.43, f32[1024]{0:T(1024)S(1)} %copy-done.33, f32[1024]{0:T(1024)S(1)} %copy-done.41, ...), kind=kOutput, calls=%fused_computation.118 | convolution fusion | flops 8604611584 | bytes 31485952 | tf_op jit(solution)/shard_map/dot_general | solution.py:60
  376.5 4.4 fusion.129
  383.1 3.8 convolution_convert_fusion
  386.9 6.4 reshape.482
  393.3 5.6 copy.59
  398.9 405.5 %while.48 = (s32[]{:T(128)}, f32[1024,16,64]{0,2,1:T(8,128)}, f32[1024,16,64]{0,2,1:T(8,128)}, f32[2,512,16,64]{1,0,3,2:T(2,128)}, bf16[2,512,16,64]{1,3,2,0:T(8...) while((s32[]{:T(128)}, f32[1024,16,64]{0,2,1:T(8,128)}, ...), condition=%wide.region_14.15_spmd.clone, body=%wide.region_12.14_spmd.clone.sunk | while | flops 5591549952 | bytes 350955680 | solution.py:125
  399.4 17.7 %fusion.200 = f32[16,512,1024]{2,1,0:T(8,128)} fusion(bf16[1024,16,64]{0,2,1:T(8,128)(2,1)} %get-tuple-element.583, bf16[2,512,16,64]{1,3,2,0:T(8,128)(2,1)} %get-tuple-element.582, s32[]{:T(128)S(6)} %copy.117), kind=kOutput, calls=%fused_computation.40.clone.1 | convolution fusion | flops 1073741824 | bytes 36700164 | tf_op jit(solution)/shard_map/while/body/eval_jaxpr/while/body/eval_jaxpr/qhd,khd->hqk/dot_general | solution.py:107
  417.0 13.1 fusion.201
  430.5 57.0 %bitcast_add_fusion.4 = f32[1024,16,64]{0,2,1:T(8,128)} fusion(f32[1024,16,64]{0,2,1:T(8,128)} %get-tuple-element.561, f32[16,512,1024]{2,1,0:T(8,128)} %fusion.200, f32[16,512,1024]{2,1,0:T(8,128)} %fusion.201, f32[16,512]{1,0:T(8,128)S(1)} %dynamic-slice_bitcast_fusion.2, pred[512,1024]{1,0:T(8,128)(4,1)S(1)} %broadcast_compare_fusion.5, ...), kind=kOutput, calls=%fused_computation.37.clone.1 | convolution fusion | flops 1168122880 | bytes 144769024 | tf_op jit(solution)/shard_map/while/body/eval_jaxpr/while/body/eval_jaxpr/hqk,qhd->khd/dot_general | solution.py:113
  487.5 17.6 %bitcast_add_fusion.5 = f32[1024,16,64]{0,2,1:T(8,128)} fusion(f32[1024,16,64]{0,2,1:T(8,128)} %get-tuple-element.562, f32[16,512,1024]{2,1,0:T(8,128)} %fusion.201, f32[16,512]{1,0:T(8,128)S(1)} %dynamic-slice_bitcast_fusion.2, pred[512,1024]{1,0:T(8,128)(4,1)S(1)} %broadcast_compare_fusion.5, pred[]{:T(512)S(6)} %compare.3, ...), kind=kOutput, calls=%fused_computation.36.clone.1 | convolution fusion | flops 1109393408 | bytes 43548676 | tf_op jit(solution)/shard_map/while/body/eval_jaxpr/while/body/eval_jaxpr/hqk,qhd->khd/dot_general | solution.py:116
  505.1 52.5 %fusion.202 = f32[1,512,16,64]{1,3,2,0:T(8,128)} fusion(bf16[1024,16,64]{0,2,1:T(8,128)(2,1)S(1)} %get-tuple-element.580, f32[16,512,1024]{2,1,0:T(8,128)} %fusion.200, f32[16,512,1024]{2,1,0:T(8,128)} %fusion.201, f32[16,512]{1,0:T(8,128)S(1)} %dynamic-slice_bitcast_fusion.2, pred[512,1024]{1,0:T(8,128)(4,1)S(1)} %broadcast_compare_fusion.5), kind=kOutput, calls=%fused_computation.38.clone.1 | convolution fusion | flops 1166025728 | bytes 71860224 | tf_op jit(solution)/shard_map/while/body/eval_jaxpr/while/body/eval_jaxpr/hqk,khd->qhd/dot_general | solution.py:112
  557.6 5.1 copy.92
  562.8 38.1 %dynamic_update_slice.33 = f32[2,512,16,64]{1,0,3,2:T(2,128)} dynamic-update-slice(f32[2,512,16,64]{1,0,3,2:T(2,128)} %get-tuple-element.563, f32[1,512,16,64]{1,0,3,2:T(1,128)} %copy.92, s32[]{:T(128)S(6)} %copy.117, s32[]{:T(128)} %constant.49.clone.1..sunk, s32[]{:T(128)} %constant.49.clone.1..sunk, s32[]{:T(128)} %constant.49.clone.1..sunk) | dynamic-update-slice | bytes 4194308 | tf_op jit(solution)/shard_map/while/body/eval_jaxpr/while/body/jit(dynamic_update_index_in_dim)/dynamic_update_slice | solution.py:125
  600.9 17.7 %fusion.200 = f32[16,512,1024]{2,1,0:T(8,128)} fusion(bf16[1024,16,64]{0,2,1:T(8,128)(2,1)} %get-tuple-element.583, bf16[2,512,16,64]{1,3,2,0:T(8,128)(2,1)} %get-tuple-element.582, s32[]{:T(128)S(6)} %copy.117), kind=kOutput, calls=%fused_computation.40.clone.1 | convolution fusion | flops 1073741824 | bytes 36700164 | tf_op jit(solution)/shard_map/while/body/eval_jaxpr/while/body/eval_jaxpr/qhd,khd->hqk/dot_general | solution.py:107
  618.6 13.1 fusion.201
  632.1 57.5 %bitcast_add_fusion.4 = f32[1024,16,64]{0,2,1:T(8,128)} fusion(f32[1024,16,64]{0,2,1:T(8,128)} %get-tuple-element.561, f32[16,512,1024]{2,1,0:T(8,128)} %fusion.200, f32[16,512,1024]{2,1,0:T(8,128)} %fusion.201, f32[16,512]{1,0:T(8,128)S(1)} %dynamic-slice_bitcast_fusion.2, pred[512,1024]{1,0:T(8,128)(4,1)S(1)} %broadcast_compare_fusion.5, ...), kind=kOutput, calls=%fused_computation.37.clone.1 | convolution fusion | flops 1168122880 | bytes 144769024 | tf_op jit(solution)/shard_map/while/body/eval_jaxpr/while/body/eval_jaxpr/hqk,qhd->khd/dot_general | solution.py:113
  689.6 18.9 %bitcast_add_fusion.5 = f32[1024,16,64]{0,2,1:T(8,128)} fusion(f32[1024,16,64]{0,2,1:T(8,128)} %get-tuple-element.562, f32[16,512,1024]{2,1,0:T(8,128)} %fusion.201, f32[16,512]{1,0:T(8,128)S(1)} %dynamic-slice_bitcast_fusion.2, pred[512,1024]{1,0:T(8,128)(4,1)S(1)} %broadcast_compare_fusion.5, pred[]{:T(512)S(6)} %compare.3, ...), kind=kOutput, calls=%fused_computation.36.clone.1 | convolution fusion | flops 1109393408 | bytes 43548676 | tf_op jit(solution)/shard_map/while/body/eval_jaxpr/while/body/eval_jaxpr/hqk,qhd->khd/dot_general | solution.py:116
  708.5 52.5 %fusion.202 = f32[1,512,16,64]{1,3,2,0:T(8,128)} fusion(bf16[1024,16,64]{0,2,1:T(8,128)(2,1)S(1)} %get-tuple-element.580, f32[16,512,1024]{2,1,0:T(8,128)} %fusion.200, f32[16,512,1024]{2,1,0:T(8,128)} %fusion.201, f32[16,512]{1,0:T(8,128)S(1)} %dynamic-slice_bitcast_fusion.2, pred[512,1024]{1,0:T(8,128)(4,1)S(1)} %broadcast_compare_fusion.5), kind=kOutput, calls=%fused_computation.38.clone.1 | convolution fusion | flops 1166025728 | bytes 71860224 | tf_op jit(solution)/shard_map/while/body/eval_jaxpr/while/body/eval_jaxpr/hqk,khd->qhd/dot_general | solution.py:112
  761.0 5.1 copy.92
  766.1 38.1 %dynamic_update_slice.33 = f32[2,512,16,64]{1,0,3,2:T(2,128)} dynamic-update-slice(f32[2,512,16,64]{1,0,3,2:T(2,128)} %get-tuple-element.563, f32[1,512,16,64]{1,0,3,2:T(1,128)} %copy.92, s32[]{:T(128)S(6)} %copy.117, s32[]{:T(128)} %constant.49.clone.1..sunk, s32[]{:T(128)} %constant.49.clone.1..sunk, s32[]{:T(128)} %constant.49.clone.1..sunk) | dynamic-update-slice | bytes 4194308 | tf_op jit(solution)/shard_map/while/body/eval_jaxpr/while/body/jit(dynamic_update_index_in_dim)/dynamic_update_slice | solution.py:125
  804.5 6.7 broadcast_in_dim.100
  811.1 4.7 multiply_subtract_fusion.1
  815.8 4.2 maximum_bitcast_fusion
  820.0 8.6 fusion.82
  828.6 14.4 fusion.125
  843.0 2.8 fusion.108
  845.8 2.9 copy.68
  848.8 7.9 fusion.114
  856.7 12.5 fusion.135
  869.3 16.2 %fusion.102 = f32[1024,4096]{1,0:T(8,128)} fusion(bf16[1024,1024]{1,0:T(8,128)(2,1)} %multiply_convert_fusion.3, bf16[1024,4096]{1,0:T(8,128)(2,1)} %get-tuple-element.363), kind=kOutput, calls=%fused_computation.122 | convolution fusion | flops 8589934592 | bytes 27262976 | tf_op jit(solution)/shard_map/dot_general | solution.py:54
  886.2 12.5 multiply_convert_fusion.1
  898.7 3.3 copy-done.13
  902.0 11.5 fusion.136
  916.1 5.8 fusion.81
  922.0 4.4 fusion.94
  926.7 5.0 convert_reduce_fusion.1
  931.6 60.1 %all-reduce.15 = (bf16[1024]{0:T(1024)(128)(2,1)S(1)}, bf16[1024]{0:T(1024)(128)(2,1)S(1)}, bf16[3072]{0:T(1024)(128)(2,1)S(1)}, bf16[1024]{0:T(1024)(128)(2,1)S...) all-reduce(f32[1024]{0:T(1024)S(1)} %get-tuple-element.289, ...), channel_id=2, replica_groups=mesh['dp'=2,'fsdp'=16] {'fsdp'}, use_global_device_ids=true, to_apply=%region_18.19.clone | all-reduce | flops 13312 | bytes 79872
  992.3 4.9 all-reduce.17
  1005.0 118.3 %reduce-scatter.8.cloned.1.call-done = f32[64,3072]{1,0:T(8,128)} async-done(((f32[1024,3072]{1,0:T(8,128)}), f32[64,3072]{1,0:T(8,128)}) %reduce-scatter.8.cloned.1.call-update) | async-done | bytes 786448 | tf_op jit(solution)/shard_map/reduce_scatter | solution.py:156
  1125.3 178.8 %reduce-scatter.12.cloned.1.call-done = f32[64,4096]{1,0:T(8,128)} async-done(((f32[1024,4096]{1,0:T(8,128)}), f32[64,4096]{1,0:T(8,128)}) %reduce-scatter.12.cloned.1.call-update) | async-done | bytes 1048592 | tf_op jit(solution)/shard_map/reduce_scatter | solution.py:135
  1306.2 178.4 %reduce-scatter.14.cloned.1.call-done = f32[256,1024]{1,0:T(8,128)} async-done(((f32[4096,1024]{1,0:T(8,128)}), f32[256,1024]{1,0:T(8,128)}) %reduce-scatter.14.cloned.1.call-update) | async-done | bytes 1048592 | tf_op jit(solution)/shard_map/reduce_scatter | solution.py:137
  1486.7 15.3 add_convert_fusion.1
  1501.9 48.5 %all-reduce.21.cloned.1.call-done = (bf16[16,2048]{0,1:T(8,128)(2,1)}, bf16[64,3072]{1,0:T(8,128)(2,1)}, bf16[64,1024]{1,0:T(8,128)(2,1)}, bf16[64,4096]{1,0:T(8,128)(2,1)}, bf16[256,1024]{1,0:T(8,128)(2,1)}) async-done(((bf16[16,2048]{0,1:T(8,128)(2,1)}, bf16[64,3072]{1,0:T(8,128)(2,1)}, bf16[64,1024]{1,0:T(8,128)(2,1)}, bf16[64,4096]{1,0:T(8,128)(2,1)}, bf16[256,1024]{1,0:T(8,128)(2,1)}), ...) | async-done | bytes 1638416 | tf_op jit(solution)/shard_map/psum | solution.py:164
  (265 shorter events, 70.4 us)
Async XLA Ops:
  7.2 103.9 %copy-start = (bf16[1024,256]{1,0:T(8,128)(2,1)S(1)}, bf16[1024,256]{1,0:T(8,128)(2,1)}, u32[]{:S(2)}) copy-start(bf16[1024,256]{1,0:T(8,128)(2,1)} %param.22) | copy-start | bytes 1572868
  7.2 81.3 %copy-start.6 = (bf16[1024,1024]{1,0:T(8,128)(2,1)S(1)}, bf16[1024,1024]{1,0:T(8,128)(2,1)}, u32[]{:S(2)}) copy-start(bf16[1024,1024]{1,0:T(8,128)(2,1)} %param.21) | copy-start | bytes 6291460
  7.2 84.1 %copy-start.60 = (bf16[256]{0:T(256)(128)(2,1)S(1)}, bf16[256]{0:T(256)(128)(2,1)}, u32[]{:S(2)}) copy-start(bf16[256]{0:T(256)(128)(2,1)} %param.35) | copy-start | bytes 1540
  7.2 103.9 %all-gather.7.cloned.1.call-start = ((), (), s32[]{:S(2)}) async-start(), calls=%async_computation.5 | async-start | bytes 1114112 | tf_op jit(solution)/shard_map/all_gather | solution.py:199
  8.0 111.3 %all-gather.9.cloned.1.call-start = ((), (), s32[]{:S(2)}) async-start(), calls=%async_computation.6 | async-start | bytes 6684672 | tf_op jit(solution)/shard_map/all_gather | solution.py:200
  8.7 260.0 %all-gather.11.cloned.1.call-start = ((), (), s32[]{:S(2)}) async-start(), calls=%async_computation.7 | async-start | bytes 2228224 | tf_op jit(solution)/shard_map/all_gather | solution.py:202
  9.4 270.2 %all-gather.13.cloned.1.call-start = ((), (), s32[]{:S(2)}) async-start(), calls=%async_computation.8 | async-start | bytes 8912896 | tf_op jit(solution)/shard_map/all_gather | solution.py:228
  10.0 296.2 %all-gather.15.cloned.1.call-start = ((), (), s32[]{:S(2)}) async-start(), calls=%async_computation.9 | async-start | bytes 8912896 | tf_op jit(solution)/shard_map/all_gather | solution.py:230
  10.6 990.8 %reduce-scatter.16.cloned.1.call-start = ((), (), s32[]{:S(2)}) async-start(), calls=%async_computation.14 | async-start | bytes 2228224
  86.5 27.2 %copy-start.50 = (f32[1024]{0:T(1024)}, f32[1024]{0:T(1024)S(1)}, u32[]{:S(2)}) copy-start(f32[1024]{0:T(1024)S(1)} %convert_element_type.180) | copy-start | bytes 12292
  86.5 27.2 %copy-start.34 = (f32[1024]{0:T(1024)}, f32[1024]{0:T(1024)S(1)}, u32[]{:S(2)}) copy-start(f32[1024]{0:T(1024)S(1)} %convert_element_type.179) | copy-start | bytes 12292
  88.5 25.2 %copy-start.30 = (f32[1024]{0:T(1024)}, f32[1024]{0:T(1024)S(1)}, u32[]{:S(2)}) copy-start(f32[1024]{0:T(1024)S(1)} %broadcast_multiply_fusion.1) | copy-start | bytes 12292
  89.2 24.5 %copy-start.36 = (f32[1024]{0:T(1024)}, f32[1024]{0:T(1024)S(1)}, u32[]{:S(2)}) copy-start(f32[1024]{0:T(1024)S(1)} %fusion.120) | copy-start | bytes 12292
  111.1 41.1 %copy-start.19 = (f32[1024,32]{0,1:T(8,128)}, f32[1024,32]{0,1:T(8,128)S(1)}, u32[]{:S(2)}) copy-start(f32[1024,32]{0,1:T(8,128)S(1)} %get-tuple-element.390) | copy-start | bytes 393220
  113.7 3.2 copy-start.8
  158.5 7.5 copy-start.21
  182.0 16.1 %copy-start.3 = (bf16[1024,16,64]{0,2,1:T(8,128)(2,1)S(1)}, bf16[1024,16,64]{0,2,1:T(8,128)(2,1)}, u32[]{:S(2)}) copy-start(bf16[1024,16,64]{0,2,1:T(8,128)(2,1)} %get-tuple-element.545) | copy-start | bytes 6291460 | tf_op jit(solution)/shard_map/while/body/eval_jaxpr/while
  182.0 16.1 %copy-start.17 = (bf16[2,512,16,64]{1,3,2,0:T(8,128)(2,1)S(1)}, bf16[2,512,16,64]{1,3,2,0:T(8,128)(2,1)}, u32[]{:S(2)}) copy-start(bf16[2,512,16,64]{1,3,2,0:T(8,128)(2,1)} %get-tuple-element.530) | copy-start | bytes 6291460 | tf_op jit(solution)/shard_map/while/body/eval_jaxpr/while
  230.2 15.6 copy-start.3
  230.2 15.6 copy-start.17
  262.2 6.5 copy-start.1
  262.3 6.5 copy-start.26
  262.3 6.4 copy-start.28
  262.3 6.5 copy-start.55
  268.7 8.5 slice-start
  268.8 8.5 slice-start.1
  279.6 26.6 %copy-start.14 = (bf16[1024,1024]{1,0:T(8,128)(2,1)S(1)}, bf16[1024,1024]{1,0:T(8,128)(2,1)}, u32[]{:S(2)}) copy-start(bf16[1024,1024]{1,0:T(8,128)(2,1)} %param.24) | copy-start | bytes 6291460
  279.6 26.6 %copy-start.38 = (f32[16,1,256]{2,1,0:T(1,128)S(1)}, f32[16,1,256]{2,1,0:T(1,128)}, u32[]{:S(2)}) copy-start(f32[16,1,256]{2,1,0:T(1,128)} %convert_element_type.226) | copy-start | bytes 49156
  306.2 52.1 %copy-start.9 = (f32[1024,2048]{1,0:T(8,128)S(1)}, f32[1024,2048]{1,0:T(8,128)}, u32[]{:S(2)}) copy-start(f32[1024,2048]{1,0:T(8,128)} %copy-done.8) | copy-start | bytes 25165828
  306.2 52.1 %copy-start.33 = (f32[1024]{0:T(1024)S(1)}, f32[1024]{0:T(1024)}, u32[]{:S(2)}) copy-start(f32[1024]{0:T(1024)} %copy-done.32) | copy-start | bytes 12292
  306.2 52.1 %copy-start.41 = (f32[1024]{0:T(1024)S(1)}, f32[1024]{0:T(1024)}, u32[]{:S(2)}) copy-start(f32[1024]{0:T(1024)} %convert_element_type.186) | copy-start | bytes 12292
  306.2 52.1 %copy-start.43 = (f32[1024]{0:T(1024)S(1)}, f32[1024]{0:T(1024)}, u32[]{:S(2)}) copy-start(f32[1024]{0:T(1024)} %copy-done.42) | copy-start | bytes 12292
  306.2 52.1 %copy-start.49 = (f32[1024]{0:T(1024)S(1)}, f32[1024]{0:T(1024)}, u32[]{:S(2)}) copy-start(f32[1024]{0:T(1024)} %convert_element_type.187) | copy-start | bytes 12292
  358.3 18.2 %copy-start.47 = (f32[1024]{0:T(1024)S(1)}, f32[1024]{0:T(1024)}, u32[]{:S(2)}) copy-start(f32[1024]{0:T(1024)} %copy-done.46) | copy-start | bytes 12292
  376.5 6.5 copy-start.59
  393.3 5.6 copy-start.2
  393.3 5.6 copy-start.22
  393.3 5.6 copy-start.27
  393.3 5.6 copy-start.29
  399.4 17.7 %copy-start.5 = (bf16[2,512,16,64]{1,3,2,0:T(8,128)(2,1)S(1)}, bf16[2,512,16,64]{1,3,2,0:T(8,128)(2,1)}, u32[]{:S(2)}) copy-start(bf16[2,512,16,64]{1,3,2,0:T(8,128)(2,1)} %get-tuple-element.577) | copy-start | bytes 6291460 | tf_op jit(solution)/shard_map/while/body/eval_jaxpr/while
  600.9 17.7 %copy-start.5 = (bf16[2,512,16,64]{1,3,2,0:T(8,128)(2,1)S(1)}, bf16[2,512,16,64]{1,3,2,0:T(8,128)(2,1)}, u32[]{:S(2)}) copy-start(bf16[2,512,16,64]{1,3,2,0:T(8,128)(2,1)} %get-tuple-element.577) | copy-start | bytes 6291460 | tf_op jit(solution)/shard_map/while/body/eval_jaxpr/while
  804.4 6.7 copy-start.20
  804.4 6.7 copy-start.23
  820.0 8.6 copy-start.7
  820.0 8.6 copy-start.31
  820.0 8.6 copy-start.35
  820.0 8.6 copy-start.37
  820.0 8.6 copy-start.51
  828.6 14.4 copy-start.61
  848.7 154.7 %reduce-scatter.10.cloned.1.call-start = ((), (), s32[]{:S(2)}) async-start(), calls=%async_computation.11 | async-start | bytes 4456448 | tf_op jit(solution)/shard_map/reduce_scatter | solution.py:158
  856.7 266.6 %reduce-scatter.8.cloned.1.call-start = ((), (), s32[]{:S(2)}) async-start(), calls=%async_computation.10 | async-start | bytes 13369344 | tf_op jit(solution)/shard_map/reduce_scatter | solution.py:156
  869.2 434.9 %reduce-scatter.12.cloned.1.call-start = ((), (), s32[]{:S(2)}) async-start(), calls=%async_computation.12 | async-start | bytes 17825792 | tf_op jit(solution)/shard_map/reduce_scatter | solution.py:135
  885.5 599.1 %reduce-scatter.14.cloned.1.call-start = ((), (), s32[]{:S(2)}) async-start(), calls=%async_computation.13 | async-start | bytes 17825792 | tf_op jit(solution)/shard_map/reduce_scatter | solution.py:137
  886.2 15.8 %copy-start.15 = (bf16[1024,1024]{1,0:T(8,128)(2,1)S(1)}, bf16[1024,1024]{1,0:T(8,128)(2,1)}, u32[]{:S(2)}) copy-start(bf16[1024,1024]{1,0:T(8,128)(2,1)} %param.24) | copy-start | bytes 6291460
  898.6 3.3 copy-start.13
  913.5 636.9 %all-reduce.21.cloned.1.call-start = ((), (), s32[]{:S(2)}) async-start(), calls=%async_computation.15 | async-start | bytes 4194304 | tf_op jit(solution)/shard_map/psum | solution.py:164
  916.1 5.9 copy-start.45
  922.0 4.4 copy-start.12
  922.0 4.7 copy-start.16
  926.6 5.0 copy-start.54
  926.6 5.0 copy-start.56
  926.6 5.0 copy-start.57
  1550.4 5.8 copy-start.25
  1550.4 6.8 copy-start.24
  (15 other events, 25.7 us)
Sparse Core Ops, SparseCore 0:
  10.2 40.6 all-gather.6
  53.2 60.4 all-gather.8
  115.9 40.2 all-gather.10
  158.2 73.0 all-gather.12
  233.3 72.8 all-gather.14
  848.8 60.3 reduce-scatter.15
  913.1 72.1 reduce-scatter.9
  989.4 133.8 reduce-scatter.7
  1127.4 176.6 reduce-scatter.11
  1308.1 176.4 reduce-scatter.13
  1488.2 62.1 all-reduce.20
where the time goes:
time: 1580 us; the launch traced here: 1570 us
  matrix products  569 us (36%)
  waiting for transfers between devices  538 us (34%)
  local copies, waits for them, and re-layouts  170 us (11%)
  blocking collectives  147 us (9%)
  other arithmetic  121 us (8%)
  between operations  18.2 us (1%)
    reduce_scatter x1, waiting for transfers between devices, reduce_mlp(): lax.psum_scatter(up_grad, 'fsdp', scatter_dimension=0, tiled=True)  179 us
    reduce_scatter x1, waiting for transfers between devices, reduce_mlp(): lax.psum_scatter(down_grad, 'fsdp', scatter_dimension=0, tiled=True)  178 us
    unnamed x2, blocking collectives  124 us
    reduce_scatter x1, waiting for transfers between devices, reduce_attn(): lax.psum_scatter(qkv_grad, 'fsdp', scatter_dimension=0, tiled=True)  118 us
    dot_general x2, matrix products, one_block(): jnp.einsum('hqk,qhd->khd', grad_raw, query_block, preferred_element_type=...  115 us
    dot_general x2, matrix products, one_block(): jnp.einsum('hqk,khd->qhd', grad_raw, key, preferred_element_type=jnp.floa...  105 us
    dot_general x4, matrix products, product_right(): lax.dot_general(left, right, (((1,), (1,)), ((), ())), preferred_element_...  88.5 us
    dynamic_update_slice x4, local copies, waits for them, and re-layouts, attend_backward(): lax.scan(one_block, (zeros_kv, zeros_kv), (query_blocks, seg_blocks, grad...  86.5 us
  transfers between devices with their start and end apart: 11, of which 5 were waited for; matrix products, arithmetic and copies ran while one was open for 19% of the time, Pallas kernels for 0%

commit v1 on v0

v1 whole, which is shorter than its diff:
```python
import functools
import math

import jax
import jax.numpy as jnp
from jax import lax
from jax.experimental import pallas as pl
from jax.experimental.pallas import tpu as pltpu
from jax.sharding import PartitionSpec as P

HEADS = 16
HEAD_DIM = 64
LANES = 128
BLOCK = 256


def positions_of(segments):
    index = jnp.broadcast_to(jnp.arange(segments.shape[1], dtype=jnp.int32), segments.shape)
    starts = jnp.concatenate(
        [jnp.ones((segments.shape[0], 1), dtype=bool), segments[:, 1:] != segments[:, :-1]], axis=1
    )
    first = lax.cummax(jnp.where(starts, index, jnp.zeros_like(index)), axis=1)
    return index - first


def rotary_tables(positions, head_width):
    steps_half = jnp.arange(head_width // 2, dtype=jnp.float32)
    inverse = jnp.exp(steps_half * (-2.0 * math.log(10000.0) / head_width))
    angles = positions.astype(jnp.float32)[..., None] * inverse
    return (jnp.cos(angles), jnp.sin(angles))


def block_bounds(segments, block):
    rows, seq = segments.shape
    parts = segments.reshape(rows, seq // block, block)
    first, last = (parts[:, :, 0], parts[:, :, -1])
    low = jnp.sum((last[:, None, :] < first[:, :, None]).astype(jnp.int32), axis=-1)
    high = jnp.sum((first[:, None, :] <= last[:, :, None]).astype(jnp.int32), axis=-1)
    return (low, high - low)


def partner(values, lane):
    ahead = pltpu.roll(values, LANES - HEAD_DIM // 2, 1)
    behind = pltpu.roll(values, HEAD_DIM // 2, 1)
    return jnp.where(lane % HEAD_DIM < HEAD_DIM // 2, ahead, behind)


def head_masks():
    lane = lax.broadcasted_iota(jnp.int32, (1, LANES), 1)
    own = (lane < HEAD_DIM).astype(jnp.float32)
    return (own.astype(jnp.bfloat16), (1.0 - own).astype(jnp.bfloat16))


def dot_nt(left, right):
    return lax.dot_general(
        left, right, (((1,), (1,)), ((), ())), preferred_element_type=jnp.float32
    )


def dot_tn(left, right):
    return lax.dot_general(
        left, right, (((0,), (0,)), ((), ())), preferred_element_type=jnp.float32
    )


def same_document(col_ref, row_ref, start, size, at, block):
    col = col_ref[pl.ds(start, size), :]
    row = row_ref[0, :, pl.ds(at, block)]
    return jnp.concatenate([col] * (block // LANES), axis=1) == row


def forward_kernel(
    low_ref, count_ref, q_ref, k_ref, v_ref, cos_ref, sin_ref, col_ref, row_ref,
    mixed_ref, query_ref, key_ref, value_ref, lse_ref, *, block
):
    row_at = pl.program_id(0)
    seq = q_ref.shape[0]
    blocks = seq // block
    lane = lax.broadcasted_iota(jnp.int32, (seq, LANES), 1)
    cosine, sine = (cos_ref[...], sin_ref[...])
    q, k = (q_ref[...], k_ref[...])
    rotated = q * cosine + partner(q, lane) * sine
    query_ref[...] = rotated.astype(jnp.bfloat16) * jnp.bfloat16(HEAD_DIM**-0.5)
    key_ref[...] = (k * cosine + partner(k, lane) * sine).astype(jnp.bfloat16)
    value_ref[...] = v_ref[...].astype(jnp.bfloat16)
    masks = head_masks()

    def one_block(i, carry):
        at = pl.multiple_of(i * block, block)
        low = low_ref[row_at, i]
        count = count_ref[row_at, i]
        start = pl.multiple_of(low * block, block)
        for size_at in range(1, blocks + 1):

            @pl.when(count == size_at)
            def _(size=size_at * block):
                keys = key_ref[pl.ds(start, size), :]
                values = value_ref[pl.ds(start, size), :]
                query = query_ref[pl.ds(at, block), :]
                same = same_document(col_ref, row_ref, start, size, at, block)
                weights = []
                for head in range(2):
                    scores = jnp.where(same, dot_nt(keys, query * masks[head]), -1e30)
                    peak = jnp.max(scores, axis=0, keepdims=True)
                    expo = jnp.exp(scores - peak)
                    total = jnp.sum(expo, axis=0, keepdims=True)
                    lse_ref[0, pl.ds(head, 1), pl.ds(at, block)] = peak + jnp.log(total)
                    weights.append((expo * (1.0 / total)).astype(jnp.bfloat16))
                mixed = dot_tn(weights[0], values * masks[0]) + dot_tn(
                    weights[1], values * masks[1]
                )
                mixed_ref[pl.ds(at, block), :] = mixed.astype(jnp.bfloat16)

        return carry

    lax.fori_loop(0, blocks, one_block, 0)


def backward_kernel(
    low_ref, count_ref, query_ref, key_ref, value_ref, grad_ref, lse_ref, cos_ref, sin_ref,
    col_ref, row_ref, gq_ref, gk_ref, gv_ref, bias_ref, dq_acc, dk_acc, dv_acc, *, block
):
    row_at = pl.program_id(0)
    seq = query_ref.shape[0]
    blocks = seq // block
    dk_acc[...] = jnp.zeros_like(dk_acc)
    dv_acc[...] = jnp.zeros_like(dv_acc)
    masks = head_masks()

    def one_block(i, carry):
        at = pl.multiple_of(i * block, block)
        low = low_ref[row_at, i]
        count = count_ref[row_at, i]
        start = pl.multiple_of(low * block, block)
        for size_at in range(1, blocks + 1):

            @pl.when(count == size_at)
            def _(size=size_at * block):
                keys = key_ref[pl.ds(start, size), :]
                values = value_ref[pl.ds(start, size), :]
                query = query_ref[pl.ds(at, block), :]
                grad = grad_ref[pl.ds(at, block), :]
                same = same_document(col_ref, row_ref, start, size, at, block)
                dq = jnp.zeros((block, LANES), jnp.float32)
                dk = jnp.zeros((size, LANES), jnp.float32)
                dv = jnp.zeros((size, LANES), jnp.float32)
                for head in range(2):
                    own_query = query * masks[head]
                    own_grad = grad * masks[head]
                    scores = jnp.where(same, dot_nt(keys, own_query), -1e30)
                    lse = lse_ref[0, pl.ds(head, 1), pl.ds(at, block)]
                    probs = jnp.exp(scores - lse)
                    grad_probs = dot_nt(values, own_grad)
                    inner = jnp.sum(probs * grad_probs, axis=0, keepdims=True)
                    grad_raw = (probs * (grad_probs - inner)).astype(jnp.bfloat16)
                    dv = dv + jnp.dot(
                        probs.astype(jnp.bfloat16), own_grad, preferred_element_type=jnp.float32
                    )
                    dk = dk + jnp.dot(grad_raw, own_query, preferred_element_type=jnp.float32)
                    dq = dq + dot_tn(grad_raw, keys * masks[head])
                dq_acc[pl.ds(at, block), :] = dq
                dk_acc[pl.ds(start, size), :] += dk
                dv_acc[pl.ds(start, size), :] += dv

        return carry

    lax.fori_loop(0, blocks, one_block, 0)
    lane = lax.broadcasted_iota(jnp.int32, (seq, LANES), 1)
    cosine, sine = (cos_ref[...], sin_ref[...])
    dq = dq_acc[...] * (HEAD_DIM**-0.5)
    dk = dk_acc[...]
    dv = dv_acc[...]
    gq = dq * cosine - partner(dq, lane) * sine
    gk = dk * cosine - partner(dk, lane) * sine
    gq_ref[...] = gq.astype(jnp.bfloat16)
    gk_ref[...] = gk.astype(jnp.bfloat16)
    gv_ref[...] = dv.astype(jnp.bfloat16)
    bias_ref[0, 0:1, :] = jnp.sum(gq, axis=0, keepdims=True)
    bias_ref[0, 1:2, :] = jnp.sum(gk, axis=0, keepdims=True)
    bias_ref[0, 2:3, :] = jnp.sum(dv, axis=0, keepdims=True)


def attention_tables(segments):
    rows, seq = segments.shape
    cosine, sine = rotary_tables(positions_of(segments), HEAD_DIM)
    reach = (rows * seq, HEAD_DIM // 2)
    cosine, sine = (cosine.reshape(reach), sine.reshape(reach))
    cos_wide = jnp.concatenate([cosine] * 4, axis=1)
    sin_wide = jnp.concatenate([-sine, sine] * 2, axis=1)
    col = jnp.broadcast_to(segments.reshape(rows * seq, 1), (rows * seq, LANES))
    row = segments.reshape(rows, 1, seq)
    return (cos_wide, sin_wide, col, row)


def attend_forward(qkv, tables, bounds, block):
    cos_wide, sin_wide, col, row = tables
    rows, _, seq = row.shape
    width = qkv.shape[1] // 3
    pairs = width // LANES
    tile = lambda shift: pl.BlockSpec((seq, LANES), lambda r, h, *_: (r, h + shift))
    whole = pl.BlockSpec((seq, LANES), lambda r, h, *_: (r, 0))
    lines = pl.BlockSpec((1, 1, seq), lambda r, h, *_: (r, 0, 0))
    low = jax.ShapeDtypeStruct((rows * seq, width), jnp.bfloat16)
    return pl.pallas_call(
        functools.partial(forward_kernel, block=block),
        grid_spec=pltpu.PrefetchScalarGridSpec(
            num_scalar_prefetch=2,
            grid=(rows, pairs),
            in_specs=[tile(0), tile(pairs), tile(2 * pairs), whole, whole, whole, lines],
            out_specs=[
                tile(0), tile(0), tile(0), tile(0),
                pl.BlockSpec((1, 2, seq), lambda r, h, *_: (r * pairs + h, 0, 0)),
            ],
        ),
        out_shape=[low, low, low, low, jax.ShapeDtypeStruct((rows * pairs, 2, seq), jnp.float32)],
        name="attend_forward",
    )(*bounds, qkv, qkv, qkv, cos_wide, sin_wide, col, row)


def attend_backward(query, key, value, grad_mixed, lse, tables, bounds, block):
    cos_wide, sin_wide, col, row = tables
    rows, _, seq = row.shape
    width = query.shape[1]
    pairs = width // LANES
    tile = pl.BlockSpec((seq, LANES), lambda r, h, *_: (r, h))
    whole = pl.BlockSpec((seq, LANES), lambda r, h, *_: (r, 0))
    lines = pl.BlockSpec((1, 1, seq), lambda r, h, *_: (r, 0, 0))
    low = jax.ShapeDtypeStruct((rows * seq, width), jnp.bfloat16)
    acc = pltpu.VMEM((seq, LANES), jnp.float32)
    return pl.pallas_call(
        functools.partial(backward_kernel, block=block),
        grid_spec=pltpu.PrefetchScalarGridSpec(
            num_scalar_prefetch=2,
            grid=(rows, pairs),
            in_specs=[
                tile, tile, tile, tile,
                pl.BlockSpec((1, 2, seq), lambda r, h, *_: (r * pairs + h, 0, 0)),
                whole, whole, whole, lines,
            ],
            out_specs=[
                tile, tile, tile,
                pl.BlockSpec((1, 3, LANES), lambda r, h, *_: (r, 0, h)),
            ],
            scratch_shapes=[acc, acc, acc],
        ),
        out_shape=[low, low, low, jax.ShapeDtypeStruct((rows, 3, width), jnp.float32)],
        name="attend_backward",
    )(*bounds, query, key, value, grad_mixed, lse, cos_wide, sin_wide, col, row)


def norm_mod(values, gain, bias, shift):
    center = jnp.mean(values, axis=-1, keepdims=True)
    centered = values - center
    spread = jnp.mean(centered * centered, axis=-1, keepdims=True)
    return (centered * lax.rsqrt(spread + 1e-05) * gain + bias) * (1.0 + shift)


def gelu_exact(values):
    return jax.nn.gelu(values, approximate=False)


def product(left, right):
    return jnp.dot(left, right, preferred_element_type=jnp.float32)


def product_left(left, right):
    return lax.dot_general(
        left, right, (((0,), (0,)), ((), ())), preferred_element_type=jnp.float32
    )


def product_right(left, right):
    return lax.dot_general(
        left, right, (((1,), (1,)), ((), ())), preferred_element_type=jnp.float32
    )


def gather(part):
    return lax.all_gather(part, "fsdp", axis=0, tiled=True)


def pack(parts, rows):
    flat = jnp.concatenate(parts, axis=-1)
    room = rows * LANES * -(-flat.shape[-1] // (rows * LANES))
    flat = jnp.pad(flat, ((0, 0), (0, room - flat.shape[-1])))
    return flat.reshape(flat.shape[0] * rows, room // rows)


def unpack(packed, sizes, shards):
    flat = packed.reshape(shards, -1)
    parts, at = ([], 0)
    for size in sizes:
        parts.append(flat[:, at : at + size].reshape(-1))
        at += size
    return parts


def reduce_weight(partial):
    share = lax.psum_scatter(
        partial.astype(jnp.bfloat16), "fsdp", scatter_dimension=0, tiled=True
    )
    if lax.axis_size("dp") == 2:
        other = lax.ppermute(share, "dp", [(0, 1), (1, 0)])
        return share.astype(jnp.float32) + other.astype(jnp.float32)
    return lax.psum(share.astype(jnp.float32), "dp")


def per_device(
    tokens,
    time_embed,
    segments,
    cotangent,
    attn_norm_gain,
    attn_norm_bias,
    time_weight,
    qkv_weight,
    qkv_bias,
    out_weight,
    out_bias,
    mlp_norm_gain,
    mlp_norm_bias,
    up_weight,
    up_bias,
    down_weight,
    down_bias,
):
    width = tokens.shape[1]
    rows, seq = segments.shape
    shards = lax.axis_size("fsdp")
    total_tokens = tokens.shape[0] * lax.axis_size("dp") * shards
    factor = 1.0 / math.sqrt(total_tokens)
    block = min(BLOCK, seq)
    time_rows, time_cols = time_weight.shape

    small = (
        attn_norm_gain, attn_norm_bias, qkv_bias, out_bias,
        mlp_norm_gain, mlp_norm_bias, up_bias, down_bias,
    )
    sizes = [part.shape[0] for part in small]
    first = jnp.concatenate([time_weight, pack([p[None] for p in small], time_rows)], axis=1)
    first = gather(first)
    w_qkv = gather(qkv_weight)
    w_out = gather(out_weight)
    w_up = gather(up_weight)
    w_down = gather(down_weight)
    w_time = first[:, :time_cols]
    gain_one, bias_one, b_qkv, b_out, gain_two, bias_two, b_up, b_down = (
        part.astype(jnp.float32) for part in unpack(first[:, time_cols:], sizes, shards)
    )

    tables = attention_tables(segments)
    bounds = block_bounds(segments, block)
    modulation = product(time_embed, w_time)
    tokens_float = tokens.astype(jnp.float32)
    norm_one, pull_one = jax.vjp(
        norm_mod, tokens_float, gain_one, bias_one, modulation[:, :width]
    )
    normed_one = norm_one.astype(jnp.bfloat16)
    qkv = product(normed_one, w_qkv) + b_qkv
    mixed, query, key, value, lse = attend_forward(qkv, tables, bounds, block)
    hidden = tokens_float + product(mixed, w_out) + b_out
    norm_two, pull_two = jax.vjp(norm_mod, hidden, gain_two, bias_two, modulation[:, width:])
    normed_two = norm_two.astype(jnp.bfloat16)
    up = product(normed_two, w_up) + b_up
    active_float, pull_gelu = jax.vjp(gelu_exact, up)
    active = active_float.astype(jnp.bfloat16)
    grad_out = cotangent.astype(jnp.float32)
    down_share = reduce_weight(product_left(active, cotangent))
    output = hidden + product(active, w_down) + b_down
    layer_out = output.astype(jnp.bfloat16)

    down_bias_sum = jnp.sum(grad_out, axis=0)
    grad_active = product_right(cotangent, w_down)
    (grad_up,) = pull_gelu(grad_active)
    up_bias_sum = jnp.sum(grad_up, axis=0)
    grad_up_low = grad_up.astype(jnp.bfloat16)
    up_share = reduce_weight(product_left(normed_two, grad_up_low))
    grad_normed_two = product_right(grad_up_low, w_up)
    grad_hidden_part, gain_two_sum, bias_two_sum, grad_shift_two = pull_two(grad_normed_two)
    grad_hidden = grad_out + grad_hidden_part
    out_bias_sum = jnp.sum(grad_hidden, axis=0)
    grad_hidden_low = grad_hidden.astype(jnp.bfloat16)
    out_share = reduce_weight(product_left(mixed, grad_hidden_low))
    grad_mixed = product_right(grad_hidden_low, w_out).astype(jnp.bfloat16)
    grad_query, grad_key, grad_value, qkv_bias_rows = attend_backward(
        query, key, value, grad_mixed, lse, tables, bounds, block
    )
    qkv_bias_sum = jnp.sum(qkv_bias_rows, axis=0).reshape(-1)
    grad_qkv_low = jnp.concatenate([grad_query, grad_key, grad_value], axis=1)
    qkv_share = reduce_weight(product_left(normed_one, grad_qkv_low))
    grad_normed_one = product_right(grad_qkv_low, w_qkv)
    grad_tokens_part, gain_one_sum, bias_one_sum, grad_shift_one = pull_one(grad_normed_one)
    tokens_grad = (grad_hidden + grad_tokens_part).astype(jnp.bfloat16)
    grad_shift = jnp.concatenate([grad_shift_one, grad_shift_two], axis=1).astype(jnp.bfloat16)
    time_sum = product_left(time_embed, grad_shift)
    small_sums = (
        gain_one_sum, bias_one_sum, qkv_bias_sum, out_bias_sum,
        gain_two_sum, bias_two_sum, up_bias_sum, down_bias_sum,
    )
    packed = pack([part.reshape(shards, -1) for part in small_sums], time_rows)
    last_share = reduce_weight(jnp.concatenate([time_sum, packed], axis=1))
    smalls = unpack(last_share[:, time_cols:] * factor, sizes, 1)
    return (
        layer_out,
        tokens_grad,
        smalls[0],
        smalls[1],
        last_share[:, :time_cols] * factor,
        qkv_share * factor,
        smalls[2],
        out_share * factor,
        smalls[3],
        smalls[4],
        smalls[5],
        up_share * factor,
        smalls[6],
        down_share * factor,
        smalls[7],
    )


def solution(mesh):
    placed = (
        P(("dp", "fsdp"), None),
        P(("dp", "fsdp"), None),
        P(("dp", "fsdp"), None),
        P(("dp", "fsdp"), None),
        P("fsdp"),
        P("fsdp"),
        P("fsdp", None),
        P("fsdp", None),
        P("fsdp"),
        P("fsdp", None),
        P("fsdp"),
        P("fsdp"),
        P("fsdp"),
        P("fsdp", None),
        P("fsdp"),
        P("fsdp", None),
        P("fsdp"),
    )
    return jax.shard_map(
        per_device,
        mesh=mesh,
        in_specs=placed,
        out_specs=(
            P(("dp", "fsdp"), None),
            P(("dp", "fsdp"), None),
            P("fsdp"),
            P("fsdp"),
            P("fsdp", None),
            P("fsdp", None),
            P("fsdp"),
            P("fsdp", None),
            P("fsdp"),
            P("fsdp"),
            P("fsdp"),
            P("fsdp", None),
            P("fsdp"),
            P("fsdp", None),
            P("fsdp"),
        ),
        check_vma=False,
    )
```

time: 1580 us -> 929 us (0.59)
  matrix products: 569 us -> 190 us
  blocking collectives: 147 us -> 0 us
  local copies, waits for them, and re-layouts: 170 us -> 26 us
  Pallas kernels: 0 us -> 76.6 us
  other arithmetic: 121 us -> 56.6 us
    dot_general x14 -> x0, matrix products: 378 us -> none  [the longest x2 115 us: one_block(): jnp.einsum('hqk,qhd->khd', grad_raw, query_block, preferred_element_type=...]
    all_gather x5, waiting for transfers between devices: 10.4 us -> 195 us  [gather(): return lax.all_gather(part, 'fsdp', axis=0, tiled=True)]
    reduce_scatter x4 -> x5, waiting for transfers between devices: 476 us -> 345 us  [reduce_weight(): lax.psum_scatter(partial.astype(jnp.bfloat16), 'fsdp', scatter_dimension=...]
    unnamed x2 -> x0, blocking collectives: 124 us -> none
    dynamic_update_slice x4 -> x0, local copies, waits for them, and re-layouts: 86.5 us -> none  [attend_backward(): lax.scan(one_block, (zeros_kv, zeros_kv), (query_blocks, seg_blocks, grad...]
    pallas_call x0 -> x2, Pallas kernels: none -> 76.6 us  [the longest x1 40.3 us: attend_backward(): pl.pallas_call(functools.partial(backward_kernel, block=block), grid_spec...]
    psum x1 -> x0, waiting for transfers between devices: 48.5 us -> none  [reduce_attn(): lax.psum(shares[2].astype(jnp.bfloat16), 'dp').astype(jnp.float32)]
    reduce_sum x3 -> x2, other arithmetic: 37.5 us -> 6.5 us  [the longest x1 6.28 us: per_device(): out_bias_sum = jnp.sum(grad_hidden, axis=0)]
  transfers between devices with their start and end apart: 11 -> 15, of which waited for: 5 -> 10; matrix products, arithmetic and copies ran while one was open for 19% -> 15% of each run, Pallas kernels for 0% -> 4%
where the time goes in v1:
time: 929 us; the launch traced here: 924 us
  waiting for transfers between devices  551 us (59%)
  matrix products  190 us (20%)
  Pallas kernels  76.6 us (8%)
  other arithmetic  56.6 us (6%)
  local copies, waits for them, and re-layouts  26 us (3%)
  between operations  15.1 us (2%)
    reduce_scatter x5, waiting for transfers between devices, reduce_weight(): lax.psum_scatter(partial.astype(jnp.bfloat16), 'fsdp', scatter_dimension=...  345 us
    all_gather x5, waiting for transfers between devices, gather(): return lax.all_gather(part, 'fsdp', axis=0, tiled=True)  195 us
    dot_general x4, matrix products, product_right(): lax.dot_general(left, right, (((1,), (1,)), ((), ())), preferred_element_...  91.5 us
    dot_general x5, matrix products, product(): return jnp.dot(left, right, preferred_element_type=jnp.float32)  51 us
    dot_general x5, matrix products, product_left(): lax.dot_general(left, right, (((0,), (0,)), ((), ())), preferred_element_...  47.6 us
    pallas_call x1, Pallas kernels, attend_backward(): pl.pallas_call(functools.partial(backward_kernel, block=block), grid_spec...  40.3 us
    pallas_call x1, Pallas kernels, attend_forward(): pl.pallas_call(functools.partial(forward_kernel, block=block), grid_spec=...  36.4 us
  transfers between devices with their start and end apart: 15, of which 10 were waited for; matrix products, arithmetic and copies ran while one was open for 15% of the time, Pallas kernels for 4%

profile of v1, /device:TPU:0, one launch (start us, length us, event | category | flops | bytes accessed | tf_op | source)
XLA Modules:
  0.0 923.5 jit_solution(10082780518370741374)
XLA Ops:
  7.3 0.8 broadcast_in_dim.63
  8.7 0.8 concatenate.34
  9.6 1.5 pad_maximum_fusion.3
  11.1 0.7 all-gather.8.cloned.1.call-update
  11.9 0.7 all-gather.10.cloned.1.call-update
  13.8 2.0 reduce.2
  16.9 1.3 reduce.12
  18.5 0.8 slice_compare_fusion
  20.5 1.9 fusion.39
  22.4 1.8 pad_maximum_fusion.1
  25.1 0.7 fusion.18
  26.4 25.8 %all-gather.6.cloned.1.call-done = bf16[256,2176]{1,0:T(8,128)(2,1)} async-done(((bf16[16,2176]{1,0:T(8,128)(2,1)}), bf16[256,2176]{1,0:T(8,128)(2,1)}) %all-gather.6.cloned.1.call-update) | async-done | bytes 1114128 | tf_op jit(solution)/shard_map/all_gather | solution.py:279
  52.2 0.8 slice.114
  54.1 2.5 convolution_bitcast_fusion
  56.7 3.3 copy-done.3
  60.0 2.6 fusion.15
  62.5 52.4 %all-gather.8.cloned.1.call-done = bf16[1024,3072]{1,0:T(8,128)(2,1)} async-done(((bf16[64,3072]{1,0:T(8,128)(2,1)}), bf16[1024,3072]{1,0:T(8,128)(2,1)}) %all-gather.8.cloned.1.call-update) | async-done | bytes 6291472 | tf_op jit(solution)/shard_map/all_gather | solution.py:279
  114.9 12.0 %broadcast_add_fusion.q_ref.k_ref.v_ref = f32[1024,3072]{1,0:T(8,128)} fusion(f32[3072]{0:T(1024)S(1)} %reshape.531, bf16[1024,1024]{1,0:T(8,128)(2,1)} %fusion.15, bf16[1024,3072]{1,0:T(8,128)(2,1)} %all-gather.8.cloned.1.call-done), kind=kOutput, calls=%fused_computation.21 | convolution fusion | flops 6445596672 | bytes 20983808 | tf_op jit(solution)/shard_map/dot_general | solution.py:263
  126.9 1.0 broadcast_in_dim.71.col_ref
  127.9 36.4 %attend_forward.1 = (bf16[1024,1024]{1,0:T(8,128)(2,1)}, bf16[1024,1024]{1,0:T(8,128)(2,1)}, bf16[1024,1024]{1,0:T(8,128)(2,1)}, bf16[1024,1024]{1,0:T(8,128)(2,1)}, f32[8,2,1024]{2,1,0:T(2,128)}) custom-call(s32[1,4]{1,0:T(1,128)} %bitcast.86, s32[1,4]{1,0:T(1,128)} %bitcast_subtract_fusion.count_ref, f32[1024,3072]{1,0:T(8,128)} %broadcast_add_fusion.q_ref.k_ref.v_ref, ...), custom_call_target="tpu_custom_call" | custom-call | tf_op jit(solution)/shard_map/attend_forward/pallas_call | solution.py:204
  164.4 5.1 fusion.54
  170.1 1.3 copy-done.5
  171.5 2.3 multiply_convert_fusion.2
  173.8 58.5 %all-gather.12.cloned.1.call-done = bf16[1024,4096]{1,0:T(8,128)(2,1)} async-done(((bf16[64,4096]{1,0:T(8,128)(2,1)}), bf16[1024,4096]{1,0:T(8,128)(2,1)}) %all-gather.12.cloned.1.call-update) | async-done | bytes 8388624 | tf_op jit(solution)/shard_map/all_gather | solution.py:279
  232.4 16.2 %fusion.55 = f32[1024,4096]{1,0:T(8,128)} fusion(bf16[1024,1024]{1,0:T(8,128)(2,1)} %multiply_convert_fusion.2, bf16[1024,4096]{1,0:T(8,128)(2,1)} %all-gather.12.cloned.1.call-done), kind=kOutput, calls=%fused_computation.131 | convolution fusion | flops 8589934592 | bytes 27262976 | tf_op jit(solution)/shard_map/dot_general | solution.py:263
  248.5 58.7 %all-gather.14.cloned.1.call-done = bf16[4096,1024]{1,0:T(8,128)(2,1)} async-done(((bf16[256,1024]{1,0:T(8,128)(2,1)}), bf16[4096,1024]{1,0:T(8,128)(2,1)}) %all-gather.14.cloned.1.call-update) | async-done | bytes 8388624 | tf_op jit(solution)/shard_map/all_gather | solution.py:279
  307.3 51.4 %fusion.48 = (bf16[4096]{0:T(1024)(128)(2,1)S(1)}, bf16[1024,4096]{1,0:T(8,128)(2,1)}, f32[1024,4096]{1,0:T(8,128)}) fusion(f32[1024,4096]{1,0:T(8,128)} %fusion.55, f32[4096]{0:T(1024)S(1)} %bitcast.79, bf16[1024,1024]{1,0:T(8,128)(2,1)S(1)} %copy-done.7, bf16[4096,1024]{1,0:T(8,128)(2,1)} %all-gather.14.cloned.1.call-done), kind=kOutput, calls=%fused_computation.127 | convolution fusion | flops 8900308992 | bytes 52453376 | tf_op jit(solution)/shard_map/dot_general | solution.py:273
  358.7 18.1 %multiply_reduce_fusion = (bf16[1024]{0:T(1024)(128)(2,1)S(1)}, f32[1024]{0:T(1024)S(1)}, bf16[1024]{0:T(1024)(128)(2,1)S(1)}, f32[1024,1024]{1,0:T(8,128)}, bf16[1024,1024]{1,0:T(8,128)(2,1)}) fusion(f32[1024,1024]{1,0:T(8,128)} %copy-done.5, f32[1024]{0:T(1024)S(1)} %copy-done.26, f32[1024]{0:T(1024)S(1)} %copy-done.18, f32[1024]{0:T(1024)S(1)} %copy-done.24, ...), kind=kOutput, calls=%fused_computation.48 | convolution fusion | flops 8604611584 | bytes 31481856 | tf_op jit(solution)/shard_map/dot_general | solution.py:273
  376.8 5.6 fusion.51
  382.5 6.6 convolution_convert_fusion.4.grad_ref
  389.2 40.3 %attend_backward.1 = (bf16[1024,1024]{1,0:T(8,128)(2,1)}, bf16[1024,1024]{1,0:T(8,128)(2,1)}, bf16[1024,1024]{1,0:T(8,128)(2,1)}, f32[1,3,1024]{2,1,0:T(4,128)}) custom-call(s32[1,4]{1,0:T(1,128)} %bitcast.87, s32[1,4]{1,0:T(1,128)} %bitcast_subtract_fusion.count_ref, bf16[1024,1024]{1,0:T(8,128)(2,1)} %get-tuple-element.25.query_ref, ...), custom_call_target="tpu_custom_call" | custom-call | tf_op jit(solution)/shard_map/attend_backward/pallas_call | solution.py:230
  429.4 0.7 convert.59
  430.3 1.9 constant_dynamic-update-slice_fusion.2
  433.3 0.9 copy-done.2
  434.3 15.5 %fusion.47 = (bf16[1024]{0:T(1024)(128)(2,1)S(1)}, f32[1024]{0:T(1024)S(1)}, f32[1024,1024]{1,0:T(8,128)}, bf16[1024,1024]{1,0:T(8,128)(2,1)}) fusion(f32[1024]{0:T(1024)S(1)} %copy-done.20, f32[1024]{0:T(1024)S(1)} %copy-done.15, bf16[1024,1024]{1,0:T(8,128)(2,1)S(1)} %copy-done.2, f32[1024,2048]{1,0:T(8,128)} %copy-done.3, f32[1024]{0:T(1024)S(1)} %copy-done.35, ...), kind=kOutput, calls=%fused_computation.126 | convolution fusion | flops 6456080384 | bytes 25188352 | tf_op jit(solution)/shard_map/dot_general | solution.py:273
  449.8 3.8 fusion.17
  453.7 6.3 fusion.46
  460.4 3.6 fusion.33
  464.0 1.1 pad_maximum_fusion
  465.0 2.4 copy.73
  467.5 6.8 convolution_convert_fusion.3
  474.4 11.2 %convolution_convert_fusion.2 = bf16[1024,3072]{1,0:T(8,128)(2,1)} fusion(bf16[1024,1024]{1,0:T(8,128)(2,1)} %fusion.15, bf16[1024,3072]{1,0:T(8,128)(2,1)} %copy-done.12), kind=kOutput, calls=%fused_computation.29 | convolution fusion | flops 6445596672 | bytes 14680064 | tf_op jit(solution)/shard_map/dot_general | solution.py:267
  485.7 12.6 %multiply_convert_fusion = bf16[1024,4096]{1,0:T(8,128)(2,1)S(1)} fusion(f32[1024,4096]{1,0:T(8,128)} %get-tuple-element.74, f32[1024,4096]{1,0:T(8,128)} %fusion.55, f32[4096]{0:T(1024)S(1)} %bitcast.80), kind=kLoop, calls=%fused_computation.3 | loop fusion | flops 16777216 | bytes 41959424 | tf_op jit(solution)/shard_map/convert_element_type | solution.py:366
  498.3 3.3 copy-done.6
  501.6 11.3 %convolution_convert_fusion = bf16[4096,1024]{1,0:T(8,128)(2,1)} fusion(bf16[1024,4096]{1,0:T(8,128)(2,1)S(1)} %multiply_convert_fusion, bf16[1024,1024]{1,0:T(8,128)(2,1)S(1)} %copy-done.8), kind=kOutput, calls=%fused_computation.17 | convolution fusion | flops 8594128896 | bytes 18874368 | tf_op jit(solution)/shard_map/dot_general | solution.py:267
  512.9 1.5 copy-done.9
  514.5 14.8 %convolution_convert_fusion.1 = bf16[1024,4096]{1,0:T(8,128)(2,1)} fusion(bf16[1024,1024]{1,0:T(8,128)(2,1)S(1)} %copy-done.9, bf16[1024,4096]{1,0:T(8,128)(2,1)} %get-tuple-element.73), kind=kOutput, calls=%fused_computation.18 | convolution fusion | flops 8594128896 | bytes 18874368 | tf_op jit(solution)/shard_map/dot_general | solution.py:267
  529.3 0.7 copy-done.31
  530.0 4.2 reduce-scatter.16.cloned.1.call-done
  534.2 1.4 collective-permute-start
  535.7 15.2 %add_convert_fusion.1 = bf16[1024,1024]{1,0:T(8,128)(2,1)} fusion(f32[1024,1024]{1,0:T(8,128)} %copy-done.5, f32[1024]{0:T(1024)S(1)} %reshape.536, bf16[1024,4096]{1,0:T(8,128)(2,1)} %copy-done.6, bf16[4096,1024]{1,0:T(8,128)(2,1)} %all-gather.14.cloned.1.call-done), kind=kOutput, calls=%fused_computation.56 | convolution fusion | flops 8593080320 | bytes 23072768 | tf_op jit(solution)/shard_map/dot_general | solution.py:263
  552.8 46.1 %reduce-scatter.10.cloned.1.call-done = bf16[64,1024]{1,0:T(8,128)(2,1)} async-done(((bf16[1024,1024]{1,0:T(8,128)(2,1)}), bf16[64,1024]{1,0:T(8,128)(2,1)}) %reduce-scatter.10.cloned.1.call-update) | async-done | bytes 131088 | tf_op jit(solution)/shard_map/reduce_scatter | solution.py:299
  598.9 1.5 collective-permute-start.2
  600.4 86.5 %reduce-scatter.8.cloned.1.call-done = bf16[64,3072]{1,0:T(8,128)(2,1)} async-done(((bf16[1024,3072]{1,0:T(8,128)(2,1)}), bf16[64,3072]{1,0:T(8,128)(2,1)}) %reduce-scatter.8.cloned.1.call-update) | async-done | bytes 393232 | tf_op jit(solution)/shard_map/reduce_scatter | solution.py:299
  686.9 1.5 collective-permute-start.1
  689.0 1.6 add_multiply_fusion.3
  690.6 102.9 %reduce-scatter.14.cloned.1.call-done = bf16[256,1024]{1,0:T(8,128)(2,1)} async-done(((bf16[4096,1024]{1,0:T(8,128)(2,1)}), bf16[256,1024]{1,0:T(8,128)(2,1)}) %reduce-scatter.14.cloned.1.call-update) | async-done | bytes 524304 | tf_op jit(solution)/shard_map/reduce_scatter | solution.py:299
  793.6 1.5 collective-permute-start.4
  795.0 105.5 %reduce-scatter.12.cloned.1.call-done = bf16[64,4096]{1,0:T(8,128)(2,1)} async-done(((bf16[1024,4096]{1,0:T(8,128)(2,1)}), bf16[64,4096]{1,0:T(8,128)(2,1)}) %reduce-scatter.12.cloned.1.call-update) | async-done | bytes 524304 | tf_op jit(solution)/shard_map/reduce_scatter | solution.py:299
  900.6 1.5 collective-permute-start.3
  902.1 2.0 add_multiply_fusion.2
  904.0 2.2 add_multiply_fusion
  906.3 7.8 collective-permute-done.3
  914.1 2.2 add_multiply_fusion.1
  (158 shorter events, 12.3 us)
Async XLA Ops:
  7.2 47.0 %copy-start = (bf16[1024,256]{1,0:T(8,128)(2,1)S(1)}, bf16[1024,256]{1,0:T(8,128)(2,1)}, u32[]{:S(2)}) copy-start(bf16[1024,256]{1,0:T(8,128)(2,1)} %param.18) | copy-start | bytes 1572868
  7.2 17.0 %copy-start.1 = (bf16[1024,1024]{1,0:T(8,128)(2,1)S(1)}, bf16[1024,1024]{1,0:T(8,128)(2,1)}, u32[]{:S(2)}) copy-start(bf16[1024,1024]{1,0:T(8,128)(2,1)} %param.17) | copy-start | bytes 6291460
  7.2 45.0 %all-gather.6.cloned.1.call-start = ((), (), s32[]{:S(2)}) async-start(), calls=%async_computation.5 | async-start | bytes 1183744 | tf_op jit(solution)/shard_map/all_gather | solution.py:279
  11.1 103.8 %all-gather.8.cloned.1.call-start = ((), (), s32[]{:S(2)}) async-start(), calls=%async_computation.6 | async-start | bytes 6684672 | tf_op jit(solution)/shard_map/all_gather | solution.py:279
  11.8 152.5 %all-gather.10.cloned.1.call-start = ((), (), s32[]{:S(2)}) async-start(), calls=%async_computation.7 | async-start | bytes 2228224 | tf_op jit(solution)/shard_map/all_gather | solution.py:279
  12.6 219.8 %all-gather.12.cloned.1.call-start = ((), (), s32[]{:S(2)}) async-start(), calls=%async_computation.8 | async-start | bytes 8912896 | tf_op jit(solution)/shard_map/all_gather | solution.py:279
  13.1 294.1 %all-gather.14.cloned.1.call-start = ((), (), s32[]{:S(2)}) async-start(), calls=%async_computation.9 | async-start | bytes 8912896 | tf_op jit(solution)/shard_map/all_gather | solution.py:279
  13.7 520.5 %reduce-scatter.16.cloned.1.call-start = ((), (), s32[]{:S(2)}) async-start(), calls=%async_computation.14 | async-start | bytes 1183744 | tf_op jit(solution)/shard_map/reduce_scatter | solution.py:299
  20.4 5.4 copy-start.37
  25.1 31.5 %copy-start.14 = (f32[1024]{0:T(1024)}, f32[1024]{0:T(1024)S(1)}, u32[]{:S(2)}) copy-start(f32[1024]{0:T(1024)S(1)} %broadcast_multiply_fusion.1) | copy-start | bytes 12292
  25.8 0.6 copy-start.27
  26.4 30.3 %copy-start.21 = (f32[1024]{0:T(1024)}, f32[1024]{0:T(1024)S(1)}, u32[]{:S(2)}) copy-start(f32[1024]{0:T(1024)S(1)} %fusion.42) | copy-start | bytes 12292
  53.8 116.3 %copy-start.23 = (f32[1024]{0:T(1024)}, f32[1024]{0:T(1024)S(1)}, u32[]{:S(2)}) copy-start(f32[1024]{0:T(1024)S(1)} %reshape.533) | copy-start | bytes 12292
  53.9 2.7 copy-start.19
  54.0 116.1 %copy-start.32 = (f32[1024]{0:T(1024)}, f32[1024]{0:T(1024)S(1)}, u32[]{:S(2)}) copy-start(f32[1024]{0:T(1024)S(1)} %reshape.534) | copy-start | bytes 12292
  54.1 2.6 copy-start.34
  56.7 3.3 copy-start.3
  62.5 64.4 %copy-start.13 = (s32[1,1024]{1,0:T(1,128)S(1)}, s32[1,1024]{1,0:T(1,128)}, u32[]{:S(2)}) copy-start(s32[1,1024]{1,0:T(1,128)} %param.19) | copy-start | bytes 12292
  164.4 7.1 slice-start
  164.4 7.1 slice-start.1
  169.5 2.0 copy-start.5
  169.5 2.0 copy-start.17
  170.1 3.7 copy-start.29
  171.5 2.3 copy-start.25
  173.8 133.5 %copy-start.7 = (bf16[1024,1024]{1,0:T(8,128)(2,1)S(1)}, bf16[1024,1024]{1,0:T(8,128)(2,1)}, u32[]{:S(2)}) copy-start(bf16[1024,1024]{1,0:T(8,128)(2,1)} %param.20) | copy-start | bytes 6291460
  307.3 51.4 %copy-start.4 = (f32[1024,2048]{1,0:T(8,128)S(1)}, f32[1024,2048]{1,0:T(8,128)}, u32[]{:S(2)}) copy-start(f32[1024,2048]{1,0:T(8,128)} %copy-done.3) | copy-start | bytes 25165828
  307.3 51.4 %copy-start.18 = (f32[1024]{0:T(1024)S(1)}, f32[1024]{0:T(1024)}, u32[]{:S(2)}) copy-start(f32[1024]{0:T(1024)} %copy-done.17) | copy-start | bytes 12292
  307.3 51.4 %copy-start.24 = (f32[1024]{0:T(1024)S(1)}, f32[1024]{0:T(1024)}, u32[]{:S(2)}) copy-start(f32[1024]{0:T(1024)} %copy-done.23) | copy-start | bytes 12292
  307.3 51.4 %copy-start.26 = (f32[1024]{0:T(1024)S(1)}, f32[1024]{0:T(1024)}, u32[]{:S(2)}) copy-start(f32[1024]{0:T(1024)} %copy-done.25) | copy-start | bytes 12292
  307.3 51.4 %copy-start.33 = (f32[1024]{0:T(1024)S(1)}, f32[1024]{0:T(1024)}, u32[]{:S(2)}) copy-start(f32[1024]{0:T(1024)} %copy-done.32) | copy-start | bytes 12292
  358.7 18.1 %copy-start.30 = (f32[1024]{0:T(1024)S(1)}, f32[1024]{0:T(1024)}, u32[]{:S(2)}) copy-start(f32[1024]{0:T(1024)} %copy-done.29) | copy-start | bytes 12292
  430.3 2.2 copy-start.11
  430.3 2.9 copy-start.10
  432.5 1.7 copy-start.2
  432.5 1.7 copy-start.15
  432.5 1.7 copy-start.20
  432.5 1.7 copy-start.22
  432.5 1.7 copy-start.35
  434.2 15.5 %copy-start.12 = (bf16[1024,3072]{1,0:T(8,128)(2,1)}, bf16[1024,3072]{1,0:T(8,128)(2,1)S(1)}, u32[]{:S(2)}) copy-start(bf16[1024,3072]{1,0:T(8,128)(2,1)S(1)} %constant_dynamic-update-slice_fusion) | copy-start | bytes 18874372
  434.2 15.5 %copy-start.28 = (f32[1024]{0:T(1024)S(1)}, f32[1024]{0:T(1024)}, u32[]{:S(2)}) copy-start(f32[1024]{0:T(1024)} %copy-done.27) | copy-start | bytes 12292
  453.7 6.4 copy-start.36
  463.9 3.6 copy-start.8
  467.5 131.4 %reduce-scatter.10.cloned.1.call-start = ((), (), s32[]{:S(2)}) async-start(), calls=%async_computation.11 | async-start | bytes 2228224 | tf_op jit(solution)/shard_map/reduce_scatter | solution.py:299
  474.3 212.6 %reduce-scatter.8.cloned.1.call-start = ((), (), s32[]{:S(2)}) async-start(), calls=%async_computation.10 | async-start | bytes 6684672 | tf_op jit(solution)/shard_map/reduce_scatter | solution.py:299
  485.6 308.0 %reduce-scatter.14.cloned.1.call-start = ((), (), s32[]{:S(2)}) async-start(), calls=%async_computation.13 | async-start | bytes 8912896 | tf_op jit(solution)/shard_map/reduce_scatter | solution.py:299
  498.2 3.3 copy-start.6
  512.9 1.6 copy-start.9
  512.9 387.7 %reduce-scatter.12.cloned.1.call-start = ((), (), s32[]{:S(2)}) async-start(), calls=%async_computation.12 | async-start | bytes 8912896 | tf_op jit(solution)/shard_map/reduce_scatter | solution.py:299
  529.3 0.7 copy-start.31
  534.2 16.7 %copy-start.16 = (bf16[16,2176]{1,0:T(8,128)(2,1)S(1)}, bf16[16,2176]{1,0:T(8,128)(2,1)}, u32[]{:S(2)}) copy-start(bf16[16,2176]{1,0:T(8,128)(2,1)} %reduce-scatter.16.cloned.1.call-done) | copy-start | bytes 208900
  534.2 16.7 %collective-permute-start = (bf16[16,2176]{1,0:T(8,128)(2,1)}, bf16[16,2176]{1,0:T(8,128)(2,1)S(1)}, u32[]{:S(2)}, u32[]{:S(2)}) collective-permute-start(bf16[16,2176]{1,0:T(8,128)(2,1)} %reduce-scatter.16.cloned.1.call-done), channel_id=1, source_target_pairs={{0,16},{16,0},{1,17},{17,1},{2,18},{18,2},{3,19},{19,3},{4,20},{20... | collective-permute-start | bytes 208904 | tf_op jit(solution)/shard_map/ppermute | solution.py:303
  598.9 90.1 %collective-permute-start.2 = (bf16[64,1024]{1,0:T(8,128)(2,1)}, bf16[64,1024]{1,0:T(8,128)(2,1)S(1)}, u32[]{:S(2)}, u32[]{:S(2)}) collective-permute-start(bf16[64,1024]{1,0:T(8,128)(2,1)} %reduce-scatter.10.cloned.1.call-done), channel_id=1, source_target_pairs={{0,16},{16,0},{1,17},{17,1},{2,18},{18,2},{3,19},{19,3},{4,20},{20... | collective-permute-start | bytes 393224 | tf_op jit(solution)/shard_map/ppermute | solution.py:303
  686.9 215.2 %collective-permute-start.1 = (bf16[64,3072]{1,0:T(8,128)(2,1)}, bf16[64,3072]{1,0:T(8,128)(2,1)S(1)}, u32[]{:S(2)}, u32[]{:S(2)}) collective-permute-start(bf16[64,3072]{1,0:T(8,128)(2,1)} %reduce-scatter.8.cloned.1.call-done), channel_id=1, source_target_pairs={{0,16},{16,0},{1,17},{17,1},{2,18},{18,2},{3,19},{19,3},{4,20},{20... | collective-permute-start | bytes 1179656 | tf_op jit(solution)/shard_map/ppermute | solution.py:303
  793.6 110.5 %collective-permute-start.4 = (bf16[256,1024]{1,0:T(8,128)(2,1)}, bf16[256,1024]{1,0:T(8,128)(2,1)S(1)}, u32[]{:S(2)}, u32[]{:S(2)}) collective-permute-start(bf16[256,1024]{1,0:T(8,128)(2,1)} %reduce-scatter.14.cloned.1.call-done), channel_id=1, source_target_pairs={{0,16},{16,0},{1,17},{17,1},{2,18},{18,2},{3,19},{19,3},{4,20},{20... | collective-permute-start | bytes 1572872 | tf_op jit(solution)/shard_map/ppermute | solution.py:303
  900.6 13.5 %collective-permute-start.3 = (bf16[64,4096]{1,0:T(8,128)(2,1)}, bf16[64,4096]{1,0:T(8,128)(2,1)S(1)}, u32[]{:S(2)}, u32[]{:S(2)}) collective-permute-start(bf16[64,4096]{1,0:T(8,128)(2,1)} %reduce-scatter.12.cloned.1.call-done), channel_id=1, source_target_pairs={{0,16},{16,0},{1,17},{17,1},{2,18},{18,2},{3,19},{19,3},{4,20},{20... | collective-permute-start | bytes 1572872 | tf_op jit(solution)/shard_map/ppermute | solution.py:303
Sparse Core Ops, SparseCore 0:
  11.2 40.9 all-gather.5
  54.5 60.3 all-gather.7
  117.1 40.1 all-gather.9
  159.3 72.9 all-gather.11
  234.4 72.8 all-gather.13
  467.6 66.6 reduce-scatter.15
  538.0 60.8 reduce-scatter.9
  602.8 84.0 reduce-scatter.7
  691.0 102.5 reduce-scatter.13
  797.5 103.0 reduce-scatter.11

commit v2 on v1

--- a/solution.py
+++ b/solution.py
@@ -8,7 +8,7 @@
 from jax.experimental.pallas import tpu as pltpu
 from jax.sharding import PartitionSpec as P
 
-HEADS = 16
+
 HEAD_DIM = 64
 LANES = 128
 BLOCK = 256
@@ -255,8 +255,14 @@
     return (centered * lax.rsqrt(spread + 1e-05) * gain + bias) * (1.0 + shift)
 
 
-def gelu_exact(values):
-    return jax.nn.gelu(values, approximate=False)
+def gelu_pair(values):
+    cdf = 0.5 * (1.0 + lax.erf(values * (1.0 / math.sqrt(2.0))))
+    density = jnp.exp(-0.5 * values * values) * (1.0 / math.sqrt(2.0 * math.pi))
+    return (values * cdf, cdf + values * density)
+
+
+def after(value, *others):
+    return lax.optimization_barrier((value, *others))[0]
 
 
 def product(left, right):
@@ -296,9 +302,7 @@
 
 
 def reduce_weight(partial):
-    share = lax.psum_scatter(
-        partial.astype(jnp.bfloat16), "fsdp", scatter_dimension=0, tiled=True
-    )
+    share = lax.psum_scatter(partial, "fsdp", scatter_dimension=0, tiled=True)
     if lax.axis_size("dp") == 2:
         other = lax.ppermute(share, "dp", [(0, 1), (1, 0)])
         return share.astype(jnp.float32) + other.astype(jnp.float32)
@@ -325,7 +329,7 @@
     down_bias,
 ):
     width = tokens.shape[1]
-    rows, seq = segments.shape
+    _, seq = segments.shape
     shards = lax.axis_size("fsdp")
     total_tokens = tokens.shape[0] * lax.axis_size("dp") * shards
     factor = 1.0 / math.sqrt(total_tokens)
@@ -337,11 +341,16 @@
         mlp_norm_gain, mlp_norm_bias, up_bias, down_bias,
     )
     sizes = [part.shape[0] for part in small]
-    first = jnp.concatenate([time_weight, pack([p[None] for p in small], time_rows)], axis=1)
-    first = gather(first)
-    w_qkv = gather(qkv_weight)
-    w_out = gather(out_weight)
-    w_up = gather(up_weight)
+    fold = qkv_weight.shape[0] // time_rows
+    packed = pack([p[None] for p in small], fold * time_rows).reshape(time_rows, -1)
+    first = jnp.concatenate([time_weight, packed], axis=1)
+    first_cols = first.shape[1]
+    one = gather(jnp.concatenate([qkv_weight, first.reshape(fold * time_rows, -1)], axis=1))
+    w_qkv = one[:, : qkv_weight.shape[1]]
+    first = one[:, qkv_weight.shape[1] :].reshape(shards * time_rows, first_cols)
+    two = gather(jnp.concatenate([out_weight, up_weight], axis=1))
+    w_out = two[:, :width]
+    w_up = two[:, width:]
     w_down = gather(down_weight)
     w_time = first[:, :time_cols]
     gain_one, bias_one, b_qkv, b_out, gain_two, bias_two, b_up, b_down = (
@@ -362,32 +371,38 @@
     norm_two, pull_two = jax.vjp(norm_mod, hidden, gain_two, bias_two, modulation[:, width:])
     normed_two = norm_two.astype(jnp.bfloat16)
     up = product(normed_two, w_up) + b_up
-    active_float, pull_gelu = jax.vjp(gelu_exact, up)
-    active = active_float.astype(jnp.bfloat16)
+    active_float, slope = gelu_pair(up)
+    active, slope = lax.optimization_barrier((active_float.astype(jnp.bfloat16), slope))
     grad_out = cotangent.astype(jnp.float32)
-    down_share = reduce_weight(product_left(active, cotangent))
+    down_sum = product_left(active, cotangent).astype(jnp.bfloat16)
+    down_share = reduce_weight(down_sum)
+    w_down = after(w_down, down_sum)
     output = hidden + product(active, w_down) + b_down
     layer_out = output.astype(jnp.bfloat16)
 
     down_bias_sum = jnp.sum(grad_out, axis=0)
     grad_active = product_right(cotangent, w_down)
-    (grad_up,) = pull_gelu(grad_active)
+    grad_up = grad_active * slope
     up_bias_sum = jnp.sum(grad_up, axis=0)
     grad_up_low = grad_up.astype(jnp.bfloat16)
-    up_share = reduce_weight(product_left(normed_two, grad_up_low))
-    grad_normed_two = product_right(grad_up_low, w_up)
+    up_sum = product_left(normed_two, grad_up_low).astype(jnp.bfloat16)
+    grad_normed_two = product_right(after(grad_up_low, up_sum), w_up)
     grad_hidden_part, gain_two_sum, bias_two_sum, grad_shift_two = pull_two(grad_normed_two)
     grad_hidden = grad_out + grad_hidden_part
     out_bias_sum = jnp.sum(grad_hidden, axis=0)
     grad_hidden_low = grad_hidden.astype(jnp.bfloat16)
-    out_share = reduce_weight(product_left(mixed, grad_hidden_low))
-    grad_mixed = product_right(grad_hidden_low, w_out).astype(jnp.bfloat16)
+    out_sum = product_left(mixed, grad_hidden_low).astype(jnp.bfloat16)
+    two_sum = jnp.concatenate([out_sum, up_sum], axis=1)
+    two_share = reduce_weight(two_sum)
+    out_share = two_share[:, :width]
+    up_share = two_share[:, width:]
+    grad_mixed = product_right(after(grad_hidden_low, two_sum), w_out).astype(jnp.bfloat16)
     grad_query, grad_key, grad_value, qkv_bias_rows = attend_backward(
         query, key, value, grad_mixed, lse, tables, bounds, block
     )
     qkv_bias_sum = jnp.sum(qkv_bias_rows, axis=0).reshape(-1)
     grad_qkv_low = jnp.concatenate([grad_query, grad_key, grad_value], axis=1)
-    qkv_share = reduce_weight(product_left(normed_one, grad_qkv_low))
+    qkv_sum = product_left(normed_one, grad_qkv_low).astype(jnp.bfloat16)
     grad_normed_one = product_right(grad_qkv_low, w_qkv)
     grad_tokens_part, gain_one_sum, bias_one_sum, grad_shift_one = pull_one(grad_normed_one)
     tokens_grad = (grad_hidden + grad_tokens_part).astype(jnp.bfloat16)
@@ -397,8 +412,13 @@
         gain_one_sum, bias_one_sum, qkv_bias_sum, out_bias_sum,
         gain_two_sum, bias_two_sum, up_bias_sum, down_bias_sum,
     )
-    packed = pack([part.reshape(shards, -1) for part in small_sums], time_rows)
-    last_share = reduce_weight(jnp.concatenate([time_sum, packed], axis=1))
+    packed = pack([part.reshape(shards, -1) for part in small_sums], fold * time_rows)
+    packed = packed.reshape(shards * time_rows, -1)
+    last_sum = jnp.concatenate([time_sum, packed], axis=1).astype(jnp.bfloat16)
+    last_sum = last_sum.reshape(qkv_sum.shape[0], -1)
+    one_share = reduce_weight(jnp.concatenate([qkv_sum, last_sum], axis=1))
+    qkv_share = one_share[:, : qkv_sum.shape[1]]
+    last_share = one_share[:, qkv_sum.shape[1] :].reshape(time_rows, first_cols)
     smalls = unpack(last_share[:, time_cols:] * factor, sizes, 1)
     return (
         layer_out,
@@ -439,6 +459,7 @@
         P("fsdp", None),
         P("fsdp"),
     )
+
     return jax.shard_map(
         per_device,
         mesh=mesh,

time: 929 us -> 769 us (0.83)
  waiting for transfers between devices: 551 us -> 433 us
  matrix products: 190 us -> 145 us
  local copies, waits for them, and re-layouts: 26 us -> 40.8 us
    all_gather x5 -> x3, waiting for transfers between devices: 195 us -> 114 us  [gather(): return lax.all_gather(part, 'fsdp', axis=0, tiled=True)]
    reduce_scatter x5 -> x3, waiting for transfers between devices: 345 us -> 301 us  [reduce_weight(): share = lax.psum_scatter(partial, 'fsdp', scatter_dimension=0, tiled=True)]
    dot_general x4, matrix products: 91.5 us -> 51.1 us  [product_right(): lax.dot_general(left, right, (((1,), (1,)), ((), ())), preferred_element_...]
    concatenate x2 -> x6, other arithmetic: 2.57 us -> 17.4 us  [the longest x1 6.83 us: per_device(): one_share = reduce_weight(jnp.concatenate([qkv_sum, last_sum], axis=1))]
    unnamed x87 -> x93, local copies, waits for them, and re-layouts: 17.7 us -> 20.1 us
  transfers between devices with their start and end apart: 15 -> 9, of which waited for: 10 -> 8; matrix products, arithmetic and copies ran while one was open for 15% -> 13% of each run, Pallas kernels for 4% -> 5%
where the time goes in v2:
time: 769 us; the launch traced here: 764 us
  waiting for transfers between devices  433 us (56%)
  matrix products  145 us (19%)
  Pallas kernels  76.5 us (10%)
  other arithmetic  48.6 us (6%)
  local copies, waits for them, and re-layouts  40.8 us (5%)
  between operations  14.9 us (2%)
    reduce_scatter x3, waiting for transfers between devices, reduce_weight(): share = lax.psum_scatter(partial, 'fsdp', scatter_dimension=0, tiled=True)  301 us
    all_gather x3, waiting for transfers between devices, gather(): return lax.all_gather(part, 'fsdp', axis=0, tiled=True)  114 us
    dot_general x5, matrix products, product(): return jnp.dot(left, right, preferred_element_type=jnp.float32)  52.7 us
    dot_general x4, matrix products, product_right(): lax.dot_general(left, right, (((1,), (1,)), ((), ())), preferred_element_...  51.1 us
    dot_general x5, matrix products, product_left(): lax.dot_general(left, right, (((0,), (0,)), ((), ())), preferred_element_...  41.5 us
    pallas_call x1, Pallas kernels, attend_backward(): pl.pallas_call(functools.partial(backward_kernel, block=block), grid_spec...  40.1 us
    pallas_call x1, Pallas kernels, attend_forward(): pl.pallas_call(functools.partial(forward_kernel, block=block), grid_spec=...  36.3 us
    unnamed x93, local copies, waits for them, and re-layouts  20.1 us
  transfers between devices with their start and end apart: 9, of which 8 were waited for; matrix products, arithmetic and copies ran while one was open for 13% of the time, Pallas kernels for 5%

profile of v2, /device:TPU:0, one launch (start us, length us, event | category | flops | bytes accessed | tf_op | source)
XLA Modules:
  0.0 764.1 jit_solution(7818647155993814962)
XLA Ops:
  7.3 0.7 broadcast_in_dim.63
  8.6 0.8 concatenate.46
  9.5 0.8 pad_maximum_fusion.7
  10.4 1.8 pad_maximum_fusion.6
  12.3 2.1 pad_maximum_fusion.3
  17.5 2.0 reduce.2
  20.5 1.9 fusion.41
  22.4 1.8 pad_maximum_fusion.4
  26.4 58.1 %all-gather.4.cloned.1.call-done = bf16[1024,3712]{1,0:T(8,128)(2,1)} async-done(((bf16[64,3712]{1,0:T(8,128)(2,1)}), bf16[1024,3712]{1,0:T(8,128)(2,1)}) %all-gather.4.cloned.1.call-update) | async-done | bytes 7602192 | tf_op jit(solution)/shard_map/all_gather | solution.py:285
  84.5 2.5 slice.146
  87.0 3.6 reshape.511
  90.6 1.0 slice.147
  92.8 2.6 convolution_bitcast_fusion
  95.4 3.3 copy-done.2
  98.7 1.4 fusion.20
  100.1 13.1 %broadcast_add_fusion.q_ref.k_ref.v_ref = f32[1024,3072]{1,0:T(8,128)} fusion(f32[3072]{0:T(1024)S(1)} %reshape.537, bf16[1024,1024]{1,0:T(8,128)(2,1)S(1)} %fusion.20, bf16[1024,3712]{1,0:T(8,128)(2,1)} %all-gather.4.cloned.1.call-done), kind=kOutput, calls=%fused_computation.18 | convolution fusion | flops 6445596672 | bytes 20983808 | tf_op jit(solution)/shard_map/dot_general | solution.py:269
  113.2 1.0 broadcast_in_dim.71.col_ref
  114.2 36.3 %attend_forward.1 = (bf16[1024,1024]{1,0:T(8,128)(2,1)}, bf16[1024,1024]{1,0:T(8,128)(2,1)}, bf16[1024,1024]{1,0:T(8,128)(2,1)}, bf16[1024,1024]{1,0:T(8,128)(2,1)}, f32[8,2,1024]{2,1,0:T(2,128)}) custom-call(s32[1,4]{1,0:T(1,128)} %bitcast.87, s32[1,4]{1,0:T(1,128)} %bitcast_subtract_fusion.count_ref, f32[1024,3072]{1,0:T(8,128)} %broadcast_add_fusion.q_ref.k_ref.v_ref, ...), custom_call_target="tpu_custom_call" | custom-call | tf_op jit(solution)/shard_map/attend_forward/pallas_call | solution.py:204
  150.6 22.9 %all-gather.6.cloned.1.call-done = bf16[1024,5120]{1,0:T(8,128)(2,1)} async-done(((bf16[64,5120]{1,0:T(8,128)(2,1)}), bf16[1024,5120]{1,0:T(8,128)(2,1)}) %all-gather.6.cloned.1.call-update) | async-done | bytes 10485776 | tf_op jit(solution)/shard_map/all_gather | solution.py:285
  173.5 4.8 fusion.57
  178.9 1.8 multiply_convert_fusion.2
  180.8 2.2 slice-done.7
  183.0 0.9 slice-done.8
  183.9 16.7 %fusion.3 = (f32[1024,4096]{1,0:T(8,128)}, bf16[1024,4096]{1,0:T(8,128)(2,1)S(1)}) fusion(f32[4096]{0:T(1024)S(1)} %bitcast.86, bf16[1024,1024]{1,0:T(8,128)(2,1)S(1)} %multiply_convert_fusion.2, bf16[1024,5120]{1,0:T(8,128)(2,1)S(1)} %bitcast.101), kind=kOutput, calls=%fused_computation.4 | convolution fusion | flops 8636071936 | bytes 35667968 | tf_op jit(solution)/shard_map/dot_general | solution.py:269
  200.6 3.3 copy-done.33
  204.0 11.3 %convolution_convert_fusion.1 = bf16[4096,1024]{1,0:T(8,128)(2,1)} fusion(bf16[1024,4096]{1,0:T(8,128)(2,1)S(1)} %get-tuple-element.30, bf16[1024,1024]{1,0:T(8,128)(2,1)S(1)} %copy-done.6), kind=kOutput, calls=%fused_computation.11 | convolution fusion | flops 8594128896 | bytes 18874368 | tf_op jit(solution)/shard_map/dot_general | solution.py:273
  215.3 33.1 %all-gather.8.cloned.1.call-done = bf16[4096,1024]{1,0:T(8,128)(2,1)} async-done(((bf16[256,1024]{1,0:T(8,128)(2,1)}), bf16[4096,1024]{1,0:T(8,128)(2,1)}) %all-gather.8.cloned.1.call-update) | async-done | bytes 8388624 | tf_op jit(solution)/shard_map/all_gather | solution.py:285
  248.4 17.3 %fusion.55 = (bf16[4096]{0:T(1024)(128)(2,1)S(1)}, bf16[1024,4096]{1,0:T(8,128)(2,1)}) fusion(f32[1024,4096]{1,0:T(8,128)} %get-tuple-element.32, bf16[4096,1024]{1,0:T(8,128)(2,1)} %all-gather.8.cloned.1.call-done, bf16[1024,1024]{1,0:T(8,128)(2,1)} %param.20), kind=kOutput, calls=%fused_computation.130 | convolution fusion | flops 8602513408 | bytes 35659776 | tf_op jit(solution)/shard_map/dot_general | solution.py:279
  265.7 14.9 %convolution_convert_fusion = bf16[1024,4096]{1,0:T(8,128)(2,1)} fusion(bf16[1024,1024]{1,0:T(8,128)(2,1)S(1)} %copy-done.10, bf16[1024,4096]{1,0:T(8,128)(2,1)} %get-tuple-element.33), kind=kOutput, calls=%fused_computation.10 | convolution fusion | flops 8594128896 | bytes 18874368 | tf_op jit(solution)/shard_map/dot_general | solution.py:273
  280.6 16.8 %multiply_reduce_fusion = (bf16[1024]{0:T(1024)(128)(2,1)S(1)}, f32[1024]{0:T(1024)S(1)}, bf16[1024]{0:T(1024)(128)(2,1)S(1)}, f32[1024,1024]{1,0:T(8,128)S(1)}, bf16[1024,1024]{1,0:T(8,128)(2,1)}) fusion(f32[1024,1024]{1,0:T(8,128)S(1)} %copy-done.4, f32[1024]{0:T(1024)S(1)} %fusion.46, f32[1024]{0:T(1024)S(1)} %broadcast_multiply_fusion, ...), kind=kOutput, calls=%fused_computation.48 | convolution fusion | flops 8604611584 | bytes 31481856 | tf_op jit(solution)/shard_map/dot_general | solution.py:279
  297.4 1.9 fusion.53
  300.1 1.4 copy-done.5
  301.5 1.0 copy-done.32
  302.5 2.4 convolution_convert_fusion.4
  305.0 0.7 slice-done.5
  305.7 4.7 pad_maximum_fusion
  310.4 5.9 convolution_convert_fusion.3.grad_ref
  316.3 40.1 %attend_backward.1 = (bf16[1024,1024]{1,0:T(8,128)(2,1)}, bf16[1024,1024]{1,0:T(8,128)(2,1)}, bf16[1024,1024]{1,0:T(8,128)(2,1)}, f32[1,3,1024]{2,1,0:T(4,128)}) custom-call(s32[1,4]{1,0:T(1,128)} %bitcast.88, s32[1,4]{1,0:T(1,128)} %bitcast_subtract_fusion.count_ref, bf16[1024,1024]{1,0:T(8,128)(2,1)} %get-tuple-element.34.query_ref, ...), custom_call_target="tpu_custom_call" | custom-call | tf_op jit(solution)/shard_map/attend_backward/pallas_call | solution.py:230
  356.5 1.9 constant_dynamic-update-slice_fusion.2
  359.5 0.9 copy-done.14
  360.4 9.4 %convolution_convert_fusion.2 = bf16[1024,3072]{1,0:T(8,128)(2,1)} fusion(bf16[1024,1024]{1,0:T(8,128)(2,1)S(1)} %copy-done.14, bf16[1024,3072]{1,0:T(8,128)(2,1)S(1)} %constant_dynamic-update-slice_fusion), kind=kOutput, calls=%fused_computation.26 | convolution fusion | flops 6445596672 | bytes 14680064 | tf_op jit(solution)/shard_map/dot_general | solution.py:273
  369.8 11.0 %fusion.51 = (bf16[1024]{0:T(1024)(128)(2,1)S(1)}, f32[1024]{0:T(1024)S(1)}, f32[1024,1024]{1,0:T(8,128)S(1)}, bf16[1024,1024]{1,0:T(8,128)(2,1)}) fusion(f32[1024]{0:T(1024)S(1)} %copy-done.21, f32[1024]{0:T(1024)S(1)} %copy-done.19, bf16[1024,1024]{1,0:T(8,128)(2,1)S(1)} %copy-done.1, f32[1024,2048]{1,0:T(8,128)S(1)} %bitcast.76, ...), kind=kOutput, calls=%fused_computation.128 | convolution fusion | flops 6456080384 | bytes 25188352 | tf_op jit(solution)/shard_map/dot_general | solution.py:279
  380.9 1.9 copy-done.8
  382.8 2.4 fusion.22
  386.1 3.6 fusion.35
  389.7 1.1 pad_maximum_fusion.2
  390.8 2.4 copy.63
  393.2 3.4 convert_element_type.214
  396.6 6.8 pad_maximum_fusion.1
  404.8 15.4 %add_convert_fusion.1 = bf16[1024,1024]{1,0:T(8,128)(2,1)} fusion(f32[1024,1024]{1,0:T(8,128)} %copy-done.3, f32[1024]{0:T(1024)S(1)} %reshape.542, bf16[1024,4096]{1,0:T(8,128)(2,1)} %copy-done.33, bf16[4096,1024]{1,0:T(8,128)(2,1)} %all-gather.8.cloned.1.call-done), kind=kOutput, calls=%fused_computation.53 | convolution fusion | flops 8593080320 | bytes 23072768 | tf_op jit(solution)/shard_map/dot_general | solution.py:269
  420.3 87.3 %reduce-scatter.4.cloned.1.call-done = bf16[64,3712]{1,0:T(8,128)(2,1)} async-done(((bf16[1024,3712]{1,0:T(8,128)(2,1)}), bf16[64,3712]{1,0:T(8,128)(2,1)}) %reduce-scatter.4.cloned.1.call-update) | async-done | bytes 475152 | tf_op jit(solution)/shard_map/reduce_scatter | solution.py:305
  507.6 1.5 collective-permute-start
  509.1 6.0 add_convert_fusion
  515.1 4.9 collective-permute-done
  520.2 0.9 slice_multiply_fusion.1
  521.1 93.5 %reduce-scatter.8.cloned.1.call-done = bf16[256,1024]{1,0:T(8,128)(2,1)} async-done(((bf16[4096,1024]{1,0:T(8,128)(2,1)}), bf16[256,1024]{1,0:T(8,128)(2,1)}) %reduce-scatter.8.cloned.1.call-update) | async-done | bytes 524304 | tf_op jit(solution)/shard_map/reduce_scatter | solution.py:305
  614.6 1.5 collective-permute-start.2
  617.8 119.9 %reduce-scatter.6.cloned.1.call-done = bf16[64,5120]{1,0:T(8,128)(2,1)} async-done(((bf16[1024,5120]{1,0:T(8,128)(2,1)}), bf16[64,5120]{1,0:T(8,128)(2,1)}) %reduce-scatter.6.cloned.1.call-update) | async-done | bytes 655376 | tf_op jit(solution)/shard_map/reduce_scatter | solution.py:305
  737.7 1.5 collective-permute-start.1
  739.9 2.2 add_multiply_fusion.1
  742.1 12.0 %collective-permute-done.1 = bf16[64,5120]{1,0:T(8,128)(2,1)S(1)} collective-permute-done((bf16[64,5120]{1,0:T(8,128)(2,1)}, bf16[64,5120]{1,0:T(8,128)(2,1)S(1)}, u32[]{:S(2)}, u32[]{:S(2)}) %collective-permute-start.1) | collective-permute-done | bytes 655392 | tf_op jit(solution)/shard_map/ppermute | solution.py:307
  754.0 1.2 convert_add_fusion.1
  755.3 0.7 slice_multiply_fusion.2
  756.0 1.1 slice_multiply_fusion
  (164 shorter events, 15.5 us)
Async XLA Ops:
  7.2 85.6 %copy-start = (bf16[1024,256]{1,0:T(8,128)(2,1)S(1)}, bf16[1024,256]{1,0:T(8,128)(2,1)}, u32[]{:S(2)}) copy-start(bf16[1024,256]{1,0:T(8,128)(2,1)} %param.18) | copy-start | bytes 1572868
  7.2 8.5 %copy-start.17 = (s32[1,1024]{1,0:T(1,128)S(1)}, s32[1,1024]{1,0:T(1,128)}, u32[]{:S(2)}) copy-start(s32[1,1024]{1,0:T(1,128)} %param.19) | copy-start | bytes 12292
  7.2 77.3 %all-gather.4.cloned.1.call-start = ((), (), s32[]{:S(2)}) async-start(), calls=%async_computation.3 | async-start | bytes 8077312 | tf_op jit(solution)/shard_map/all_gather | solution.py:285
  12.3 12.0 %copy-start.1 = (bf16[1024,1024]{1,0:T(8,128)(2,1)S(1)}, bf16[1024,1024]{1,0:T(8,128)(2,1)}, u32[]{:S(2)}) copy-start(bf16[1024,1024]{1,0:T(8,128)(2,1)} %param.17) | copy-start | bytes 6291460
  12.3 161.2 %all-gather.6.cloned.1.call-start = ((), (), s32[]{:S(2)}) async-start(), calls=%async_computation.4 | async-start | bytes 11141120 | tf_op jit(solution)/shard_map/all_gather | solution.py:285
  14.4 233.9 %all-gather.8.cloned.1.call-start = ((), (), s32[]{:S(2)}) async-start(), calls=%async_computation.5 | async-start | bytes 8912896 | tf_op jit(solution)/shard_map/all_gather | solution.py:285
  15.2 492.4 %reduce-scatter.4.cloned.1.call-start = ((), (), s32[]{:S(2)}) async-start(), calls=%async_computation.6 | async-start | bytes 8077312 | tf_op jit(solution)/shard_map/reduce_scatter | solution.py:305
  20.4 5.4 copy-start.31
  25.1 70.3 %copy-start.18 = (f32[1024]{0:T(1024)}, f32[1024]{0:T(1024)S(1)}, u32[]{:S(2)}) copy-start(f32[1024]{0:T(1024)S(1)} %broadcast_multiply_fusion.1) | copy-start | bytes 12292
  25.8 0.6 copy-start.24
  26.4 69.0 %copy-start.22 = (f32[1024]{0:T(1024)}, f32[1024]{0:T(1024)S(1)}, u32[]{:S(2)}) copy-start(f32[1024]{0:T(1024)S(1)} %fusion.45) | copy-start | bytes 12292
  92.6 2.8 copy-start.27
  92.6 2.8 copy-start.20
  95.4 3.4 copy-start.2
  100.1 13.1 %copy-start.13 = (bf16[1024,1024]{1,0:T(8,128)(2,1)}, bf16[1024,1024]{1,0:T(8,128)(2,1)S(1)}, u32[]{:S(2)}) copy-start(bf16[1024,1024]{1,0:T(8,128)(2,1)S(1)} %fusion.20) | copy-start | bytes 6291460
  173.5 5.4 slice-start
  173.5 5.5 slice-start.1
  173.5 7.3 slice-start.6
  173.5 9.5 %slice-start.7 = ((s8[10485760]{0:T(1024)(128)(4,1)}), s8[4194304]{0:T(1024)(128)(4,1)S(1)}, s32[]{:S(2)}) async-start(s8[10485760]{0:T(1024)(128)(4,1)} %bitcast.100), calls=%async_computation.16 | async-start | bytes 8388608
  178.3 2.5 copy-start.3
  178.3 5.6 slice-start.8
  180.8 19.8 %copy-start.9 = (bf16[1024,1024]{1,0:T(8,128)(2,1)}, bf16[1024,1024]{1,0:T(8,128)(2,1)S(1)}, u32[]{:S(2)}) copy-start(bf16[1024,1024]{1,0:T(8,128)(2,1)S(1)} %multiply_convert_fusion.2) | copy-start | bytes 6291460
  183.9 20.1 %copy-start.6 = (bf16[1024,1024]{1,0:T(8,128)(2,1)S(1)}, bf16[1024,1024]{1,0:T(8,128)(2,1)}, u32[]{:S(2)}) copy-start(bf16[1024,1024]{1,0:T(8,128)(2,1)} %param.20) | copy-start | bytes 6291460
  200.6 3.3 copy-start.33
  248.4 17.3 %copy-start.10 = (bf16[1024,1024]{1,0:T(8,128)(2,1)S(1)}, bf16[1024,1024]{1,0:T(8,128)(2,1)}, u32[]{:S(2)}) copy-start(bf16[1024,1024]{1,0:T(8,128)(2,1)} %copy-done.9) | copy-start | bytes 6291460
  265.7 14.9 %copy-start.4 = (f32[1024,1024]{1,0:T(8,128)S(1)}, f32[1024,1024]{1,0:T(8,128)}, u32[]{:S(2)}) copy-start(f32[1024,1024]{1,0:T(8,128)} %copy-done.3) | copy-start | bytes 12582916
  297.4 2.0 copy-start.7
  299.3 2.1 copy-start.5
  299.3 3.1 copy-start.32
  301.5 3.5 copy-start.15
  301.5 3.5 slice-start.4
  302.5 3.2 slice-start.5
  356.4 2.2 copy-start.12
  356.4 2.8 copy-start.11
  358.7 1.7 copy-start.14
  358.7 11.1 %slice-start.2 = ((s8[8388608]{0:T(1024)(128)(4,1)}), s8[4194304]{0:T(1024)(128)(4,1)S(1)}, s32[]{:S(2)}) async-start(s8[8388608]{0:T(1024)(128)(4,1)} %bitcast.75), calls=%async_computation.11 | async-start | bytes 8388608
  360.4 9.4 %slice-start.3 = ((s8[8388608]{0:T(1024)(128)(4,1)}), s8[4194304]{0:T(1024)(128)(4,1)S(1)}, s32[]{:S(2)}) async-start(s8[8388608]{0:T(1024)(128)(4,1)} %bitcast.75), calls=%async_computation.12 | async-start | bytes 8388608
  360.4 9.4 %copy-start.19 = (f32[1024]{0:T(1024)S(1)}, f32[1024]{0:T(1024)}, u32[]{:S(2)}) copy-start(f32[1024]{0:T(1024)} %copy-done.18) | copy-start | bytes 12292
  360.4 9.4 %copy-start.21 = (f32[1024]{0:T(1024)S(1)}, f32[1024]{0:T(1024)}, u32[]{:S(2)}) copy-start(f32[1024]{0:T(1024)} %copy-done.20) | copy-start | bytes 12292
  360.4 9.4 %copy-start.23 = (f32[1024]{0:T(1024)S(1)}, f32[1024]{0:T(1024)}, u32[]{:S(2)}) copy-start(f32[1024]{0:T(1024)} %copy-done.22) | copy-start | bytes 12292
  360.4 9.4 %copy-start.28 = (f32[1024]{0:T(1024)S(1)}, f32[1024]{0:T(1024)}, u32[]{:S(2)}) copy-start(f32[1024]{0:T(1024)} %copy-done.27) | copy-start | bytes 12292
  369.8 11.0 %copy-start.25 = (f32[1024]{0:T(1024)S(1)}, f32[1024]{0:T(1024)}, u32[]{:S(2)}) copy-start(f32[1024]{0:T(1024)} %copy-done.24) | copy-start | bytes 12292
  380.9 2.0 copy-start.8
  380.9 4.5 copy-start.30
  380.9 4.9 copy-start.29
  403.5 211.1 %reduce-scatter.8.cloned.1.call-start = ((), (), s32[]{:S(2)}) async-start(), calls=%async_computation.8 | async-start | bytes 8912896 | tf_op jit(solution)/shard_map/reduce_scatter | solution.py:305
  404.1 0.7 copy-start.26
  404.1 333.6 %reduce-scatter.6.cloned.1.call-start = ((), (), s32[]{:S(2)}) async-start(), calls=%async_computation.7 | async-start | bytes 11141120 | tf_op jit(solution)/shard_map/reduce_scatter | solution.py:305
  507.6 12.4 %copy-start.16 = (bf16[64,3712]{1,0:T(8,128)(2,1)S(1)}, bf16[64,3712]{1,0:T(8,128)(2,1)}, u32[]{:S(2)}) copy-start(bf16[64,3712]{1,0:T(8,128)(2,1)} %reduce-scatter.4.cloned.1.call-done) | copy-start | bytes 1425412
  507.6 12.4 %collective-permute-start = (bf16[64,3712]{1,0:T(8,128)(2,1)}, bf16[64,3712]{1,0:T(8,128)(2,1)S(1)}, u32[]{:S(2)}, u32[]{:S(2)}) collective-permute-start(bf16[64,3712]{1,0:T(8,128)(2,1)} %reduce-scatter.4.cloned.1.call-done), channel_id=1, source_target_pairs={{0,16},{16,0},{1,17},{17,1},{2,18},{18,2},{3,19},{19,3},{4,20},{20... | collective-permute-start | bytes 1425416 | tf_op jit(solution)/shard_map/ppermute | solution.py:307
  614.6 125.3 %collective-permute-start.2 = (bf16[256,1024]{1,0:T(8,128)(2,1)}, bf16[256,1024]{1,0:T(8,128)(2,1)S(1)}, u32[]{:S(2)}, u32[]{:S(2)}) collective-permute-start(bf16[256,1024]{1,0:T(8,128)(2,1)} %reduce-scatter.8.cloned.1.call-done), channel_id=1, source_target_pairs={{0,16},{16,0},{1,17},{17,1},{2,18},{18,2},{3,19},{19,3},{4,20},{20... | collective-permute-start | bytes 1572872 | tf_op jit(solution)/shard_map/ppermute | solution.py:307
  737.7 16.3 %collective-permute-start.1 = (bf16[64,5120]{1,0:T(8,128)(2,1)}, bf16[64,5120]{1,0:T(8,128)(2,1)S(1)}, u32[]{:S(2)}, u32[]{:S(2)}) collective-permute-start(bf16[64,5120]{1,0:T(8,128)(2,1)} %reduce-scatter.6.cloned.1.call-done), channel_id=1, source_target_pairs={{0,16},{16,0},{1,17},{17,1},{2,18},{18,2},{3,19},{19,3},{4,20},{20... | collective-permute-start | bytes 1966088 | tf_op jit(solution)/shard_map/ppermute | solution.py:307
Sparse Core Ops, SparseCore 0:
  12.4 72.0 all-gather.3
  87.4 86.0 all-gather.5
  175.6 72.6 all-gather.7
  403.6 103.9 reduce-scatter.3
  511.5 103.0 reduce-scatter.7
  618.5 119.1 reduce-scatter.5

commit v3 on v2

--- a/solution.py
+++ b/solution.py
@@ -301,6 +301,44 @@
     return parts
 
 
+def plane_share(partial):
+    if lax.axis_size("dp") != 2:
+        return partial
+    rows, cols = (partial.shape[0] // 2, partial.shape[1] // 2)
+    plane, core = (lax.axis_index("dp"), lax.axis_index("fsdp") % 2)
+
+    def part(core_at, plane_at):
+        return lax.dynamic_slice(partial, (core_at * rows, plane_at * cols), (rows, cols))
+
+    shards = lax.axis_size("fsdp")
+    sent = lax.ppermute(
+        part(1 - core, 1 - plane), "fsdp", [(i, i ^ 1) for i in range(shards)]
+    )
+    both = part(core, 1 - plane).astype(jnp.float32) + sent.astype(jnp.float32)
+    other = lax.ppermute(both.astype(jnp.bfloat16), "dp", [(0, 1), (1, 0)])
+    kept = part(core, plane).astype(jnp.float32) + other.astype(jnp.float32)
+    mine = lax.dynamic_slice(partial, (0, plane * cols), (2 * rows, cols))
+    return lax.dynamic_update_slice(mine, kept.astype(jnp.bfloat16), (core * rows, 0))
+
+
+def reduce_planes(shares):
+    share = lax.psum_scatter(
+        jnp.concatenate(shares, axis=1), "fsdp", scatter_dimension=0, tiled=True
+    )
+    cuts = [sum(s.shape[1] for s in shares[:i]) for i in range(1, len(shares))]
+    if lax.axis_size("dp") != 2:
+        total = lax.psum(share.astype(jnp.float32), "dp")
+        return jnp.split(total, cuts, axis=1)
+    other = lax.ppermute(share, "dp", [(0, 1), (1, 0)])
+    first = lax.axis_index("dp") == 0
+    left = jnp.where(first, share, other).astype(jnp.float32)
+    right = jnp.where(first, other, share).astype(jnp.float32)
+    return [
+        jnp.concatenate(pair, axis=1)
+        for pair in zip(jnp.split(left, cuts, axis=1), jnp.split(right, cuts, axis=1))
+    ]
+
+
 def reduce_weight(partial):
     share = lax.psum_scatter(partial, "fsdp", scatter_dimension=0, tiled=True)
     if lax.axis_size("dp") == 2:
@@ -386,24 +424,24 @@
     up_bias_sum = jnp.sum(grad_up, axis=0)
     grad_up_low = grad_up.astype(jnp.bfloat16)
     up_sum = product_left(normed_two, grad_up_low).astype(jnp.bfloat16)
+    up_half = plane_share(up_sum)
     grad_normed_two = product_right(after(grad_up_low, up_sum), w_up)
     grad_hidden_part, gain_two_sum, bias_two_sum, grad_shift_two = pull_two(grad_normed_two)
     grad_hidden = grad_out + grad_hidden_part
     out_bias_sum = jnp.sum(grad_hidden, axis=0)
     grad_hidden_low = grad_hidden.astype(jnp.bfloat16)
     out_sum = product_left(mixed, grad_hidden_low).astype(jnp.bfloat16)
-    two_sum = jnp.concatenate([out_sum, up_sum], axis=1)
-    two_share = reduce_weight(two_sum)
-    out_share = two_share[:, :width]
-    up_share = two_share[:, width:]
-    grad_mixed = product_right(after(grad_hidden_low, two_sum), w_out).astype(jnp.bfloat16)
+    out_half = plane_share(out_sum)
+    out_share, up_share = reduce_planes([out_half, up_half])
+    grad_mixed = product_right(after(grad_hidden_low, out_sum), w_out).astype(jnp.bfloat16)
     grad_query, grad_key, grad_value, qkv_bias_rows = attend_backward(
         query, key, value, grad_mixed, lse, tables, bounds, block
     )
     qkv_bias_sum = jnp.sum(qkv_bias_rows, axis=0).reshape(-1)
     grad_qkv_low = jnp.concatenate([grad_query, grad_key, grad_value], axis=1)
     qkv_sum = product_left(normed_one, grad_qkv_low).astype(jnp.bfloat16)
-    grad_normed_one = product_right(grad_qkv_low, w_qkv)
+    qkv_half = plane_share(qkv_sum)
+    grad_normed_one = product_right(after(grad_qkv_low, qkv_sum), w_qkv)
     grad_tokens_part, gain_one_sum, bias_one_sum, grad_shift_one = pull_one(grad_normed_one)
     tokens_grad = (grad_hidden + grad_tokens_part).astype(jnp.bfloat16)
     grad_shift = jnp.concatenate([grad_shift_one, grad_shift_two], axis=1).astype(jnp.bfloat16)
@@ -416,9 +454,11 @@
     packed = packed.reshape(shards * time_rows, -1)
     last_sum = jnp.concatenate([time_sum, packed], axis=1).astype(jnp.bfloat16)
     last_sum = last_sum.reshape(qkv_sum.shape[0], -1)
-    one_share = reduce_weight(jnp.concatenate([qkv_sum, last_sum], axis=1))
-    qkv_share = one_share[:, : qkv_sum.shape[1]]
-    last_share = one_share[:, qkv_sum.shape[1] :].reshape(time_rows, first_cols)
+    last_cols = last_sum.shape[1]
+    last_sum = jnp.pad(last_sum, ((0, 0), (0, -last_cols % (2 * LANES))))
+    last_half = plane_share(last_sum)
+    qkv_share, last_share = reduce_planes([qkv_half, last_half])
+    last_share = last_share[:, :last_cols].reshape(time_rows, first_cols)
     smalls = unpack(last_share[:, time_cols:] * factor, sizes, 1)
     return (
         layer_out,

time: 769 us -> 740 us (0.962)
  waiting for transfers between devices: 433 us -> 365 us
  starting transfers between devices: 4.64 us -> 21.4 us
  local copies, waits for them, and re-layouts: 40.8 us -> 54.4 us
  other arithmetic: 48.6 us -> 57.3 us
    reduce_scatter x3 -> x1, waiting for transfers between devices: 301 us -> 97 us  [reduce_weight(): share = lax.psum_scatter(partial, 'fsdp', scatter_dimension=0, tiled=True)]
    ppermute x0 -> x10, waiting for transfers between devices: none -> 92 us  [the longest x4 77.5 us: plane_share(): other = lax.ppermute(both.astype(jnp.bfloat16), 'dp', [(0, 1), (1, 0)])]
    reduce_scatter x0 -> x2, waiting for transfers between devices: none -> 50.5 us  [reduce_planes(): lax.psum_scatter(jnp.concatenate(shares, axis=1), 'fsdp', scatter_dimensi...]
    ppermute x0 -> x10, starting transfers between devices: none -> 19.6 us  [the longest x4 12.6 us: plane_share(): lax.ppermute(part(1 - core, 1 - plane), 'fsdp', [(i, i ^ 1) for i in rang...]
    dynamic_slice x0 -> x8, local copies, waits for them, and re-layouts: none -> 12.4 us  [the longest x4 7.22 us: plane_share(): mine = lax.dynamic_slice(partial, (0, plane * cols), (2 * rows, cols))]
    convert_element_type x0 -> x6, other arithmetic: none -> 10.6 us  [the longest x4 9.45 us: plane_share(): other = lax.ppermute(both.astype(jnp.bfloat16), 'dp', [(0, 1), (1, 0)])]
    ppermute x3 -> x1, waiting for transfers between devices: 16.9 us -> 10.2 us  [reduce_weight(): other = lax.ppermute(share, 'dp', [(0, 1), (1, 0)])]
  transfers between devices with their start and end apart: 9 -> 17, of which waited for: 8 -> 12; matrix products, arithmetic and copies ran while one was open for 13% -> 21% of each run, Pallas kernels for 5% -> 5%
where the time goes in v3:
time: 740 us; the launch traced here: 734 us
  waiting for transfers between devices  365 us (49%)
  matrix products  145 us (20%)
  Pallas kernels  76.5 us (10%)
  other arithmetic  57.3 us (8%)
  local copies, waits for them, and re-layouts  54.4 us (7%)
  starting transfers between devices  21.4 us (3%)
  between operations  15.1 us (2%)
    all_gather x3, waiting for transfers between devices, gather(): return lax.all_gather(part, 'fsdp', axis=0, tiled=True)  114 us
    reduce_scatter x1, waiting for transfers between devices, reduce_weight(): share = lax.psum_scatter(partial, 'fsdp', scatter_dimension=0, tiled=True)  97 us
    ppermute x4, waiting for transfers between devices, plane_share(): other = lax.ppermute(both.astype(jnp.bfloat16), 'dp', [(0, 1), (1, 0)])  77.5 us
    dot_general x5, matrix products, product(): return jnp.dot(left, right, preferred_element_type=jnp.float32)  52.8 us
    reduce_scatter x2, waiting for transfers between devices, reduce_planes(): lax.psum_scatter(jnp.concatenate(shares, axis=1), 'fsdp', scatter_dimensi...  50.5 us
    dot_general x4, matrix products, product_right(): lax.dot_general(left, right, (((1,), (1,)), ((), ())), preferred_element_...  50.5 us
    dot_general x5, matrix products, product_left(): lax.dot_general(left, right, (((0,), (0,)), ((), ())), preferred_element_...  41.3 us
    pallas_call x1, Pallas kernels, attend_backward(): pl.pallas_call(functools.partial(backward_kernel, block=block), grid_spec...  40.1 us
  transfers between devices with their start and end apart: 17, of which 12 were waited for; matrix products, arithmetic and copies ran while one was open for 21% of the time, Pallas kernels for 5%

profile of v3, /device:TPU:0, one launch (start us, length us, event | category | flops | bytes accessed | tf_op | source)
XLA Modules:
  0.0 734.3 jit_solution(7025703036629856601)
XLA Ops:
  10.4 1.8 pad_maximum_fusion.6
  12.3 2.1 pad_maximum_fusion.3
  17.5 2.0 reduce.2
  20.5 1.9 fusion.45
  22.4 1.8 pad_maximum_fusion.4
  26.4 58.1 %all-gather.4.cloned.1.call-done = bf16[1024,3712]{1,0:T(8,128)(2,1)} async-done(((bf16[64,3712]{1,0:T(8,128)(2,1)}), bf16[1024,3712]{1,0:T(8,128)(2,1)}) %all-gather.4.cloned.1.call-update) | async-done | bytes 7602192 | tf_op jit(solution)/shard_map/all_gather | solution.py:285
  84.5 2.5 slice.134
  87.0 3.6 reshape.511
  92.8 2.6 convolution_bitcast_fusion
  95.4 3.4 copy-done.2
  98.8 1.4 fusion.20
  100.2 13.1 %broadcast_add_fusion.q_ref.k_ref.v_ref = f32[1024,3072]{1,0:T(8,128)} fusion(f32[3072]{0:T(1024)S(1)} %reshape.537, bf16[1024,1024]{1,0:T(8,128)(2,1)S(1)} %fusion.20, bf16[1024,3712]{1,0:T(8,128)(2,1)} %all-gather.4.cloned.1.call-done), kind=kOutput, calls=%fused_computation.16 | convolution fusion | flops 6445596672 | bytes 20983808 | tf_op jit(solution)/shard_map/dot_general | solution.py:269
  114.2 36.3 %attend_forward.1 = (bf16[1024,1024]{1,0:T(8,128)(2,1)}, bf16[1024,1024]{1,0:T(8,128)(2,1)}, bf16[1024,1024]{1,0:T(8,128)(2,1)}, bf16[1024,1024]{1,0:T(8,128)(2,1)}, f32[8,2,1024]{2,1,0:T(2,128)}) custom-call(s32[1,4]{1,0:T(1,128)} %bitcast.85, s32[1,4]{1,0:T(1,128)} %bitcast_subtract_fusion.count_ref, f32[1024,3072]{1,0:T(8,128)} %broadcast_add_fusion.q_ref.k_ref.v_ref, ...), custom_call_target="tpu_custom_call" | custom-call | tf_op jit(solution)/shard_map/attend_forward/pallas_call | solution.py:204
  150.6 23.3 %all-gather.6.cloned.1.call-done = bf16[1024,5120]{1,0:T(8,128)(2,1)} async-done(((bf16[64,5120]{1,0:T(8,128)(2,1)}), bf16[1024,5120]{1,0:T(8,128)(2,1)}) %all-gather.6.cloned.1.call-update) | async-done | bytes 10485776 | tf_op jit(solution)/shard_map/all_gather | solution.py:285
  173.8 4.8 fusion.61
  179.3 1.8 multiply_convert_fusion.2
  181.2 2.2 slice-done.5
  184.3 16.7 %fusion.3 = (f32[1024,4096]{1,0:T(8,128)}, bf16[1024,4096]{1,0:T(8,128)(2,1)S(1)}) fusion(f32[4096]{0:T(1024)S(1)} %bitcast.84, bf16[1024,1024]{1,0:T(8,128)(2,1)S(1)} %multiply_convert_fusion.2, bf16[1024,5120]{1,0:T(8,128)(2,1)S(1)} %bitcast.99), kind=kOutput, calls=%fused_computation.4 | convolution fusion | flops 8636071936 | bytes 35667968 | tf_op jit(solution)/shard_map/dot_general | solution.py:269
  201.1 3.3 copy-done.35
  204.4 11.3 %convolution_convert_fusion.1 = bf16[4096,1024]{1,0:T(8,128)(2,1)} fusion(bf16[1024,4096]{1,0:T(8,128)(2,1)S(1)} %get-tuple-element.31, bf16[1024,1024]{1,0:T(8,128)(2,1)S(1)} %copy-done.7), kind=kOutput, calls=%fused_computation.9 | convolution fusion | flops 8594128896 | bytes 18874368 | tf_op jit(solution)/shard_map/dot_general | solution.py:273
  215.7 32.6 %all-gather.8.cloned.1.call-done = bf16[4096,1024]{1,0:T(8,128)(2,1)} async-done(((bf16[256,1024]{1,0:T(8,128)(2,1)}), bf16[4096,1024]{1,0:T(8,128)(2,1)}) %all-gather.8.cloned.1.call-update) | async-done | bytes 8388624 | tf_op jit(solution)/shard_map/all_gather | solution.py:285
  248.4 17.3 %fusion.59 = (bf16[4096]{0:T(1024)(128)(2,1)S(1)}, bf16[1024,4096]{1,0:T(8,128)(2,1)}) fusion(f32[1024,4096]{1,0:T(8,128)} %get-tuple-element.33, bf16[4096,1024]{1,0:T(8,128)(2,1)} %all-gather.8.cloned.1.call-done, bf16[1024,1024]{1,0:T(8,128)(2,1)} %param.20), kind=kOutput, calls=%fused_computation.152 | convolution fusion | flops 8602513408 | bytes 35659776 | tf_op jit(solution)/shard_map/dot_general | solution.py:279
  265.7 14.9 %convolution_convert_fusion = bf16[1024,4096]{1,0:T(8,128)(2,1)} fusion(bf16[1024,1024]{1,0:T(8,128)(2,1)S(1)} %copy-done.12, bf16[1024,4096]{1,0:T(8,128)(2,1)} %get-tuple-element.34), kind=kOutput, calls=%fused_computation.8 | convolution fusion | flops 8594128896 | bytes 18874368 | tf_op jit(solution)/shard_map/dot_general | solution.py:273
  280.6 16.8 %multiply_reduce_fusion = (bf16[1024]{0:T(1024)(128)(2,1)S(1)}, f32[1024]{0:T(1024)S(1)}, bf16[1024]{0:T(1024)(128)(2,1)S(1)}, f32[1024,1024]{1,0:T(8,128)S(1)}, bf16[1024,1024]{1,0:T(8,128)(2,1)}) fusion(f32[1024,1024]{1,0:T(8,128)S(1)} %copy-done.4, f32[1024]{0:T(1024)S(1)} %fusion.50, f32[1024]{0:T(1024)S(1)} %broadcast_multiply_fusion, ...), kind=kOutput, calls=%fused_computation.49 | convolution fusion | flops 8604611584 | bytes 31481856 | tf_op jit(solution)/shard_map/dot_general | solution.py:279
  297.5 1.9 fusion.57
  300.1 1.4 copy-done.5
  302.5 3.8 convolution_convert_fusion.4
  306.3 5.3 convolution_convert_fusion.3.grad_ref
  311.6 40.1 %attend_backward.1 = (bf16[1024,1024]{1,0:T(8,128)(2,1)}, bf16[1024,1024]{1,0:T(8,128)(2,1)}, bf16[1024,1024]{1,0:T(8,128)(2,1)}, f32[1,3,1024]{2,1,0:T(4,128)}) custom-call(s32[1,4]{1,0:T(1,128)} %bitcast.86, s32[1,4]{1,0:T(1,128)} %bitcast_subtract_fusion.count_ref, bf16[1024,1024]{1,0:T(8,128)(2,1)} %get-tuple-element.35.query_ref, ...), custom_call_target="tpu_custom_call" | custom-call | tf_op jit(solution)/shard_map/attend_backward/pallas_call | solution.py:230
  351.8 1.9 constant_dynamic-update-slice_fusion.2
  355.7 7.8 %convolution_convert_fusion.2 = bf16[1024,3072]{1,0:T(8,128)(2,1)S(1)} fusion(bf16[1024,1024]{1,0:T(8,128)(2,1)S(1)} %copy-done.16, bf16[1024,3072]{1,0:T(8,128)(2,1)S(1)} %constant_dynamic-update-slice_fusion), kind=kOutput, calls=%fused_computation.24 | convolution fusion | flops 6445596672 | bytes 14680064 | tf_op jit(solution)/shard_map/dot_general | solution.py:273
  363.5 1.4 dynamic_slice.51
  364.9 1.7 copy-done.10
  366.6 12.4 %collective-permute-start = (bf16[512,1536]{1,0:T(8,128)(2,1)}, bf16[512,1536]{1,0:T(8,128)(2,1)}, u32[]{:S(2)}, u32[]{:S(2)}) collective-permute-start(bf16[512,1536]{1,0:T(8,128)(2,1)} %dynamic_slice.51), channel_id=1, source_target_pairs={{0,1},{1,0},{2,3},{3,2},{4,5},{5,4},{6,7},{7,6},{8,9},{9,8},{10,11... | collective-permute-start | bytes 4718600 | tf_op jit(solution)/shard_map/ppermute | solution.py:314
  379.1 11.0 %fusion.55 = (bf16[1024]{0:T(1024)(128)(2,1)S(1)}, f32[1024]{0:T(1024)S(1)}, f32[1024,1024]{1,0:T(8,128)S(1)}, bf16[1024,1024]{1,0:T(8,128)(2,1)}) fusion(f32[1024]{0:T(1024)S(1)} %copy-done.23, f32[1024]{0:T(1024)S(1)} %copy-done.21, bf16[1024,1024]{1,0:T(8,128)(2,1)S(1)} %copy-done.1, f32[1024,2048]{1,0:T(8,128)S(1)} %bitcast.76, ...), kind=kOutput, calls=%fused_computation.150 | convolution fusion | flops 6456080384 | bytes 25188352 | tf_op jit(solution)/shard_map/dot_general | solution.py:279
  390.1 1.9 copy-done.9
  392.1 2.4 fusion.22
  395.4 3.6 fusion.35
  399.0 3.4 add_convert_fusion.5
  402.4 1.5 collective-permute-start.1
  405.0 2.4 copy.63
  407.4 3.4 convert_element_type.294
  411.9 1.7 collective-permute-done.2
  416.6 2.1 constant_dynamic-slice_fusion.2
  418.7 28.7 %collective-permute-done.3 = bf16[512,384]{1,0:T(8,128)(2,1)S(1)} collective-permute-done((bf16[512,384]{1,0:T(8,128)(2,1)S(1)}, bf16[512,384]{1,0:T(8,128)(2,1)S(1)}, u32[]{:S(2)}, u32[]{:S(2)}) %collective-permute-start.3) | collective-permute-done | bytes 393248 | tf_op jit(solution)/shard_map/ppermute | solution.py:318
  447.5 2.3 fusion.41
  449.8 2.1 pad_maximum_fusion.1
  452.2 1.7 dynamic_slice.63
  454.1 4.7 collective-permute-done.7
  458.8 3.8 add_convert_fusion.1
  465.1 2.1 collective-permute-done.5
  469.1 1.4 constant_dynamic-slice_fusion.1
  470.4 2.5 constant_dynamic-slice_fusion
  473.0 48.8 %collective-permute-done.6 = bf16[512,512]{1,0:T(8,128)(2,1)} collective-permute-done((bf16[512,512]{1,0:T(8,128)(2,1)S(1)}, bf16[512,512]{1,0:T(8,128)(2,1)}, u32[]{:S(2)}, u32[]{:S(2)}) %collective-permute-start.6) | collective-permute-done | bytes 524320 | tf_op jit(solution)/shard_map/ppermute | solution.py:318
  523.2 3.1 fusion.38
  526.3 2.7 pad_maximum_fusion
  529.8 15.6 %add_convert_fusion.3 = bf16[1024,1024]{1,0:T(8,128)(2,1)} fusion(f32[1024,1024]{1,0:T(8,128)} %copy-done.3, f32[1024]{0:T(1024)S(1)} %reshape.542, bf16[1024,4096]{1,0:T(8,128)(2,1)} %copy-done.35, bf16[4096,1024]{1,0:T(8,128)(2,1)} %all-gather.8.cloned.1.call-done), kind=kOutput, calls=%fused_computation.54 | convolution fusion | flops 8593080320 | bytes 23072768 | tf_op jit(solution)/shard_map/dot_general | solution.py:269
  546.7 6.2 add_convert_fusion.2
  555.6 50.5 %reduce-scatter.6.cloned.1.call-done = bf16[64,2560]{1,0:T(8,128)(2,1)} async-done(((bf16[1024,2560]{1,0:T(8,128)(2,1)}), bf16[64,2560]{1,0:T(8,128)(2,1)}) %reduce-scatter.6.cloned.1.call-update) | async-done | bytes 327696 | tf_op jit(solution)/shard_map/reduce_scatter | solution.py:325
  606.1 1.5 collective-permute-start.9
  608.5 6.0 collective-permute-done.9
  615.6 97.0 %reduce-scatter.8.cloned.1.call-done = bf16[256,1024]{1,0:T(8,128)(2,1)} async-done(((bf16[4096,1024]{1,0:T(8,128)(2,1)}), bf16[256,1024]{1,0:T(8,128)(2,1)}) %reduce-scatter.8.cloned.1.call-update) | async-done | bytes 524304 | tf_op jit(solution)/shard_map/reduce_scatter | solution.py:343
  712.6 1.5 collective-permute-start.10
  716.0 10.2 %collective-permute-done.10 = bf16[256,1024]{1,0:T(8,128)(2,1)S(1)} collective-permute-done((bf16[256,1024]{1,0:T(8,128)(2,1)}, bf16[256,1024]{1,0:T(8,128)(2,1)S(1)}, u32[]{:S(2)}, u32[]{:S(2)}) %collective-permute-start.10) | collective-permute-done | bytes 524320 | tf_op jit(solution)/shard_map/ppermute | solution.py:345
  (203 shorter events, 39.9 us)
Async XLA Ops:
  7.2 85.6 %copy-start = (bf16[1024,256]{1,0:T(8,128)(2,1)S(1)}, bf16[1024,256]{1,0:T(8,128)(2,1)}, u32[]{:S(2)}) copy-start(bf16[1024,256]{1,0:T(8,128)(2,1)} %param.18) | copy-start | bytes 1572868
  7.2 8.6 %copy-start.19 = (s32[1,1024]{1,0:T(1,128)S(1)}, s32[1,1024]{1,0:T(1,128)}, u32[]{:S(2)}) copy-start(s32[1,1024]{1,0:T(1,128)} %param.19) | copy-start | bytes 12292
  7.2 77.3 %all-gather.4.cloned.1.call-start = ((), (), s32[]{:S(2)}) async-start(), calls=%async_computation.3 | async-start | bytes 8077312 | tf_op jit(solution)/shard_map/all_gather | solution.py:285
  12.3 12.0 %copy-start.1 = (bf16[1024,1024]{1,0:T(8,128)(2,1)S(1)}, bf16[1024,1024]{1,0:T(8,128)(2,1)}, u32[]{:S(2)}) copy-start(bf16[1024,1024]{1,0:T(8,128)(2,1)} %param.17) | copy-start | bytes 6291460
  12.3 161.6 %all-gather.6.cloned.1.call-start = ((), (), s32[]{:S(2)}) async-start(), calls=%async_computation.4 | async-start | bytes 11141120 | tf_op jit(solution)/shard_map/all_gather | solution.py:285
  14.4 234.0 %all-gather.8.cloned.1.call-start = ((), (), s32[]{:S(2)}) async-start(), calls=%async_computation.5 | async-start | bytes 8912896 | tf_op jit(solution)/shard_map/all_gather | solution.py:285
  15.2 530.3 %reduce-scatter.4.cloned.1.call-start = ((), (), s32[]{:S(2)}) async-start(), calls=%async_computation.6 | async-start | bytes 4177920 | tf_op jit(solution)/shard_map/reduce_scatter | solution.py:325
  20.4 5.4 copy-start.33
  25.1 70.3 %copy-start.20 = (f32[1024]{0:T(1024)}, f32[1024]{0:T(1024)S(1)}, u32[]{:S(2)}) copy-start(f32[1024]{0:T(1024)S(1)} %broadcast_multiply_fusion.1) | copy-start | bytes 12292
  25.8 0.6 copy-start.26
  26.4 69.0 %copy-start.24 = (f32[1024]{0:T(1024)}, f32[1024]{0:T(1024)S(1)}, u32[]{:S(2)}) copy-start(f32[1024]{0:T(1024)S(1)} %fusion.49) | copy-start | bytes 12292
  92.6 2.8 copy-start.29
  92.6 2.8 copy-start.22
  95.4 3.4 copy-start.2
  100.2 13.1 %copy-start.15 = (bf16[1024,1024]{1,0:T(8,128)(2,1)}, bf16[1024,1024]{1,0:T(8,128)(2,1)S(1)}, u32[]{:S(2)}) copy-start(bf16[1024,1024]{1,0:T(8,128)(2,1)S(1)} %fusion.20) | copy-start | bytes 6291460
  173.8 5.4 slice-start
  173.8 5.5 slice-start.1
  173.8 7.3 slice-start.4
  173.8 9.5 %slice-start.5 = ((s8[10485760]{0:T(1024)(128)(4,1)}), s8[4194304]{0:T(1024)(128)(4,1)S(1)}, s32[]{:S(2)}) async-start(s8[10485760]{0:T(1024)(128)(4,1)} %bitcast.98), calls=%async_computation.14 | async-start | bytes 8388608
  178.7 2.5 copy-start.3
  178.7 5.6 slice-start.6
  181.2 19.9 %copy-start.11 = (bf16[1024,1024]{1,0:T(8,128)(2,1)}, bf16[1024,1024]{1,0:T(8,128)(2,1)S(1)}, u32[]{:S(2)}) copy-start(bf16[1024,1024]{1,0:T(8,128)(2,1)S(1)} %multiply_convert_fusion.2) | copy-start | bytes 6291460
  184.3 20.1 %copy-start.7 = (bf16[1024,1024]{1,0:T(8,128)(2,1)S(1)}, bf16[1024,1024]{1,0:T(8,128)(2,1)}, u32[]{:S(2)}) copy-start(bf16[1024,1024]{1,0:T(8,128)(2,1)} %param.20) | copy-start | bytes 6291460
  201.1 3.3 copy-start.35
  248.4 17.3 %copy-start.12 = (bf16[1024,1024]{1,0:T(8,128)(2,1)S(1)}, bf16[1024,1024]{1,0:T(8,128)(2,1)}, u32[]{:S(2)}) copy-start(bf16[1024,1024]{1,0:T(8,128)(2,1)} %copy-done.11) | copy-start | bytes 6291460
  265.7 14.9 %copy-start.4 = (f32[1024,1024]{1,0:T(8,128)S(1)}, f32[1024,1024]{1,0:T(8,128)}, u32[]{:S(2)}) copy-start(f32[1024,1024]{1,0:T(8,128)} %copy-done.3) | copy-start | bytes 12582916
  297.5 2.0 copy-start.8
  299.4 2.1 copy-start.5
  299.4 3.1 copy-start.34
  351.7 2.2 copy-start.14
  351.8 2.8 copy-start.13
  354.0 1.7 copy-start.16
  354.0 25.1 %slice-start.2 = ((s8[8388608]{0:T(1024)(128)(4,1)}), s8[4194304]{0:T(1024)(128)(4,1)S(1)}, s32[]{:S(2)}) async-start(s8[8388608]{0:T(1024)(128)(4,1)} %bitcast.75), calls=%async_computation.11 | async-start | bytes 8388608
  355.7 23.4 %slice-start.3 = ((s8[8388608]{0:T(1024)(128)(4,1)}), s8[4194304]{0:T(1024)(128)(4,1)S(1)}, s32[]{:S(2)}) async-start(s8[8388608]{0:T(1024)(128)(4,1)} %bitcast.75), calls=%async_computation.12 | async-start | bytes 8388608
  355.7 23.4 %copy-start.21 = (f32[1024]{0:T(1024)S(1)}, f32[1024]{0:T(1024)}, u32[]{:S(2)}) copy-start(f32[1024]{0:T(1024)} %copy-done.20) | copy-start | bytes 12292
  355.7 23.4 %copy-start.23 = (f32[1024]{0:T(1024)S(1)}, f32[1024]{0:T(1024)}, u32[]{:S(2)}) copy-start(f32[1024]{0:T(1024)} %copy-done.22) | copy-start | bytes 12292
  355.7 23.4 %copy-start.25 = (f32[1024]{0:T(1024)S(1)}, f32[1024]{0:T(1024)}, u32[]{:S(2)}) copy-start(f32[1024]{0:T(1024)} %copy-done.24) | copy-start | bytes 12292
  355.7 23.4 %copy-start.30 = (f32[1024]{0:T(1024)S(1)}, f32[1024]{0:T(1024)}, u32[]{:S(2)}) copy-start(f32[1024]{0:T(1024)} %copy-done.29) | copy-start | bytes 12292
  363.5 3.1 copy-start.10
  366.6 23.5 %copy-start.27 = (f32[1024]{0:T(1024)S(1)}, f32[1024]{0:T(1024)}, u32[]{:S(2)}) copy-start(f32[1024]{0:T(1024)} %copy-done.26) | copy-start | bytes 12292
  366.6 32.3 %collective-permute-start = (bf16[512,1536]{1,0:T(8,128)(2,1)}, bf16[512,1536]{1,0:T(8,128)(2,1)}, u32[]{:S(2)}, u32[]{:S(2)}) collective-permute-start(bf16[512,1536]{1,0:T(8,128)(2,1)} %dynamic_slice.51), channel_id=1, source_target_pairs={{0,1},{1,0},{2,3},{3,2},{4,5},{5,4},{6,7},{7,6},{8,9},{9,8},{10,11... | collective-permute-start | bytes 4718600 | tf_op jit(solution)/shard_map/ppermute | solution.py:314
  390.1 2.0 copy-start.9
  390.1 4.5 copy-start.32
  390.1 4.9 copy-start.31
  402.4 45.1 %collective-permute-start.1 = (bf16[512,1536]{1,0:T(8,128)(2,1)}, bf16[512,1536]{1,0:T(8,128)(2,1)}, u32[]{:S(2)}, u32[]{:S(2)}) collective-permute-start(bf16[512,1536]{1,0:T(8,128)(2,1)} %add_convert_fusion.5), channel_id=1, source_target_pairs={{0,16},{16,0},{1,17},{17,1},{2,18},{18,2},{3,19},{19,3},{4,20},{20... | collective-permute-start | bytes 4718600 | tf_op jit(solution)/shard_map/ppermute | solution.py:318
  411.8 1.8 collective-permute-start.2
  414.6 32.7 %copy-start.6 = (bf16[1024,640]{1,0:T(8,128)(2,1)S(1)}, bf16[1024,640]{1,0:T(8,128)(2,1)}, u32[]{:S(2)}) copy-start(bf16[1024,640]{1,0:T(8,128)(2,1)} %convert_element_type.294) | copy-start | bytes 3932164
  414.6 32.7 %collective-permute-start.3 = (bf16[512,384]{1,0:T(8,128)(2,1)S(1)}, bf16[512,384]{1,0:T(8,128)(2,1)S(1)}, u32[]{:S(2)}, u32[]{:S(2)}) collective-permute-start(bf16[512,384]{1,0:T(8,128)(2,1)S(1)} %add_convert_fusion.9), channel_id=1, source_target_pairs={{0,16},{16,0},{1,17},{17,1},{2,18},{18,2},{3,19},{19,3},{4,20},{20... | collective-permute-start | bytes 1179656 | tf_op jit(solution)/shard_map/ppermute | solution.py:318
  452.0 154.1 %reduce-scatter.6.cloned.1.call-start = ((), (), s32[]{:S(2)}) async-start(), calls=%async_computation.7 | async-start | bytes 5570560 | tf_op jit(solution)/shard_map/reduce_scatter | solution.py:325
  454.0 4.8 collective-permute-start.7
  462.6 60.6 %collective-permute-start.8 = (bf16[512,2048]{1,0:T(8,128)(2,1)}, bf16[512,2048]{1,0:T(8,128)(2,1)}, u32[]{:S(2)}, u32[]{:S(2)}) collective-permute-start(bf16[512,2048]{1,0:T(8,128)(2,1)} %add_convert_fusion.1), channel_id=1, source_target_pairs={{0,16},{16,0},{1,17},{17,1},{2,18},{18,2},{3,19},{19,3},{4,20},{20... | collective-permute-start | bytes 6291464 | tf_op jit(solution)/shard_map/ppermute | solution.py:318
  465.0 2.2 collective-permute-start.5
  468.3 53.5 %collective-permute-start.6 = (bf16[512,512]{1,0:T(8,128)(2,1)S(1)}, bf16[512,512]{1,0:T(8,128)(2,1)}, u32[]{:S(2)}, u32[]{:S(2)}) collective-permute-start(bf16[512,512]{1,0:T(8,128)(2,1)S(1)} %add_convert_fusion.7), channel_id=1, source_target_pairs={{0,16},{16,0},{1,17},{17,1},{2,18},{18,2},{3,19},{19,3},{4,20},{20... | collective-permute-start | bytes 1572872 | tf_op jit(solution)/shard_map/ppermute | solution.py:318
  529.0 0.7 copy-start.28
  529.0 183.6 %reduce-scatter.8.cloned.1.call-start = ((), (), s32[]{:S(2)}) async-start(), calls=%async_computation.8 | async-start | bytes 8912896 | tf_op jit(solution)/shard_map/reduce_scatter | solution.py:343
  545.4 7.4 %copy-start.18 = (bf16[64,1920]{1,0:T(8,128)(2,1)S(1)}, bf16[64,1920]{1,0:T(8,128)(2,1)}, u32[]{:S(2)}) copy-start(bf16[64,1920]{1,0:T(8,128)(2,1)} %reduce-scatter.4.cloned.1.call-done) | copy-start | bytes 737284
  545.4 7.4 %collective-permute-start.4 = (bf16[64,1920]{1,0:T(8,128)(2,1)}, bf16[64,1920]{1,0:T(8,128)(2,1)S(1)}, u32[]{:S(2)}, u32[]{:S(2)}) collective-permute-start(bf16[64,1920]{1,0:T(8,128)(2,1)} %reduce-scatter.4.cloned.1.call-done), channel_id=1, source_target_pairs={{0,16},{16,0},{1,17},{17,1},{2,18},{18,2},{3,19},{19,3},{4,20},{20... | collective-permute-start | bytes 737288 | tf_op jit(solution)/shard_map/ppermute | solution.py:332
  606.1 8.4 %collective-permute-start.9 = (bf16[64,2560]{1,0:T(8,128)(2,1)}, bf16[64,2560]{1,0:T(8,128)(2,1)S(1)}, u32[]{:S(2)}, u32[]{:S(2)}) collective-permute-start(bf16[64,2560]{1,0:T(8,128)(2,1)} %reduce-scatter.6.cloned.1.call-done), channel_id=1, source_target_pairs={{0,16},{16,0},{1,17},{17,1},{2,18},{18,2},{3,19},{19,3},{4,20},{20... | collective-permute-start | bytes 983048 | tf_op jit(solution)/shard_map/ppermute | solution.py:332
  712.6 13.5 %copy-start.17 = (bf16[256,1024]{1,0:T(8,128)(2,1)S(1)}, bf16[256,1024]{1,0:T(8,128)(2,1)}, u32[]{:S(2)}) copy-start(bf16[256,1024]{1,0:T(8,128)(2,1)} %reduce-scatter.8.cloned.1.call-done) | copy-start | bytes 1572868
  712.6 13.5 %collective-permute-start.10 = (bf16[256,1024]{1,0:T(8,128)(2,1)}, bf16[256,1024]{1,0:T(8,128)(2,1)S(1)}, u32[]{:S(2)}, u32[]{:S(2)}) collective-permute-start(bf16[256,1024]{1,0:T(8,128)(2,1)} %reduce-scatter.8.cloned.1.call-done), channel_id=1, source_target_pairs={{0,16},{16,0},{1,17},{17,1},{2,18},{18,2},{3,19},{19,3},{4,20},{20... | collective-permute-start | bytes 1572872 | tf_op jit(solution)/shard_map/ppermute | solution.py:345
Sparse Core Ops, SparseCore 0:
  12.4 72.0 all-gather.3
  87.4 86.4 all-gather.5
  176.0 72.3 all-gather.7
  452.1 69.1 reduce-scatter.3
  529.2 76.8 reduce-scatter.5
  610.0 102.5 reduce-scatter.7

commit v4 on v3

--- a/solution.py
+++ b/solution.py
@@ -303,7 +303,7 @@
 
 def plane_share(partial):
     if lax.axis_size("dp") != 2:
-        return partial
+        return (partial, partial)
     rows, cols = (partial.shape[0] // 2, partial.shape[1] // 2)
     plane, core = (lax.axis_index("dp"), lax.axis_index("fsdp") % 2)
 
@@ -315,10 +315,11 @@
         part(1 - core, 1 - plane), "fsdp", [(i, i ^ 1) for i in range(shards)]
     )
     both = part(core, 1 - plane).astype(jnp.float32) + sent.astype(jnp.float32)
-    other = lax.ppermute(both.astype(jnp.bfloat16), "dp", [(0, 1), (1, 0)])
+    both = both.astype(jnp.bfloat16)
+    other = lax.ppermute(both, "dp", [(0, 1), (1, 0)])
     kept = part(core, plane).astype(jnp.float32) + other.astype(jnp.float32)
     mine = lax.dynamic_slice(partial, (0, plane * cols), (2 * rows, cols))
-    return lax.dynamic_update_slice(mine, kept.astype(jnp.bfloat16), (core * rows, 0))
+    return (lax.dynamic_update_slice(mine, kept.astype(jnp.bfloat16), (core * rows, 0)), both)
 
 
 def reduce_planes(shares):
@@ -424,24 +425,27 @@
     up_bias_sum = jnp.sum(grad_up, axis=0)
     grad_up_low = grad_up.astype(jnp.bfloat16)
     up_sum = product_left(normed_two, grad_up_low).astype(jnp.bfloat16)
-    up_half = plane_share(up_sum)
+    up_half, _ = plane_share(up_sum)
     grad_normed_two = product_right(after(grad_up_low, up_sum), w_up)
     grad_hidden_part, gain_two_sum, bias_two_sum, grad_shift_two = pull_two(grad_normed_two)
     grad_hidden = grad_out + grad_hidden_part
     out_bias_sum = jnp.sum(grad_hidden, axis=0)
     grad_hidden_low = grad_hidden.astype(jnp.bfloat16)
     out_sum = product_left(mixed, grad_hidden_low).astype(jnp.bfloat16)
-    out_half = plane_share(out_sum)
+    out_half, _ = plane_share(out_sum)
     out_share, up_share = reduce_planes([out_half, up_half])
     grad_mixed = product_right(after(grad_hidden_low, out_sum), w_out).astype(jnp.bfloat16)
     grad_query, grad_key, grad_value, qkv_bias_rows = attend_backward(
         query, key, value, grad_mixed, lse, tables, bounds, block
     )
     qkv_bias_sum = jnp.sum(qkv_bias_rows, axis=0).reshape(-1)
+    grad_query, grad_key, grad_value, _ = lax.optimization_barrier(
+        (grad_query, grad_key, grad_value, up_half)
+    )
     grad_qkv_low = jnp.concatenate([grad_query, grad_key, grad_value], axis=1)
     qkv_sum = product_left(normed_one, grad_qkv_low).astype(jnp.bfloat16)
-    qkv_half = plane_share(qkv_sum)
-    grad_normed_one = product_right(after(grad_qkv_low, qkv_sum), w_qkv)
+    qkv_half, qkv_sent = plane_share(qkv_sum)
+    grad_normed_one = product_right(after(grad_qkv_low, qkv_sent), w_qkv)
     grad_tokens_part, gain_one_sum, bias_one_sum, grad_shift_one = pull_one(grad_normed_one)
     tokens_grad = (grad_hidden + grad_tokens_part).astype(jnp.bfloat16)
     grad_shift = jnp.concatenate([grad_shift_one, grad_shift_two], axis=1).astype(jnp.bfloat16)
@@ -456,7 +460,7 @@
     last_sum = last_sum.reshape(qkv_sum.shape[0], -1)
     last_cols = last_sum.shape[1]
     last_sum = jnp.pad(last_sum, ((0, 0), (0, -last_cols % (2 * LANES))))
-    last_half = plane_share(last_sum)
+    last_half, _ = plane_share(last_sum)
     qkv_share, last_share = reduce_planes([qkv_half, last_half])
     last_share = last_share[:, :last_cols].reshape(time_rows, first_cols)
     smalls = unpack(last_share[:, time_cols:] * factor, sizes, 1)

time: 740 us -> 661 us (0.89)
  waiting for transfers between devices: 365 us -> 285 us
    reduce_scatter x1, waiting for transfers between devices: 97 us -> 26.5 us  [reduce_weight(): share = lax.psum_scatter(partial, 'fsdp', scatter_dimension=0, tiled=True)]
    reduce_scatter x2, waiting for transfers between devices: 50.5 us -> 70.5 us  [reduce_planes(): lax.psum_scatter(jnp.concatenate(shares, axis=1), 'fsdp', scatter_dimensi...]
    ppermute x4, waiting for transfers between devices: 77.5 us -> 58.3 us  [plane_share(): other = lax.ppermute(both, 'dp', [(0, 1), (1, 0)])]
    ppermute x1, waiting for transfers between devices: 10.2 us -> 0.01 us  [reduce_weight(): other = lax.ppermute(share, 'dp', [(0, 1), (1, 0)])]
    unnamed x93 -> x95, local copies, waits for them, and re-layouts: 21.2 us -> 24.7 us
  transfers between devices with their start and end apart: 17 -> 17, of which waited for: 12 -> 12; matrix products, arithmetic and copies ran while one was open for 21% -> 28% of each run, Pallas kernels for 5% -> 12%
where the time goes in v4:
time: 661 us; the launch traced here: 656 us
  waiting for transfers between devices  285 us (43%)
  matrix products  145 us (22%)
  Pallas kernels  76.8 us (12%)
  other arithmetic  60.1 us (9%)
  local copies, waits for them, and re-layouts  53.6 us (8%)
  starting transfers between devices  20.6 us (3%)
  between operations  15.3 us (2%)
    all_gather x3, waiting for transfers between devices, gather(): return lax.all_gather(part, 'fsdp', axis=0, tiled=True)  117 us
    reduce_scatter x2, waiting for transfers between devices, reduce_planes(): lax.psum_scatter(jnp.concatenate(shares, axis=1), 'fsdp', scatter_dimensi...  70.5 us
    ppermute x4, waiting for transfers between devices, plane_share(): other = lax.ppermute(both, 'dp', [(0, 1), (1, 0)])  58.3 us
    dot_general x4, matrix products, product_right(): lax.dot_general(left, right, (((1,), (1,)), ((), ())), preferred_element_...  53.6 us
    dot_general x5, matrix products, product(): return jnp.dot(left, right, preferred_element_type=jnp.float32)  52.6 us
    pallas_call x1, Pallas kernels, attend_backward(): pl.pallas_call(functools.partial(backward_kernel, block=block), grid_spec...  40.4 us
    dot_general x5, matrix products, product_left(): lax.dot_general(left, right, (((0,), (0,)), ((), ())), preferred_element_...  38.3 us
    pallas_call x1, Pallas kernels, attend_forward(): pl.pallas_call(functools.partial(forward_kernel, block=block), grid_spec=...  36.3 us
  transfers between devices with their start and end apart: 17, of which 12 were waited for; matrix products, arithmetic and copies ran while one was open for 28% of the time, Pallas kernels for 12%

profile of v4, /device:TPU:0, one launch (start us, length us, event | category | flops | bytes accessed | tf_op | source)
XLA Modules:
  0.0 655.7 jit_solution(1815408178318427541)
XLA Ops:
  10.4 1.9 pad_maximum_fusion.6
  12.4 1.9 pad_maximum_fusion.3
  17.8 1.9 fusion.45
  19.8 1.8 pad_maximum_fusion.4
  23.2 61.4 %all-gather.4.cloned.1.call-done = bf16[1024,3712]{1,0:T(8,128)(2,1)} async-done(((bf16[64,3712]{1,0:T(8,128)(2,1)}), bf16[1024,3712]{1,0:T(8,128)(2,1)}) %all-gather.4.cloned.1.call-update) | async-done | bytes 7602192 | tf_op jit(solution)/shard_map/all_gather | solution.py:285
  84.6 2.5 slice.134
  87.1 3.6 reshape.511
  92.8 2.6 convolution_bitcast_fusion
  95.4 3.4 copy-done.3
  98.8 1.4 fusion.20
  100.2 13.1 %broadcast_add_fusion.q_ref.k_ref.v_ref = f32[1024,3072]{1,0:T(8,128)} fusion(f32[3072]{0:T(1024)S(1)} %reshape.537, bf16[1024,1024]{1,0:T(8,128)(2,1)S(1)} %fusion.20, bf16[1024,3712]{1,0:T(8,128)(2,1)} %all-gather.4.cloned.1.call-done), kind=kOutput, calls=%fused_computation.16 | convolution fusion | flops 6445596672 | bytes 20983808 | tf_op jit(solution)/shard_map/dot_general | solution.py:269
  114.2 36.3 %attend_forward.1 = (bf16[1024,1024]{1,0:T(8,128)(2,1)}, bf16[1024,1024]{1,0:T(8,128)(2,1)}, bf16[1024,1024]{1,0:T(8,128)(2,1)}, bf16[1024,1024]{1,0:T(8,128)(2,1)}, f32[8,2,1024]{2,1,0:T(2,128)}) custom-call(s32[1,4]{1,0:T(1,128)} %bitcast.85, s32[1,4]{1,0:T(1,128)} %bitcast_subtract_fusion.count_ref, f32[1024,3072]{1,0:T(8,128)} %broadcast_add_fusion.q_ref.k_ref.v_ref, ...), custom_call_target="tpu_custom_call" | custom-call | tf_op jit(solution)/shard_map/attend_forward/pallas_call | solution.py:204
  150.6 23.2 %all-gather.6.cloned.1.call-done = bf16[1024,5120]{1,0:T(8,128)(2,1)} async-done(((bf16[64,5120]{1,0:T(8,128)(2,1)}), bf16[1024,5120]{1,0:T(8,128)(2,1)}) %all-gather.6.cloned.1.call-update) | async-done | bytes 10485776 | tf_op jit(solution)/shard_map/all_gather | solution.py:285
  173.8 4.8 fusion.61
  179.3 1.6 multiply_convert_fusion.2
  180.9 2.4 slice-done.5
  184.3 16.7 %fusion.3 = (f32[1024,4096]{1,0:T(8,128)}, bf16[1024,4096]{1,0:T(8,128)(2,1)S(1)}) fusion(f32[4096]{0:T(1024)S(1)} %bitcast.84, bf16[1024,1024]{1,0:T(8,128)(2,1)S(1)} %multiply_convert_fusion.2, bf16[1024,5120]{1,0:T(8,128)(2,1)S(1)} %bitcast.99), kind=kOutput, calls=%fused_computation.4 | convolution fusion | flops 8636071936 | bytes 35667968 | tf_op jit(solution)/shard_map/dot_general | solution.py:269
  201.0 3.3 copy-done.36
  204.4 11.3 %convolution_convert_fusion.1 = bf16[4096,1024]{1,0:T(8,128)(2,1)} fusion(bf16[1024,4096]{1,0:T(8,128)(2,1)S(1)} %get-tuple-element.34, bf16[1024,1024]{1,0:T(8,128)(2,1)S(1)} %copy-done.7), kind=kOutput, calls=%fused_computation.9 | convolution fusion | flops 8594128896 | bytes 18874368 | tf_op jit(solution)/shard_map/dot_general | solution.py:273
  215.7 32.8 %all-gather.8.cloned.1.call-done = bf16[4096,1024]{1,0:T(8,128)(2,1)} async-done(((bf16[256,1024]{1,0:T(8,128)(2,1)}), bf16[4096,1024]{1,0:T(8,128)(2,1)}) %all-gather.8.cloned.1.call-update) | async-done | bytes 8388624 | tf_op jit(solution)/shard_map/all_gather | solution.py:285
  248.5 16.6 %fusion.59 = (bf16[4096]{0:T(1024)(128)(2,1)S(1)}, bf16[1024,4096]{1,0:T(8,128)(2,1)}) fusion(f32[1024,4096]{1,0:T(8,128)} %get-tuple-element.36, bf16[4096,1024]{1,0:T(8,128)(2,1)} %all-gather.8.cloned.1.call-done, bf16[1024,1024]{1,0:T(8,128)(2,1)S(1)} %copy-done.7), kind=kOutput, calls=%fused_computation.152 | convolution fusion | flops 8602513408 | bytes 35659776 | tf_op jit(solution)/shard_map/dot_general | solution.py:279
  265.1 13.6 %convolution_convert_fusion = bf16[1024,4096]{1,0:T(8,128)(2,1)S(1)} fusion(bf16[1024,1024]{1,0:T(8,128)(2,1)} %copy-done.11, bf16[1024,4096]{1,0:T(8,128)(2,1)} %get-tuple-element.37), kind=kOutput, calls=%fused_computation.8 | convolution fusion | flops 8594128896 | bytes 18874368 | tf_op jit(solution)/shard_map/dot_general | solution.py:273
  278.7 3.2 copy-done.9
  281.9 1.6 dynamic_slice.51
  283.8 17.6 %multiply_reduce_fusion = (bf16[1024]{0:T(1024)(128)(2,1)S(1)}, f32[1024]{0:T(1024)S(1)}, bf16[1024]{0:T(1024)(128)(2,1)S(1)}, f32[1024,1024]{1,0:T(8,128)}, bf16[1024,1024]{1,0:T(8,128)(2,1)}) fusion(f32[1024,1024]{1,0:T(8,128)} %copy-done.4, f32[1024]{0:T(1024)S(1)} %fusion.50, f32[1024]{0:T(1024)S(1)} %broadcast_multiply_fusion, f32[1024]{0:T(1024)S(1)} %reshape.539, ...), kind=kOutput, calls=%fused_computation.47 | convolution fusion | flops 8604611584 | bytes 31481856 | tf_op jit(solution)/shard_map/dot_general | solution.py:279
  301.4 4.5 fusion.57
  306.7 1.3 copy-done.5
  307.9 5.3 add_convert_fusion.2
  313.2 1.5 collective-permute-start.1
  314.7 2.4 convolution_convert_fusion.4
  317.3 1.9 collective-permute-done.7
  320.1 2.5 constant_dynamic-slice_fusion.2
  322.6 50.0 %collective-permute-done.8 = bf16[512,512]{1,0:T(8,128)(2,1)} collective-permute-done((bf16[512,512]{1,0:T(8,128)(2,1)S(1)}, bf16[512,512]{1,0:T(8,128)(2,1)}, u32[]{:S(2)}, u32[]{:S(2)}) %collective-permute-start.8) | collective-permute-done | bytes 524320 | tf_op jit(solution)/shard_map/ppermute | solution.py:319
  373.8 3.1 fusion.38
  376.9 2.8 pad_maximum_fusion
  381.4 5.3 convolution_convert_fusion.3.grad_ref
  386.6 40.4 %attend_backward.1 = (bf16[1024,1024]{1,0:T(8,128)(2,1)}, bf16[1024,1024]{1,0:T(8,128)(2,1)}, bf16[1024,1024]{1,0:T(8,128)(2,1)}, f32[1,3,1024]{2,1,0:T(4,128)}) custom-call(s32[1,4]{1,0:T(1,128)} %bitcast.86, s32[1,4]{1,0:T(1,128)} %bitcast_subtract_fusion.count_ref, bf16[1024,1024]{1,0:T(8,128)(2,1)} %get-tuple-element.38.query_ref, ...), custom_call_target="tpu_custom_call" | custom-call | tf_op jit(solution)/shard_map/attend_backward/pallas_call | solution.py:230
  427.1 1.9 constant_dynamic-update-slice_fusion.2
  431.1 7.3 %convolution_convert_fusion.2 = bf16[1024,3072]{1,0:T(8,128)(2,1)S(1)} fusion(bf16[1024,1024]{1,0:T(8,128)(2,1)S(1)} %copy-done.15, bf16[1024,3072]{1,0:T(8,128)(2,1)S(1)} %constant_dynamic-update-slice_fusion), kind=kOutput, calls=%fused_computation.24 | convolution fusion | flops 6445596672 | bytes 14680064 | tf_op jit(solution)/shard_map/dot_general | solution.py:273
  438.4 2.6 copy-done.10
  441.0 1.2 dynamic_slice.53
  442.3 11.9 %collective-permute-start.2 = (bf16[512,1536]{1,0:T(8,128)(2,1)}, bf16[512,1536]{1,0:T(8,128)(2,1)}, u32[]{:S(2)}, u32[]{:S(2)}) collective-permute-start(bf16[512,1536]{1,0:T(8,128)(2,1)} %dynamic_slice.53), channel_id=1, source_target_pairs={{0,1},{1,0},{2,3},{3,2},{4,5},{5,4},{6,7},{7,6},{8,9},{9,8},{10,11... | collective-permute-start | bytes 4718600 | tf_op jit(solution)/shard_map/ppermute | solution.py:314
  454.2 2.0 reduce.2
  457.5 3.4 add_convert_fusion.5
  460.9 1.5 collective-permute-start.3
  462.5 14.1 %fusion.55 = (bf16[1024]{0:T(1024)(128)(2,1)S(1)}, f32[1024]{0:T(1024)S(1)}, f32[1024,1024]{1,0:T(8,128)S(1)}, bf16[1024,1024]{1,0:T(8,128)(2,1)}) fusion(f32[1024]{0:T(1024)S(1)} %copy-done.25, f32[1024]{0:T(1024)S(1)} %copy-done.23, bf16[1024,1024]{1,0:T(8,128)(2,1)S(1)} %copy-done.2, f32[1024,2048]{1,0:T(8,128)} %copy-done.3, f32[1024]{0:T(1024)S(1)} %copy-done.32, ...), kind=kOutput, calls=%fused_computation.150 | convolution fusion | flops 6456080384 | bytes 25188352 | tf_op jit(solution)/shard_map/dot_general | solution.py:279
  476.6 1.9 copy-done.8
  478.6 2.4 fusion.22
  481.5 3.7 fusion.35
  486.4 2.4 copy.63
  488.8 3.4 convert_element_type.300
  493.3 1.7 collective-permute-done.4
  496.8 2.1 constant_dynamic-slice_fusion.1
  499.0 8.3 %collective-permute-done.5 = bf16[512,384]{1,0:T(8,128)(2,1)S(1)} collective-permute-done((bf16[512,384]{1,0:T(8,128)(2,1)S(1)}, bf16[512,384]{1,0:T(8,128)(2,1)S(1)}, u32[]{:S(2)}, u32[]{:S(2)}) %collective-permute-start.5) | collective-permute-done | bytes 393248 | tf_op jit(solution)/shard_map/ppermute | solution.py:319
  507.4 2.4 fusion.41
  509.8 2.2 pad_maximum_fusion.1
  512.1 15.4 %add_convert_fusion.3 = bf16[1024,1024]{1,0:T(8,128)(2,1)} fusion(f32[1024,1024]{1,0:T(8,128)} %copy-done.4, f32[1024]{0:T(1024)S(1)} %reshape.542, bf16[1024,4096]{1,0:T(8,128)(2,1)} %copy-done.36, bf16[4096,1024]{1,0:T(8,128)(2,1)} %all-gather.8.cloned.1.call-done), kind=kOutput, calls=%fused_computation.54 | convolution fusion | flops 8593080320 | bytes 23072768 | tf_op jit(solution)/shard_map/dot_general | solution.py:269
  528.3 6.1 add_convert_fusion
  534.4 2.4 collective-permute-done.9
  536.9 26.5 %reduce-scatter.8.cloned.1.call-done = bf16[256,1024]{1,0:T(8,128)(2,1)} async-done(((bf16[4096,1024]{1,0:T(8,128)(2,1)}), bf16[256,1024]{1,0:T(8,128)(2,1)}) %reduce-scatter.8.cloned.1.call-update) | async-done | bytes 524304 | tf_op jit(solution)/shard_map/reduce_scatter | solution.py:344
  563.4 1.5 collective-permute-start.10
  566.8 70.5 %reduce-scatter.4.cloned.1.call-done = bf16[64,1920]{1,0:T(8,128)(2,1)} async-done(((bf16[1024,1920]{1,0:T(8,128)(2,1)}), bf16[64,1920]{1,0:T(8,128)(2,1)}) %reduce-scatter.4.cloned.1.call-update) | async-done | bytes 245776 | tf_op jit(solution)/shard_map/reduce_scatter | solution.py:326
  637.3 1.5 collective-permute-start.6
  639.9 3.9 collective-permute-done.6
  (205 shorter events, 34.6 us)
Async XLA Ops:
  7.2 85.6 %copy-start = (bf16[1024,256]{1,0:T(8,128)(2,1)S(1)}, bf16[1024,256]{1,0:T(8,128)(2,1)}, u32[]{:S(2)}) copy-start(bf16[1024,256]{1,0:T(8,128)(2,1)} %param.18) | copy-start | bytes 1572868
  7.2 8.5 %copy-start.21 = (s32[1,1024]{1,0:T(1,128)S(1)}, s32[1,1024]{1,0:T(1,128)}, u32[]{:S(2)}) copy-start(s32[1,1024]{1,0:T(1,128)} %param.19) | copy-start | bytes 12292
  7.2 77.4 %all-gather.4.cloned.1.call-start = ((), (), s32[]{:S(2)}) async-start(), calls=%async_computation.3 | async-start | bytes 8077312 | tf_op jit(solution)/shard_map/all_gather | solution.py:285
  10.4 11.2 %copy-start.1 = (bf16[1024,1024]{1,0:T(8,128)(2,1)S(1)}, bf16[1024,1024]{1,0:T(8,128)(2,1)}, u32[]{:S(2)}) copy-start(bf16[1024,1024]{1,0:T(8,128)(2,1)} %param.17) | copy-start | bytes 6291460
  12.4 161.4 %all-gather.6.cloned.1.call-start = ((), (), s32[]{:S(2)}) async-start(), calls=%async_computation.4 | async-start | bytes 11141120 | tf_op jit(solution)/shard_map/all_gather | solution.py:285
  14.4 234.1 %all-gather.8.cloned.1.call-start = ((), (), s32[]{:S(2)}) async-start(), calls=%async_computation.5 | async-start | bytes 8912896 | tf_op jit(solution)/shard_map/all_gather | solution.py:285
  15.2 512.3 %reduce-scatter.6.cloned.1.call-start = ((), (), s32[]{:S(2)}) async-start(), calls=%async_computation.7 | async-start | bytes 5570560 | tf_op jit(solution)/shard_map/reduce_scatter | solution.py:326
  17.7 5.4 copy-start.34
  22.5 72.9 %copy-start.22 = (f32[1024]{0:T(1024)}, f32[1024]{0:T(1024)S(1)}, u32[]{:S(2)}) copy-start(f32[1024]{0:T(1024)S(1)} %broadcast_multiply_fusion.1) | copy-start | bytes 12292
  23.2 63.9 %copy-start.28 = (f32[1024]{0:T(1024)}, f32[1024]{0:T(1024)S(1)}, u32[]{:S(2)}) copy-start(f32[1024]{0:T(1024)S(1)} %fusion.23) | copy-start | bytes 12292
  23.2 72.2 %copy-start.26 = (f32[1024]{0:T(1024)}, f32[1024]{0:T(1024)S(1)}, u32[]{:S(2)}) copy-start(f32[1024]{0:T(1024)S(1)} %fusion.49) | copy-start | bytes 12292
  92.6 2.8 copy-start.31
  92.6 2.8 copy-start.24
  95.4 3.4 copy-start.3
  100.2 13.1 %copy-start.14 = (bf16[1024,1024]{1,0:T(8,128)(2,1)}, bf16[1024,1024]{1,0:T(8,128)(2,1)S(1)}, u32[]{:S(2)}) copy-start(bf16[1024,1024]{1,0:T(8,128)(2,1)S(1)} %fusion.20) | copy-start | bytes 6291460
  173.8 5.5 slice-start
  173.8 5.5 slice-start.1
  173.8 7.1 %slice-start.4 = ((s8[10485760]{0:T(1024)(128)(4,1)}), s8[4194304]{0:T(1024)(128)(4,1)S(1)}, s32[]{:S(2)}) async-start(s8[10485760]{0:T(1024)(128)(4,1)} %bitcast.98), calls=%async_computation.13 | async-start | bytes 8388608
  173.8 9.5 %slice-start.5 = ((s8[10485760]{0:T(1024)(128)(4,1)}), s8[4194304]{0:T(1024)(128)(4,1)S(1)}, s32[]{:S(2)}) async-start(s8[10485760]{0:T(1024)(128)(4,1)} %bitcast.98), calls=%async_computation.14 | async-start | bytes 8388608
  178.6 2.2 copy-start.4
  178.7 5.6 slice-start.6
  180.8 20.2 %copy-start.11 = (bf16[1024,1024]{1,0:T(8,128)(2,1)}, bf16[1024,1024]{1,0:T(8,128)(2,1)S(1)}, u32[]{:S(2)}) copy-start(bf16[1024,1024]{1,0:T(8,128)(2,1)S(1)} %multiply_convert_fusion.2) | copy-start | bytes 6291460
  184.3 20.1 %copy-start.7 = (bf16[1024,1024]{1,0:T(8,128)(2,1)S(1)}, bf16[1024,1024]{1,0:T(8,128)(2,1)}, u32[]{:S(2)}) copy-start(bf16[1024,1024]{1,0:T(8,128)(2,1)} %param.20) | copy-start | bytes 6291460
  201.0 3.3 copy-start.36
  248.5 35.3 %slice-start.2 = ((s8[8388608]{0:T(1024)(128)(4,1)}), s8[4194304]{0:T(1024)(128)(4,1)S(1)}, s32[]{:S(2)}) async-start(s8[8388608]{0:T(1024)(128)(4,1)} %bitcast.75), calls=%async_computation.11 | async-start | bytes 8388608
  265.1 18.7 %slice-start.3 = ((s8[8388608]{0:T(1024)(128)(4,1)}), s8[4194304]{0:T(1024)(128)(4,1)S(1)}, s32[]{:S(2)}) async-start(s8[8388608]{0:T(1024)(128)(4,1)} %bitcast.75), calls=%async_computation.12 | async-start | bytes 8388608
  278.6 3.2 copy-start.9
  283.5 24.4 %collective-permute-start = (bf16[512,2048]{1,0:T(8,128)(2,1)}, bf16[512,2048]{1,0:T(8,128)(2,1)}, u32[]{:S(2)}, u32[]{:S(2)}) collective-permute-start(bf16[512,2048]{1,0:T(8,128)(2,1)} %dynamic_slice.51), channel_id=1, source_target_pairs={{0,1},{1,0},{2,3},{3,2},{4,5},{5,4},{6,7},{7,6},{8,9},{9,8},{10,11... | collective-permute-start | bytes 6291464 | tf_op jit(solution)/shard_map/ppermute | solution.py:314
  305.9 2.0 copy-start.5
  307.9 9.2 %copy-start.16 = (bf16[1024,1024]{1,0:T(8,128)(2,1)}, bf16[1024,1024]{1,0:T(8,128)(2,1)S(1)}, u32[]{:S(2)}) copy-start(bf16[1024,1024]{1,0:T(8,128)(2,1)S(1)} %get-tuple-element.41) | copy-start | bytes 6291460
  307.9 6.8 %copy-start.35 = (bf16[1024,1024]{1,0:T(8,128)(2,1)S(1)}, bf16[1024,1024]{1,0:T(8,128)(2,1)}, u32[]{:S(2)}) copy-start(bf16[1024,1024]{1,0:T(8,128)(2,1)} %get-tuple-element.33) | copy-start | bytes 6291460
  313.2 60.6 %collective-permute-start.1 = (bf16[512,2048]{1,0:T(8,128)(2,1)}, bf16[512,2048]{1,0:T(8,128)(2,1)}, u32[]{:S(2)}, u32[]{:S(2)}) collective-permute-start(bf16[512,2048]{1,0:T(8,128)(2,1)} %add_convert_fusion.2), channel_id=1, source_target_pairs={{0,16},{16,0},{1,17},{17,1},{2,18},{18,2},{3,19},{19,3},{4,20},{20... | collective-permute-start | bytes 6291464 | tf_op jit(solution)/shard_map/ppermute | solution.py:319
  317.2 2.0 collective-permute-start.7
  319.4 53.2 %collective-permute-start.8 = (bf16[512,512]{1,0:T(8,128)(2,1)S(1)}, bf16[512,512]{1,0:T(8,128)(2,1)}, u32[]{:S(2)}, u32[]{:S(2)}) collective-permute-start(bf16[512,512]{1,0:T(8,128)(2,1)S(1)} %add_convert_fusion.7), channel_id=1, source_target_pairs={{0,16},{16,0},{1,17},{17,1},{2,18},{18,2},{3,19},{19,3},{4,20},{20... | collective-permute-start | bytes 1572872 | tf_op jit(solution)/shard_map/ppermute | solution.py:319
  379.8 1.6 copy-start.17
  379.8 183.7 %reduce-scatter.8.cloned.1.call-start = ((), (), s32[]{:S(2)}) async-start(), calls=%async_computation.8 | async-start | bytes 8912896 | tf_op jit(solution)/shard_map/reduce_scatter | solution.py:344
  380.4 256.9 %reduce-scatter.4.cloned.1.call-start = ((), (), s32[]{:S(2)}) async-start(), calls=%async_computation.6 | async-start | bytes 4177920 | tf_op jit(solution)/shard_map/reduce_scatter | solution.py:326
  427.1 2.2 copy-start.13
  427.1 2.9 copy-start.12
  429.3 1.7 copy-start.15
  431.1 7.3 %copy-start.18 = (bf16[1024,3072]{1,0:T(8,128)(2,1)}, bf16[1024,3072]{1,0:T(8,128)(2,1)S(1)}, u32[]{:S(2)}) copy-start(bf16[1024,3072]{1,0:T(8,128)(2,1)S(1)} %constant_dynamic-update-slice_fusion) | copy-start | bytes 18874372
  438.4 2.6 copy-start.10
  441.0 15.2 %copy-start.33 = (f32[1,3,1024]{2,1,0:T(4,128)S(1)}, f32[1,3,1024]{2,1,0:T(4,128)}, u32[]{:S(2)}) copy-start(f32[1,3,1024]{2,1,0:T(4,128)} %get-tuple-element.50) | copy-start | bytes 36868
  442.3 20.2 %copy-start.2 = (bf16[1024,1024]{1,0:T(8,128)(2,1)S(1)}, bf16[1024,1024]{1,0:T(8,128)(2,1)}, u32[]{:S(2)}) copy-start(bf16[1024,1024]{1,0:T(8,128)(2,1)} %param.17) | copy-start | bytes 6291460
  442.3 20.2 %copy-start.23 = (f32[1024]{0:T(1024)S(1)}, f32[1024]{0:T(1024)}, u32[]{:S(2)}) copy-start(f32[1024]{0:T(1024)} %copy-done.22) | copy-start | bytes 12292
  442.3 20.2 %copy-start.25 = (f32[1024]{0:T(1024)S(1)}, f32[1024]{0:T(1024)}, u32[]{:S(2)}) copy-start(f32[1024]{0:T(1024)} %copy-done.24) | copy-start | bytes 12292
  442.3 20.2 %copy-start.27 = (f32[1024]{0:T(1024)S(1)}, f32[1024]{0:T(1024)}, u32[]{:S(2)}) copy-start(f32[1024]{0:T(1024)} %copy-done.26) | copy-start | bytes 12292
  442.3 20.2 %copy-start.32 = (f32[1024]{0:T(1024)S(1)}, f32[1024]{0:T(1024)}, u32[]{:S(2)}) copy-start(f32[1024]{0:T(1024)} %copy-done.31) | copy-start | bytes 12292
  442.3 15.2 %collective-permute-start.2 = (bf16[512,1536]{1,0:T(8,128)(2,1)}, bf16[512,1536]{1,0:T(8,128)(2,1)}, u32[]{:S(2)}, u32[]{:S(2)}) collective-permute-start(bf16[512,1536]{1,0:T(8,128)(2,1)} %dynamic_slice.53), channel_id=1, source_target_pairs={{0,1},{1,0},{2,3},{3,2},{4,5},{5,4},{6,7},{7,6},{8,9},{9,8},{10,11... | collective-permute-start | bytes 4718600 | tf_op jit(solution)/shard_map/ppermute | solution.py:314
  460.9 15.7 %copy-start.29 = (f32[1024]{0:T(1024)S(1)}, f32[1024]{0:T(1024)}, u32[]{:S(2)}) copy-start(f32[1024]{0:T(1024)} %copy-done.28) | copy-start | bytes 12292
  460.9 46.5 %collective-permute-start.3 = (bf16[512,1536]{1,0:T(8,128)(2,1)}, bf16[512,1536]{1,0:T(8,128)(2,1)}, u32[]{:S(2)}, u32[]{:S(2)}) collective-permute-start(bf16[512,1536]{1,0:T(8,128)(2,1)} %add_convert_fusion.5), channel_id=1, source_target_pairs={{0,16},{16,0},{1,17},{17,1},{2,18},{18,2},{3,19},{19,3},{4,20},{20... | collective-permute-start | bytes 4718600 | tf_op jit(solution)/shard_map/ppermute | solution.py:319
  476.6 1.9 copy-start.8
  493.2 1.8 collective-permute-start.4
  493.3 5.6 copy-start.6
  496.0 11.2 %collective-permute-start.5 = (bf16[512,384]{1,0:T(8,128)(2,1)S(1)}, bf16[512,384]{1,0:T(8,128)(2,1)S(1)}, u32[]{:S(2)}, u32[]{:S(2)}) collective-permute-start(bf16[512,384]{1,0:T(8,128)(2,1)S(1)} %add_convert_fusion.9), channel_id=1, source_target_pairs={{0,16},{16,0},{1,17},{17,1},{2,18},{18,2},{3,19},{19,3},{4,20},{20... | collective-permute-start | bytes 1179656 | tf_op jit(solution)/shard_map/ppermute | solution.py:319
  509.8 2.2 copy-start.30
  527.5 9.3 %copy-start.20 = (bf16[64,2560]{1,0:T(8,128)(2,1)S(1)}, bf16[64,2560]{1,0:T(8,128)(2,1)}, u32[]{:S(2)}) copy-start(bf16[64,2560]{1,0:T(8,128)(2,1)} %reduce-scatter.6.cloned.1.call-done) | copy-start | bytes 983044
  527.5 9.3 %collective-permute-start.9 = (bf16[64,2560]{1,0:T(8,128)(2,1)}, bf16[64,2560]{1,0:T(8,128)(2,1)S(1)}, u32[]{:S(2)}, u32[]{:S(2)}) collective-permute-start(bf16[64,2560]{1,0:T(8,128)(2,1)} %reduce-scatter.6.cloned.1.call-done), channel_id=1, source_target_pairs={{0,16},{16,0},{1,17},{17,1},{2,18},{18,2},{3,19},{19,3},{4,20},{20... | collective-permute-start | bytes 983048 | tf_op jit(solution)/shard_map/ppermute | solution.py:333
  563.4 75.3 %copy-start.19 = (bf16[256,1024]{1,0:T(8,128)(2,1)S(1)}, bf16[256,1024]{1,0:T(8,128)(2,1)}, u32[]{:S(2)}) copy-start(bf16[256,1024]{1,0:T(8,128)(2,1)} %reduce-scatter.8.cloned.1.call-done) | copy-start | bytes 1572868
  563.4 75.3 %collective-permute-start.10 = (bf16[256,1024]{1,0:T(8,128)(2,1)}, bf16[256,1024]{1,0:T(8,128)(2,1)S(1)}, u32[]{:S(2)}, u32[]{:S(2)}) collective-permute-start(bf16[256,1024]{1,0:T(8,128)(2,1)} %reduce-scatter.8.cloned.1.call-done), channel_id=1, source_target_pairs={{0,16},{16,0},{1,17},{17,1},{2,18},{18,2},{3,19},{19,3},{4,20},{20... | collective-permute-start | bytes 1572872 | tf_op jit(solution)/shard_map/ppermute | solution.py:346
  637.3 6.5 collective-permute-start.6
Sparse Core Ops, SparseCore 0:
  12.5 72.0 all-gather.3
  87.4 86.2 all-gather.5
  176.0 72.4 all-gather.7
  379.9 76.9 reduce-scatter.5
  460.8 102.5 reduce-scatter.7
  567.2 70.0 reduce-scatter.3
